TPU v7x, 32 devices: a whole 2x2x4 slice. The times are simulated.
32 devices in a mesh: seq: 2 (over x), shard: 16 (over z, y, core).
Axes of the slice: x: 2, y: 2, z: 4, core: 2. Of those that a mesh axis runs over, the one named last changes fastest.
Arguments:
- tokens: bfloat16 [32, 512, 1024], P(('seq', 'shard')), may hold values from -6 to 6
- cotangent: bfloat16 [32, 512, 1024], P(('seq', 'shard')), may hold values from -6 to 6
- lengths: int32 [16], replicated, may hold values from 512 to 1024, as said below
- first_gain: bfloat16 [1024], P('shard'), may hold values from 0.25 to 1.75
- first_bias: bfloat16 [1024], P('shard'), may hold values from -1.5 to 1.5
- qkv_weight: bfloat16 [1024, 3072], P('shard'), may hold values from -0.1875 to 0.1875
- qv_bias: bfloat16 [2048], P('shard'), may hold values from -1.5 to 1.5
- dense_weight: bfloat16 [1024, 1024], P('shard'), may hold values from -0.5 to 0.5
- dense_bias: bfloat16 [1024], P('shard'), may hold values from -1.5 to 1.5
- second_gain: bfloat16 [1024], P('shard'), may hold values from 0.25 to 1.75
- second_bias: bfloat16 [1024], P('shard'), may hold values from -1.5 to 1.5
- fc1_weight: bfloat16 [1024, 4096], P('shard'), may hold values from -0.1875 to 0.1875
- fc1_bias: bfloat16 [4096], P('shard'), may hold values from -1.5 to 1.5
- fc2_weight: bfloat16 [4096, 1024], P('shard'), may hold values from -0.09375 to 0.09375
- fc2_bias: bfloat16 [1024], P('shard'), may hold values from -1.5 to 1.5
Outputs:
- block_out: bfloat16 [32, 512, 1024], P(('seq', 'shard'))
- tokens_grad: bfloat16 [32, 512, 1024], P(('seq', 'shard'))
- first_gain_grad: float32 [1024], P('shard')
- first_bias_grad: float32 [1024], P('shard')
- qkv_weight_grad: float32 [1024, 3072], P('shard')
- qv_bias_grad: float32 [2048], P('shard')
- dense_weight_grad: float32 [1024, 1024], P('shard')
- dense_bias_grad: float32 [1024], P('shard')
- second_gain_grad: float32 [1024], P('shard')
- second_bias_grad: float32 [1024], P('shard')
- fc1_weight_grad: float32 [1024, 4096], P('shard')
- fc1_bias_grad: float32 [4096], P('shard')
- fc2_weight_grad: float32 [4096, 1024], P('shard')
- fc2_bias_grad: float32 [1024], P('shard')
Inputs may be any that keep to these rules, and one draw needn't show every extreme that they name: Every length is a multiple of 32; the lengths of each group's 1 sequence sum to at most 1024, and in some group to exactly 1024.
All inputs are finite; a program needn't handle non-finite values.
Results may differ from a plain program's by a relative error of at most 0.019.
Values may be sent and summed in bfloat16 or wider, within the bound.
A program may use at most 192 MiB of HBM per device.

v0:
```python
import jax
import jax.numpy as jnp
from jax import lax
from jax.sharding import PartitionSpec as P

HEADS = 16
HEAD = 64


epsilon = 1e-05
masked_score = -1e30


def norm_rows(hidden, gain, shift):
    center = hidden - jnp.mean(hidden, axis=-1, keepdims=True)
    spread = jnp.mean(center * center, axis=-1, keepdims=True)
    return center * lax.rsqrt(spread + epsilon) * gain + shift


def gelu_tanh(values):
    return (
        0.5
        * values
        * (1.0 + jnp.tanh(0.7978845608028654 * (values + 0.044715 * values * values * values)))
    )


def layout_tables(lengths, dealing, lane_count, group_count, per_group):
    seq_rows = lengths // lane_count
    row_start = jnp.cumsum(seq_rows) - seq_rows
    picked = (dealing[:, None] == jnp.arange(dealing.shape[0], dtype=jnp.int32)[None, :]).astype(
        jnp.int32
    )
    slot_rows = jnp.sum(picked * seq_rows[:, None], axis=0).reshape(group_count, per_group)
    slot_start = jnp.sum(picked * row_start[:, None], axis=0).reshape(group_count, per_group)
    slot_before = jnp.cumsum(slot_rows, axis=1) - slot_rows
    seq_before = jnp.sum(picked * slot_before.reshape(-1)[None, :], axis=1)
    return (seq_rows, row_start, slot_rows, slot_start, slot_before, seq_before)


def per_device(
    tokens,
    cotangent,
    lengths,
    first_gain,
    first_bias,
    qkv_weight,
    qv_bias,
    dense_weight,
    dense_bias,
    second_gain,
    second_bias,
    fc1_weight,
    fc1_bias,
    fc2_weight,
    fc2_bias,
):
    shard_count = lax.axis_size("shard")
    seq_count = lax.axis_size("seq")
    lane_count = shard_count * seq_count
    model_width = tokens.shape[2]
    slot_count = tokens.shape[1]
    per_pair = slot_count // shard_count
    group_cap = slot_count * seq_count
    per_group = lengths.shape[0] // shard_count
    my_group = lax.axis_index("shard")
    dealing = jnp.arange(lengths.shape[0], dtype=jnp.int32)
    seq_rows, row_start, slot_rows, slot_start, slot_before, seq_before = layout_tables(
        lengths, dealing, lane_count, shard_count, per_group
    )
    row_in = jnp.arange(per_pair, dtype=jnp.int32)[:, None, None]
    inside = ((row_in >= slot_before[None]) & (row_in < (slot_before + slot_rows)[None])).astype(
        jnp.int32
    )
    send_live = jnp.sum(inside, axis=2) > 0
    send_row = jnp.sum(inside * (slot_start[None] + row_in - slot_before[None]), axis=2).reshape(-1)

    def pack_rows(source):
        taken = jnp.take(source, send_row, axis=0).reshape(per_pair, shard_count, model_width)
        return jnp.where(send_live[:, :, None], taken, jnp.zeros_like(taken))

    recv_x, recv_cot = (
        lax.all_to_all(pack_rows(tokens[0]), "shard", split_axis=1, concat_axis=1, tiled=True),
        lax.all_to_all(pack_rows(cotangent[0]), "shard", split_axis=1, concat_axis=1, tiled=True),
    )
    chosen = (jnp.arange(shard_count, dtype=jnp.int32) == my_group).astype(jnp.int32)[:, None]
    own_before = jnp.sum(chosen * slot_before, axis=0)
    own_rows = jnp.sum(chosen * slot_rows, axis=0)
    row_ids = jnp.arange(per_pair, dtype=jnp.int32)[:, None]
    own_in = ((row_ids >= own_before[None]) & (row_ids < (own_before + own_rows)[None])).astype(
        jnp.int32
    )
    own_live = jnp.sum(own_in, axis=1)
    member = jnp.sum(own_in * jnp.arange(per_group, dtype=jnp.int32)[None], axis=1)
    row_offset = jnp.sum(own_in * (row_ids - own_before[None]), axis=1)
    lane_ids = jnp.arange(lane_count, dtype=jnp.int32)[None, :]
    segment = jnp.broadcast_to(
        jnp.where(own_live > 0, member, -1)[:, None], (per_pair, lane_count)
    ).reshape(-1)
    position = (row_offset[:, None] * lane_count + lane_ids).reshape(-1)
    params = (
        first_gain,
        first_bias,
        qkv_weight,
        qv_bias,
        dense_weight,
        dense_bias,
        second_gain,
        second_bias,
        fc1_weight,
        fc1_bias,
        fc2_weight,
        fc2_bias,
    )
    gathered = (
        lax.all_gather(params[0], "shard", axis=0, tiled=True),
        lax.all_gather(params[1], "shard", axis=0, tiled=True),
        lax.all_gather(params[2], "shard", axis=0, tiled=True),
        lax.all_gather(params[3], "shard", axis=0, tiled=True),
        lax.all_gather(params[4], "shard", axis=0, tiled=True),
        lax.all_gather(params[5], "shard", axis=0, tiled=True),
        lax.all_gather(params[6], "shard", axis=0, tiled=True),
        lax.all_gather(params[7], "shard", axis=0, tiled=True),
        lax.all_gather(params[8], "shard", axis=0, tiled=True),
        lax.all_gather(params[9], "shard", axis=0, tiled=True),
        lax.all_gather(params[10], "shard", axis=0, tiled=True),
        lax.all_gather(params[11], "shard", axis=0, tiled=True),
    )
    (
        gain_one,
        bias_one,
        full_qkv,
        bias_qv,
        full_dense,
        bias_dense,
        gain_two,
        bias_two,
        full_up,
        bias_up,
        full_down,
        bias_down,
    ) = gathered
    gain_one32 = gain_one.astype(jnp.float32)
    bias_one32 = bias_one.astype(jnp.float32)
    gain_two32 = gain_two.astype(jnp.float32)
    bias_two32 = bias_two.astype(jnp.float32)
    hidden = recv_x.reshape(slot_count, model_width).astype(jnp.float32)
    normed_low = norm_rows(hidden, gain_one32, bias_one32).astype(jnp.bfloat16)
    bias_qv32 = bias_qv.astype(jnp.float32)
    bias_all = jnp.concatenate(
        [bias_qv32[:model_width], jnp.zeros((model_width,), jnp.float32), bias_qv32[model_width:]]
    )
    projected = (
        jnp.dot(normed_low, full_qkv, preferred_element_type=jnp.float32) + bias_all
    ).astype(jnp.bfloat16)
    projected = projected.reshape(per_pair, shard_count, 3, model_width)
    by_head = lax.all_to_all(projected, "seq", split_axis=3, concat_axis=1, tiled=True)
    head_local = model_width // seq_count // HEAD
    by_head = by_head.reshape(group_cap, 3, head_local, HEAD)
    queries = by_head[:, 0]
    keys_all = by_head[:, 1]
    values_all = by_head[:, 2]
    head_ids = lax.axis_index("seq") * head_local + jnp.arange(head_local, dtype=jnp.int32)
    slopes = 2.0 ** (-8.0 * (head_ids.astype(jnp.float32) + 1.0) / HEADS)
    scale_factor = HEAD ** (-0.5)
    q_block = min(512, group_cap)
    block_count = group_cap // q_block

    def block_scores(query_rows, begin):
        raw_dot = jnp.einsum(
            "qhd,khd->hqk", query_rows, keys_all, preferred_element_type=jnp.float32
        )
        query_pos = lax.dynamic_slice_in_dim(position, begin, q_block)
        query_seg = lax.dynamic_slice_in_dim(segment, begin, q_block)
        allowed = (
            (query_seg[:, None] == segment[None, :])
            & (segment[None, :] >= 0)
            & (position[None, :] <= query_pos[:, None])
        )
        distance = (query_pos[:, None] - position[None, :]).astype(jnp.float32)
        return jnp.where(
            allowed[None],
            raw_dot * scale_factor - slopes[:, None, None] * distance[None],
            masked_score,
        )

    def attend(block_id):
        begin = block_id * q_block
        query_rows = lax.dynamic_slice_in_dim(queries, begin, q_block)
        scored = block_scores(query_rows, begin)
        row_top = jnp.max(scored, axis=2, keepdims=True)
        expd = jnp.exp(scored - row_top)
        row_total = jnp.sum(expd, axis=2, keepdims=True)
        probs_low = (expd / row_total).astype(jnp.bfloat16)
        mixed = jnp.einsum(
            "hqk,khd->qhd", probs_low, values_all, preferred_element_type=jnp.float32
        )
        return (mixed.astype(jnp.bfloat16), row_top[:, :, 0] + jnp.log(row_total[:, :, 0]))

    attn_rows, log_totals = lax.map(attend, jnp.arange(block_count))
    attn_heads = attn_rows.reshape(per_pair, lane_count, head_local * HEAD)
    attn_tok = lax.all_to_all(attn_heads, "seq", split_axis=1, concat_axis=2, tiled=True).reshape(
        slot_count, model_width
    )
    branch = jnp.dot(attn_tok, full_dense, preferred_element_type=jnp.float32) + bias_dense.astype(
        jnp.float32
    )
    resid = hidden + branch
    normed_two = norm_rows(resid, gain_two32, bias_two32).astype(jnp.bfloat16)
    upper = jnp.dot(normed_two, full_up, preferred_element_type=jnp.float32) + bias_up.astype(
        jnp.float32
    )
    activ_low = gelu_tanh(upper).astype(jnp.bfloat16)
    down = jnp.dot(activ_low, full_down, preferred_element_type=jnp.float32) + bias_down.astype(
        jnp.float32
    )
    block_out = (resid + down).astype(jnp.bfloat16)
    again = (
        lax.all_gather(params[0], "shard", axis=0, tiled=True),
        lax.all_gather(params[1], "shard", axis=0, tiled=True),
        lax.all_gather(params[2], "shard", axis=0, tiled=True),
        lax.all_gather(params[3], "shard", axis=0, tiled=True),
        lax.all_gather(params[4], "shard", axis=0, tiled=True),
        lax.all_gather(params[5], "shard", axis=0, tiled=True),
        lax.all_gather(params[6], "shard", axis=0, tiled=True),
        lax.all_gather(params[7], "shard", axis=0, tiled=True),
        lax.all_gather(params[8], "shard", axis=0, tiled=True),
        lax.all_gather(params[9], "shard", axis=0, tiled=True),
        lax.all_gather(params[10], "shard", axis=0, tiled=True),
        lax.all_gather(params[11], "shard", axis=0, tiled=True),
    )
    back_qkv, back_dense, back_gain_one, back_gain_two, back_up, back_down = (
        again[2],
        again[4],
        again[0],
        again[6],
        again[8],
        again[10],
    )
    cot_low = recv_cot.reshape(slot_count, model_width)
    cot_full = cot_low.astype(jnp.float32)
    grad_down = jnp.dot(activ_low.T, cot_low, preferred_element_type=jnp.float32)
    grad_bdown = jnp.sum(cot_full, axis=0)
    grad_activ = jnp.dot(cot_low, back_down.T, preferred_element_type=jnp.float32)
    upper_pull = jax.vjp(gelu_tanh, upper)[1]
    grad_upper = upper_pull(grad_activ)[0].astype(jnp.bfloat16)
    grad_up = jnp.dot(normed_two.T, grad_upper, preferred_element_type=jnp.float32)
    grad_bup = jnp.sum(grad_upper.astype(jnp.float32), axis=0)
    grad_norm_two = jnp.dot(grad_upper, back_up.T, preferred_element_type=jnp.float32)
    norm_two_pull = jax.vjp(norm_rows, resid, back_gain_two.astype(jnp.float32), bias_two32)[1]
    grad_resid_ln, grad_gain_two, grad_bias_two = norm_two_pull(grad_norm_two)
    grad_resid = cot_full + grad_resid_ln
    grad_branch = grad_resid.astype(jnp.bfloat16)
    grad_dense = jnp.dot(attn_tok.T, grad_branch, preferred_element_type=jnp.float32)
    grad_bdense = jnp.sum(grad_branch.astype(jnp.float32), axis=0)
    grad_attn = jnp.dot(grad_branch, back_dense.T, preferred_element_type=jnp.float32).astype(
        jnp.bfloat16
    )
    grad_attn = grad_attn.reshape(per_pair, shard_count, model_width)
    grad_attn_heads = lax.all_to_all(
        grad_attn, "seq", split_axis=2, concat_axis=1, tiled=True
    ).reshape(group_cap, head_local, HEAD)

    def back_step(carry, block_id):
        grad_keys, grad_values = carry
        begin = block_id * q_block
        query_rows = lax.dynamic_slice_in_dim(queries, begin, q_block)
        grad_rows = lax.dynamic_slice_in_dim(grad_attn_heads, begin, q_block)
        scored = block_scores(query_rows, begin)
        probs = jnp.exp(scored - log_totals[block_id][:, :, None])
        probs_low = probs.astype(jnp.bfloat16)
        grad_probs = jnp.einsum(
            "qhd,khd->hqk", grad_rows, values_all, preferred_element_type=jnp.float32
        )
        inner_sum = jnp.sum(probs * grad_probs, axis=2, keepdims=True)
        grad_raw = (probs * (grad_probs - inner_sum) * scale_factor).astype(jnp.bfloat16)
        grad_query = jnp.einsum(
            "hqk,khd->qhd", grad_raw, keys_all, preferred_element_type=jnp.float32
        )
        grad_keys = grad_keys + jnp.einsum(
            "hqk,qhd->khd", grad_raw, query_rows, preferred_element_type=jnp.float32
        )
        grad_values = grad_values + jnp.einsum(
            "hqk,qhd->khd", probs_low, grad_rows, preferred_element_type=jnp.float32
        )
        return ((grad_keys, grad_values), grad_query.astype(jnp.bfloat16))

    zero_heads = jnp.zeros((group_cap, head_local, HEAD), jnp.float32)
    (grad_keys, grad_values), grad_queries = lax.scan(
        back_step, (zero_heads, zero_heads), jnp.arange(block_count)
    )
    grad_queries = grad_queries.reshape(group_cap, head_local, HEAD)
    grad_stack = jnp.stack(
        [grad_queries, grad_keys.astype(jnp.bfloat16), grad_values.astype(jnp.bfloat16)], axis=1
    )
    grad_stack = grad_stack.reshape(per_pair, lane_count, 3, head_local * HEAD)
    grad_proj = lax.all_to_all(grad_stack, "seq", split_axis=1, concat_axis=3, tiled=True).reshape(
        slot_count, 3 * model_width
    )
    grad_qkv = jnp.dot(normed_low.T, grad_proj, preferred_element_type=jnp.float32)
    proj_sums = jnp.sum(grad_proj.astype(jnp.float32), axis=0)
    grad_bqv = jnp.concatenate([proj_sums[:model_width], proj_sums[2 * model_width :]])
    grad_norm_one = jnp.dot(grad_proj, back_qkv.T, preferred_element_type=jnp.float32)
    norm_one_pull = jax.vjp(norm_rows, hidden, back_gain_one.astype(jnp.float32), bias_one32)[1]
    grad_hidden_ln, grad_gain_one, grad_bias_one = norm_one_pull(grad_norm_one)
    tokens_grad = (grad_resid + grad_hidden_ln).astype(jnp.bfloat16)
    back_pair = (
        block_out.reshape(per_pair, shard_count, model_width),
        tokens_grad.reshape(per_pair, shard_count, model_width),
    )
    ret_out, ret_grad = (
        lax.all_to_all(back_pair[0], "shard", split_axis=1, concat_axis=1, tiled=True),
        lax.all_to_all(back_pair[1], "shard", split_axis=1, concat_axis=1, tiled=True),
    )
    row_here = jnp.arange(slot_count, dtype=jnp.int32)[:, None]
    seq_in = ((row_here >= row_start[None]) & (row_here < (row_start + seq_rows)[None])).astype(
        jnp.int32
    )
    home_group = dealing // per_group
    fetch_rows = jnp.sum(
        seq_in * ((seq_before[None] + row_here - row_start[None]) * shard_count + home_group[None]),
        axis=1,
    )
    fetch_live = jnp.sum(seq_in, axis=1) > 0

    def unpack_rows(received):
        taken = jnp.take(received.reshape(-1, model_width), fetch_rows, axis=0)
        return jnp.where(fetch_live[:, None], taken, jnp.zeros_like(taken))[None]

    grads = (
        grad_gain_one,
        grad_bias_one,
        grad_qkv,
        grad_bqv,
        grad_dense,
        grad_bdense,
        grad_gain_two,
        grad_bias_two,
        grad_up,
        grad_bup,
        grad_down,
        grad_bdown,
    )
    pieces = (
        lax.psum_scatter(
            grads[0].astype(jnp.bfloat16), "shard", scatter_dimension=0, tiled=True
        ).astype(jnp.float32),
        lax.psum_scatter(
            grads[1].astype(jnp.bfloat16), "shard", scatter_dimension=0, tiled=True
        ).astype(jnp.float32),
        lax.psum_scatter(
            grads[2].astype(jnp.bfloat16), "shard", scatter_dimension=0, tiled=True
        ).astype(jnp.float32),
        lax.psum_scatter(
            grads[3].astype(jnp.bfloat16), "shard", scatter_dimension=0, tiled=True
        ).astype(jnp.float32),
        lax.psum_scatter(
            grads[4].astype(jnp.bfloat16), "shard", scatter_dimension=0, tiled=True
        ).astype(jnp.float32),
        lax.psum_scatter(
            grads[5].astype(jnp.bfloat16), "shard", scatter_dimension=0, tiled=True
        ).astype(jnp.float32),
        lax.psum_scatter(
            grads[6].astype(jnp.bfloat16), "shard", scatter_dimension=0, tiled=True
        ).astype(jnp.float32),
        lax.psum_scatter(
            grads[7].astype(jnp.bfloat16), "shard", scatter_dimension=0, tiled=True
        ).astype(jnp.float32),
        lax.psum_scatter(
            grads[8].astype(jnp.bfloat16), "shard", scatter_dimension=0, tiled=True
        ).astype(jnp.float32),
        lax.psum_scatter(
            grads[9].astype(jnp.bfloat16), "shard", scatter_dimension=0, tiled=True
        ).astype(jnp.float32),
        lax.psum_scatter(
            grads[10].astype(jnp.bfloat16), "shard", scatter_dimension=0, tiled=True
        ).astype(jnp.float32),
        lax.psum_scatter(
            grads[11].astype(jnp.bfloat16), "shard", scatter_dimension=0, tiled=True
        ).astype(jnp.float32),
    )
    summed = (
        lax.psum(pieces[0].astype(jnp.bfloat16), "seq").astype(jnp.float32),
        lax.psum(pieces[1].astype(jnp.bfloat16), "seq").astype(jnp.float32),
        lax.psum(pieces[2].astype(jnp.bfloat16), "seq").astype(jnp.float32),
        lax.psum(pieces[3].astype(jnp.bfloat16), "seq").astype(jnp.float32),
        lax.psum(pieces[4].astype(jnp.bfloat16), "seq").astype(jnp.float32),
        lax.psum(pieces[5].astype(jnp.bfloat16), "seq").astype(jnp.float32),
        lax.psum(pieces[6].astype(jnp.bfloat16), "seq").astype(jnp.float32),
        lax.psum(pieces[7].astype(jnp.bfloat16), "seq").astype(jnp.float32),
        lax.psum(pieces[8].astype(jnp.bfloat16), "seq").astype(jnp.float32),
        lax.psum(pieces[9].astype(jnp.bfloat16), "seq").astype(jnp.float32),
        lax.psum(pieces[10].astype(jnp.bfloat16), "seq").astype(jnp.float32),
        lax.psum(pieces[11].astype(jnp.bfloat16), "seq").astype(jnp.float32),
    )
    return (
        unpack_rows(ret_out),
        unpack_rows(ret_grad),
        summed[0],
        summed[1],
        summed[2],
        summed[3],
        summed[4],
        summed[5],
        summed[6],
        summed[7],
        summed[8],
        summed[9],
        summed[10],
        summed[11],
    )


def solution(mesh):
    in_specs = (
        P(("seq", "shard"), None, None),
        P(("seq", "shard"), None, None),
        P(),
        P("shard"),
        P("shard"),
        P("shard", None),
        P("shard"),
        P("shard", None),
        P("shard"),
        P("shard"),
        P("shard"),
        P("shard", None),
        P("shard"),
        P("shard", None),
        P("shard"),
    )
    out_specs = (
        P(("seq", "shard"), None, None),
        P(("seq", "shard"), None, None),
        P("shard"),
        P("shard"),
        P("shard", None),
        P("shard"),
        P("shard", None),
        P("shard"),
        P("shard"),
        P("shard"),
        P("shard", None),
        P("shard"),
        P("shard", None),
        P("shard"),
    )
    return jax.shard_map(
        per_device, mesh=mesh, in_specs=in_specs, out_specs=out_specs, check_vma=False
    )
```

profile of v0, /device:TPU:0, one launch (start us, length us, event | category | flops | bytes accessed | tf_op | source)
XLA Modules:
  0.0 1107.4 jit_solution(7983633704515108988)
XLA Ops:
  30.8 82.2 %all-reduce.15 = (bf16[1024]{0:T(1024)(128)(2,1)S(1)}, bf16[1024]{0:T(1024)(128)(2,1)S(1)}, bf16[1024]{0:T(1024)(128)(2,1)}, bf16[1024]{0:T(1024)(128)(2,1)}, bf16[1024]{0:T(1024)(128)(2,1)}) all-reduce(bf16[1024]{0:T(1024)(128)(2,1)S(1)} %dynamic-update-slice.1, ...), channel_id=1, replica_groups=mesh['seq'=2,'shard'=16] {'shard'}, use_global_device_ids=true, to_apply=%add.1 | all-reduce | flops 5120 | bytes 20480
  112.9 18.0 %all-gather = bf16[16,1,128]{2,1,0:T(2,128)(2,1)S(1)} all-gather(bf16[1,1,128]{2,1,0:T(2,128)(2,1)S(1)} %bitcast.199), channel_id=1, replica_groups=mesh['seq'=2,'shard'=16] {'shard'}, dimensions={0}, use_global_device_ids=true | all-gather | bytes 4352 | tf_op jit(solution)/shard_map/all_gather | solution.py:119
  152.8 16.1 %copy.165 = bf16[32,16,3,1024]{0,1,2,3:T(8,128)(2,1)} copy(bf16[32,16,3,1024]{3,2,1,0:T(4,128)(2,1)} %reshape.616) | data formatting | bytes 6291456 | tf_op jit(solution)/shard_map/reshape | solution.py:156
  168.9 19.8 %reshape.721 = bf16[2,2,393216]{2,1,0:T(2,128)(2,1)} reshape(bf16[1024,3,16,32]{3,2,1,0:T(8,128)(2,1)} %bitcast.173) | data formatting | bytes 6291456
  196.2 34.7 %all-to-all-done.1 = bf16[2,2,393216]{2,1,0:T(2,128)(2,1)} async-done(((bf16[2,2,393216]{2,1,0:T(2,128)(2,1)}), bf16[2,2,393216]{2,1,0:T(2,128)(2,1)}, u32[]{:S(2)}, u32[]{:S(2)}) %all-to-all-start.1) | async-done | bytes 3145760 | tf_op jit(solution)/shard_map/all_to_all | solution.py:157
  235.5 14.7 %reshape.722 = bf16[1024,3,16,32]{3,2,1,0:T(8,128)(2,1)} reshape(bf16[2,2,393216]{2,1,0:T(2,128)(2,1)} %all-to-all-done.1) | data formatting | bytes 6291456
  250.2 20.1 %copy.193 = bf16[32,16,3,2,512]{4,3,1,2,0:T(2,128)(2,1)} copy(bf16[32,16,3,2,512]{0,1,2,4,3:T(8,128)(2,1)} %bitcast.174) | data formatting | bytes 6291456 | tf_op jit(solution)/shard_map/all_to_all | solution.py:157
  297.2 32.3 %while.28 = (s32[]{:T(128)}, bf16[2,512,8,64]{1,3,2,0:T(8,128)(2,1)S(1)}, f32[2,8,512]{2,1,0:T(8,128)S(1)}, s32[2]{0:T(128)S(1)}, s32[1024]{0:T(1024)S(1)}, /*in...) while((s32[]{:T(128)}, ...), condition=%wide.region_10.12_spmd.clone, body=%wide.region_7.11_spmd.clone.sunk | while | flops 1119090688 | bytes 58909224 | solution.py:200
  340.6 22.3 %all-gather.1 = bf16[16,1,256]{2,1,0:T(2,128)(2,1)S(1)} all-gather(bf16[1,1,256]{2,1,0:T(2,128)(2,1)S(1)} %reshape.686), channel_id=1, replica_groups=mesh['seq'=2,'shard'=16] {'shard'}, dimensions={0}, use_global_device_ids=true | all-gather | bytes 8704 | tf_op jit(solution)/shard_map/all_gather | solution.py:125
  373.1 11.9 %fusion.89 = f32[512,4096]{1,0:T(8,128)} fusion(bf16[1024,4096]{1,0:T(8,128)(2,1)} %all-gather.11.cloned.1.call-done, f32[512,1024]{1,0:T(8,128)} %copy-done.12, f32[1024]{0:T(1024)S(1)} %convert_element_type.251, f32[1024]{0:T(1024)S(1)} %convert_element_type.250, f32[512]{0:T(512)S(1)} %fusion.84, f32[512]{0:T(512)S(1)} %broadcast_multiply_fusion.1), kind=kOutput, calls=%fused_computation.162 | convolution fusion | flops 4297588736 | bytes 18886656 | tf_op jit(solution)/shard_map/dot_general | solution.py:210
  384.9 15.3 %fusion.91 = (bf16[4096]{0:T(1024)(128)(2,1)}, bf16[512,4096]{1,0:T(8,128)(2,1)S(1)}) fusion(f32[512,4096]{1,0:T(8,128)} %fusion.89, f32[4096]{0:T(1024)S(1)} %bitcast.192, bf16[512,1024]{1,0:T(8,128)(2,1)S(1)} %bitcast.179, bf16[4096,1024]{1,0:T(8,128)(2,1)} %all-gather.13.cloned.1.call-done), kind=kOutput, calls=%fused_computation.164 | convolution fusion | flops 4349489152 | bytes 22044672 | tf_op jit(solution)/shard_map/dot_general | solution.py:244
  464.2 160.5 %while.29 = (s32[]{:T(128)}, f32[1024,8,64]{0,2,1:T(8,128)}, f32[1024,8,64]{0,2,1:T(8,128)S(1)}, bf16[2,512,8,64]{1,3,2,0:T(8,128)(2,1)}, s32[2]{0:T(128)S(1)}, ...) while((s32[]{:T(128)}, f32[1024,8,64]{0,2,1:T(8,128)}, ...), condition=%wide.region_18.20_spmd.clone, body=%wide.region_16.19_spmd.clone.sunk | while | flops 2756980736 | bytes 208250016 | solution.py:289
  490.6 23.4 %bitcast_add_fusion.5 = f32[1024,8,64]{0,2,1:T(8,128)} fusion(f32[1024,8,64]{0,2,1:T(8,128)} %get-tuple-element.773, f32[8,512,1024]{2,1,0:T(8,128)} %subtract_exponential_fusion.3, f32[8,512,1024]{2,1,0:T(8,128)} %fusion.159, pred[]{:T(512)S(6)} %compare.7, bf16[1024,8,64]{0,2,1:T(8,128)(2,1)} %get-tuple-element.797, s32[]{:T(128)S(6)} %select_n.118), kind=kOutput, calls=%fused_computation.38.clone.1 | convolution fusion | flops 558896128 | bytes 71827464 | tf_op jit(solution)/shard_map/while/body/eval_jaxpr/hqk,qhd->khd/dot_general | solution.py:280
  513.9 22.7 %fusion.160 = bf16[2,512,8,64]{1,3,2,0:T(8,128)(2,1)} fusion(bf16[2,512,8,64]{1,3,2,0:T(8,128)(2,1)} %get-tuple-element.775, s32[]{:T(128)} %get-tuple-element.772, bf16[1024,8,64]{0,2,1:T(8,128)(2,1)} %get-tuple-element.800, f32[8,512,1024]{2,1,0:T(8,128)} %subtract_exponential_fusion.3, f32[8,512,1024]{2,1,0:T(8,128)} %fusion.159), kind=kOutput, calls=%fused_computation.43.clone.1 | convolution fusion | flops 558109696 | bytes 68682240 | tf_op jit(solution)/shard_map/while/body/eval_jaxpr/hqk,khd->qhd/dot_general | solution.py:277
  570.3 24.0 %bitcast_add_fusion.5 = f32[1024,8,64]{0,2,1:T(8,128)} fusion(f32[1024,8,64]{0,2,1:T(8,128)} %get-tuple-element.773, f32[8,512,1024]{2,1,0:T(8,128)} %subtract_exponential_fusion.3, f32[8,512,1024]{2,1,0:T(8,128)} %fusion.159, pred[]{:T(512)S(6)} %compare.7, bf16[1024,8,64]{0,2,1:T(8,128)(2,1)} %get-tuple-element.797, s32[]{:T(128)S(6)} %select_n.118), kind=kOutput, calls=%fused_computation.38.clone.1 | convolution fusion | flops 558896128 | bytes 71827464 | tf_op jit(solution)/shard_map/while/body/eval_jaxpr/hqk,qhd->khd/dot_general | solution.py:280
  594.3 22.7 %fusion.160 = bf16[2,512,8,64]{1,3,2,0:T(8,128)(2,1)} fusion(bf16[2,512,8,64]{1,3,2,0:T(8,128)(2,1)} %get-tuple-element.775, s32[]{:T(128)} %get-tuple-element.772, bf16[1024,8,64]{0,2,1:T(8,128)(2,1)} %get-tuple-element.800, f32[8,512,1024]{2,1,0:T(8,128)} %subtract_exponential_fusion.3, f32[8,512,1024]{2,1,0:T(8,128)} %fusion.159), kind=kOutput, calls=%fused_computation.43.clone.1 | convolution fusion | flops 558109696 | bytes 68682240 | tf_op jit(solution)/shard_map/while/body/eval_jaxpr/hqk,khd->qhd/dot_general | solution.py:277
  652.5 35.4 %all-to-all-done.6 = bf16[32,32,3,512]{3,0,2,1:T(8,128)(2,1)} async-done(((bf16[32,32,3,512]{3,0,2,1:T(8,128)(2,1)}), bf16[32,32,3,512]{3,0,2,1:T(8,128)(2,1)}, u32[]{:S(2)}, u32[]{:S(2)}) %all-to-all-start.6) | async-done | bytes 3145760 | tf_op jit(solution)/shard_map/all_to_all | solution.py:297
  722.9 13.6 %convolution_convert_fusion = bf16[4096,1024]{1,0:T(8,128)(2,1)} fusion(bf16[512,1024]{1,0:T(8,128)(2,1)S(1)} %bitcast.180, f32[512,4096]{1,0:T(8,128)} %fusion.89, f32[4096]{0:T(1024)S(1)} %bitcast.193), kind=kOutput, calls=%fused_computation.72 | convolution fusion | flops 4320133120 | bytes 17842176 | tf_op jit(solution)/shard_map/dot_general | solution.py:242
  757.1 59.0 %all-reduce.14 = (bf16[1024]{0:T(1024)(128)(2,1)S(1)}, bf16[1024]{0:T(1024)(128)(2,1)S(1)}, bf16[1024]{0:T(1024)(128)(2,1)S(1)}, bf16[2048]{0:T(1024)(128)(2,1)S...) all-reduce(bf16[1024]{0:T(1024)(128)(2,1)S(1)} %dynamic-update-slic, ...), channel_id=1, replica_groups=mesh['seq'=2,'shard'=16] {'shard'}, use_global_device_ids=true, to_apply=%add.5 | all-reduce | flops 13312 | bytes 53248
  838.4 35.1 %all-to-all-done.3 = bf16[32,16,1024]{2,0,1:T(8,128)(2,1)} async-done(((bf16[32,16,1024]{2,0,1:T(8,128)(2,1)}), bf16[32,16,1024]{2,0,1:T(8,128)(2,1)}, u32[]{:S(2)}, u32[]{:S(2)}) %all-to-all-start.3) | async-done | bytes 1048608 | tf_op jit(solution)/shard_map/all_to_all | solution.py:312
  873.5 13.9 %all-to-all-start.7 = ((bf16[32,16,1024]{2,0,1:T(8,128)(2,1)}), bf16[32,16,1024]{2,0,1:T(8,128)(2,1)S(1)}, u32[]{:S(2)}, u32[]{:S(2)}) async-start(bf16[32,16,1024]{2,0,1:T(8,128)(2,1)} %copy.191), calls=%async_computation.7 | async-start | bytes 2097152 | tf_op jit(solution)/shard_map/all_to_all | solution.py:313
  887.5 44.5 %reduce-scatter.9.cloned.1.call-done = bf16[64,4096]{1,0:T(8,128)(2,1)} async-done(((bf16[1024,4096]{1,0:T(8,128)(2,1)}), bf16[64,4096]{1,0:T(8,128)(2,1)}) %reduce-scatter.9.cloned.1.call-update) | async-done | bytes 524304 | tf_op jit(solution)/shard_map/reduce_scatter | solution.py:369
  932.1 108.4 %reduce-scatter.11.cloned.1.call-done = bf16[256,1024]{1,0:T(8,128)(2,1)} async-done(((bf16[4096,1024]{1,0:T(8,128)(2,1)}), bf16[256,1024]{1,0:T(8,128)(2,1)}) %reduce-scatter.11.cloned.1.call-update) | async-done | bytes 524304 | tf_op jit(solution)/shard_map/reduce_scatter | solution.py:375
  1060.5 34.3 %all-reduce.20.cloned.1.call-done = (bf16[64,3072]{1,0:T(8,128)(2,1)}, bf16[64,1024]{1,0:T(8,128)(2,1)}, bf16[64,4096]{1,0:T(8,128)(2,1)}, bf16[256,1024]{1,0:T(8,128)(2,1)}) async-done(((bf16[64,3072]{1,0:T(8,128)(2,1)}, bf16[64,1024]{1,0:T(8,128)(2,1)}, bf16[64,4096]{1,0:T(8,128)(2,1)}, bf16[256,1024]{1,0:T(8,128)(2,1)}), (bf16[64,3072]{1,0:T(8,128)(2,1)}, bf16[64,1024]{1,0:T(8,128)(2,1)}, ...) | async-done | bytes 1572880 | tf_op jit(solution)/shard_map/psum | solution.py:385
  (397 shorter events, 390.1 us)
Async XLA Ops:
  7.2 127.9 %all-gather.7.cloned.1.call-start = ((), (), s32[]{:S(2)}) async-start(), calls=%async_computation.12 | async-start | bytes 6684672 | tf_op jit(solution)/shard_map/all_gather | solution.py:118
  7.9 359.8 %all-gather.9.cloned.1.call-start = ((), (), s32[]{:S(2)}) async-start(), calls=%async_computation.13 | async-start | bytes 2228224 | tf_op jit(solution)/shard_map/all_gather | solution.py:120
  8.7 364.4 %all-gather.11.cloned.1.call-start = ((), (), s32[]{:S(2)}) async-start(), calls=%async_computation.14 | async-start | bytes 8912896 | tf_op jit(solution)/shard_map/all_gather | solution.py:124
  17.1 95.8 %copy-start.57 = (bf16[128]{0:T(256)(128)(2,1)S(1)}, bf16[128]{0:T(256)(128)(2,1)}, u32[]{:S(2)}) copy-start(bf16[128]{0:T(256)(128)(2,1)} %param.27) | copy-start | bytes 772
  20.9 110.0 %all-to-all-start = ((bf16[32,16,1024]{2,0,1:T(8,128)(2,1)}), bf16[32,16,1024]{2,0,1:T(8,128)(2,1)S(1)}, u32[]{:S(2)}, u32[]{:S(2)}) async-start(bf16[32,16,1024]{2,0,1:T(8,128)(2,1)} %get-tuple-element.521), calls=%async_computation | async-start | bytes 2097152 | tf_op jit(solution)/shard_map/all_to_all | solution.py:83
  188.8 42.1 %all-to-all-start.1 = ((bf16[2,2,393216]{2,1,0:T(2,128)(2,1)}), bf16[2,2,393216]{2,1,0:T(2,128)(2,1)}, u32[]{:S(2)}, u32[]{:S(2)}) async-start(bf16[2,2,393216]{2,1,0:T(2,128)(2,1)} %reshape.721), calls=%async_computation.1 | async-start | bytes 6291456 | tf_op jit(solution)/shard_map/all_to_all | solution.py:157
  194.0 190.9 %all-gather.13.cloned.1.call-start = ((), (), s32[]{:S(2)}) async-start(), calls=%async_computation.15 | async-start | bytes 8912896 | tf_op jit(solution)/shard_map/all_gather | solution.py:126
  230.9 106.0 %all-to-all-start.4 = ((bf16[32,16,1024]{2,0,1:T(8,128)(2,1)}), bf16[32,16,1024]{2,0,1:T(8,128)(2,1)}, u32[]{:S(2)}, u32[]{:S(2)}) async-start(bf16[32,16,1024]{2,0,1:T(8,128)(2,1)} %get-tuple-element.520), calls=%async_computation.4 | async-start | bytes 2097152 | tf_op jit(solution)/shard_map/all_to_all | solution.py:84
  336.9 29.4 %all-to-all-start.2 = ((bf16[32,32,512]{2,0,1:T(8,128)(2,1)}), bf16[32,32,512]{2,0,1:T(8,128)(2,1)S(1)}, u32[]{:S(2)}, u32[]{:S(2)}) async-start(bf16[32,32,512]{2,0,1:T(8,128)(2,1)} %copy.172), calls=%async_computation.2 | async-start | bytes 2097152 | tf_op jit(solution)/shard_map/all_to_all | solution.py:202
  340.5 65.3 %copy-start.41 = (f32[1024]{0:T(1024)}, f32[1024]{0:T(1024)S(1)}, u32[]{:S(2)}) copy-start(f32[1024]{0:T(1024)S(1)} %convert_element_type.250) | copy-start | bytes 12292
  366.3 40.2 %copy-start.9 = (bf16[32,16,1024]{2,1,0:T(8,128)(2,1)}, bf16[32,16,1024]{2,1,0:T(8,128)(2,1)S(1)}, u32[]{:S(2)}) copy-start(bf16[32,16,1024]{2,1,0:T(8,128)(2,1)S(1)} %copy.177) | copy-start | bytes 3145732
  422.4 19.1 %all-to-all-start.5 = ((bf16[2,2,131072]{2,1,0:T(2,128)(2,1)}), bf16[2,2,131072]{2,1,0:T(2,128)(2,1)}, u32[]{:S(2)}, u32[]{:S(2)}) async-start(bf16[2,2,131072]{2,1,0:T(2,128)(2,1)} %reshape.723), calls=%async_computation.5 | async-start | bytes 2097152 | tf_op jit(solution)/shard_map/all_to_all | solution.py:260
  426.8 460.7 %reduce-scatter.7.cloned.1.call-start = ((), (), s32[]{:S(2)}) async-start(), calls=%async_computation.17 | async-start | bytes 2228224 | tf_op jit(solution)/shard_map/reduce_scatter | solution.py:357
  646.3 41.7 %all-to-all-start.6 = ((bf16[32,32,3,512]{3,0,2,1:T(8,128)(2,1)}), bf16[32,32,3,512]{3,0,2,1:T(8,128)(2,1)}, u32[]{:S(2)}, u32[]{:S(2)}) async-start(bf16[32,32,3,512]{3,0,2,1:T(8,128)(2,1)} %copy.188), calls=%async_computation.6 | async-start | bytes 6291456 | tf_op jit(solution)/shard_map/all_to_all | solution.py:297
  651.6 235.9 %reduce-scatter.5.cloned.1.call-start = ((), (), s32[]{:S(2)}) async-start(), calls=%async_computation.16 | async-start | bytes 6684672 | tf_op jit(solution)/shard_map/reduce_scatter | solution.py:351
  710.6 221.4 %reduce-scatter.9.cloned.1.call-start = ((), (), s32[]{:S(2)}) async-start(), calls=%async_computation.18 | async-start | bytes 8912896 | tf_op jit(solution)/shard_map/reduce_scatter | solution.py:369
  721.6 318.9 %reduce-scatter.11.cloned.1.call-start = ((), (), s32[]{:S(2)}) async-start(), calls=%async_computation.19 | async-start | bytes 8912896 | tf_op jit(solution)/shard_map/reduce_scatter | solution.py:375
  754.3 61.8 %copy-start.15 = (f32[512,1024]{1,0:T(8,128)S(1)}, f32[512,1024]{1,0:T(8,128)}, u32[]{:S(2)}) copy-start(f32[512,1024]{1,0:T(8,128)} %copy-done.12) | copy-start | bytes 6291460
  829.2 44.3 %all-to-all-start.3 = ((bf16[32,16,1024]{2,0,1:T(8,128)(2,1)}), bf16[32,16,1024]{2,0,1:T(8,128)(2,1)}, u32[]{:S(2)}, u32[]{:S(2)}) async-start(bf16[32,16,1024]{2,0,1:T(8,128)(2,1)} %copy.174), calls=%async_computation.3 | async-start | bytes 2097152 | tf_op jit(solution)/shard_map/all_to_all | solution.py:312
  836.9 205.6 %copy-start.53 = (s32[16]{0:T(128)S(1)}, s32[16]{0:T(128)}, u32[]{:S(2)}) copy-start(s32[16]{0:T(128)} %copy-done.52) | copy-start | bytes 196
  836.9 205.6 %copy-start.59 = (s32[16]{0:T(128)S(1)}, s32[16]{0:T(128)}, u32[]{:S(2)}) copy-start(s32[16]{0:T(128)} %copy-done.58) | copy-start | bytes 196
  873.5 182.7 %all-to-all-start.7 = ((bf16[32,16,1024]{2,0,1:T(8,128)(2,1)}), bf16[32,16,1024]{2,0,1:T(8,128)(2,1)S(1)}, u32[]{:S(2)}, u32[]{:S(2)}) async-start(bf16[32,16,1024]{2,0,1:T(8,128)(2,1)} %copy.191), calls=%async_computation.7 | async-start | bytes 2097152 | tf_op jit(solution)/shard_map/all_to_all | solution.py:313
  887.4 207.4 %all-reduce.20.cloned.1.call-start = ((), (), s32[]{:S(2)}) async-start(), calls=%async_computation.20 | async-start | bytes 3145728 | tf_op jit(solution)/shard_map/psum | solution.py:385
  1058.8 41.9 %copy-start.1 = (bf16[1,512,1024]{2,1,0:T(8,128)(2,1)S(1)}, bf16[1,512,1024]{2,1,0:T(8,128)(2,1)}, u32[]{:S(2)}) copy-start(bf16[1,512,1024]{2,1,0:T(8,128)(2,1)} %param.21) | copy-start | bytes 3145732
  (64 other events, 529.0 us)
Sparse Core Ops, SparseCore 0:
  10.3 77.3 all-gather.6
  89.9 40.1 all-gather.8
  132.2 73.6 all-gather.10
  207.9 89.5 all-gather.12
  431.2 59.3 reduce-scatter.6
  710.7 81.6 reduce-scatter.4
  796.4 135.5 reduce-scatter.8
  936.1 104.3 reduce-scatter.10
  1043.0 51.7 all-reduce.19
where the time goes:
time: 1120 us; the launch traced here: 1110 us
  waiting for transfers between devices  306 us (27%)
  matrix products  265 us (24%)
  local copies, waits for them, and re-layouts  223 us (20%)
  blocking collectives  186 us (17%)
  other arithmetic  53 us (5%)
  starting transfers between devices  49.2 us (4%)
  between operations  17.9 us (2%)
    unnamed x2, blocking collectives  141 us
    reduce_scatter x1, waiting for transfers between devices, per_device(): lax.psum_scatter(grads[10].astype(jnp.bfloat16), 'shard', scatter_dimensi...  108 us
    unnamed x172, local copies, waits for them, and re-layouts  69.6 us
    dot_general x2, matrix products, back_step(): jnp.einsum('hqk,qhd->khd', grad_raw, query_rows, preferred_element_type=j...  47.3 us
    dot_general x2, matrix products, back_step(): jnp.einsum('hqk,khd->qhd', grad_raw, keys_all, preferred_element_type=jnp...  45.3 us
    reduce_scatter x1, waiting for transfers between devices, per_device(): lax.psum_scatter(grads[8].astype(jnp.bfloat16), 'shard', scatter_dimensio...  44.5 us
    all_to_all x1, waiting for transfers between devices, per_device(): lax.all_to_all(grad_stack, 'seq', split_axis=1, concat_axis=3, tiled=True)  35.4 us
    all_to_all x1, waiting for transfers between devices, per_device(): lax.all_to_all(back_pair[0], 'shard', split_axis=1, concat_axis=1, tiled=...  35.1 us
  transfers between devices with their start and end apart: 17, of which 7 were waited for; matrix products, arithmetic and copies ran while one was open for 44% of the time, Pallas kernels for 0%

commit v1 on v0

v1 whole, which is shorter than its diff:
```python
import functools

import jax
import jax.numpy as jnp
from jax import lax
from jax.experimental import pallas as pl
from jax.experimental.pallas import tpu as pltpu
from jax.sharding import PartitionSpec as P

HEADS = 16
HEAD = 64
ROWS = 8

epsilon = 1e-05
masked_score = -1e30
f32 = jnp.float32
bf16 = jnp.bfloat16


def gelu_tanh(values):
    return (
        0.5
        * values
        * (1.0 + jnp.tanh(0.7978845608028654 * (values + 0.044715 * values * values * values)))
    )


def normalize(hidden):
    center = hidden - jnp.mean(hidden, axis=-1, keepdims=True)
    spread = jnp.mean(center * center, axis=-1, keepdims=True)
    root = lax.rsqrt(spread + epsilon)
    return center * root, root


def norm_pull(grad, gain, xhat, root):
    scaled = grad * gain
    return root * (
        scaled
        - jnp.mean(scaled, axis=-1, keepdims=True)
        - xhat * jnp.mean(scaled * xhat, axis=-1, keepdims=True)
    )


def slot_ids(first, count, lanes):
    place = first + lax.broadcasted_iota(jnp.int32, (count, 1), 0)
    block, inside = place // (ROWS * lanes), place % (ROWS * lanes)
    return (block * ROWS + inside % ROWS) * lanes + inside // ROWS


def attn_mask(scored, allowed):
    return jnp.where(allowed, scored, masked_score)


def attn_fwd_kernel(lanes, tile, one_seq, slope_ref, idc_ref, idr_ref, beginc_ref, q_ref, k_ref, v_ref, o_ref):
    tokens = q_ref.shape[0]
    block = ROWS * lanes
    lane_id = lax.broadcasted_iota(jnp.int32, (1, 2 * HEAD), 1)
    for b in range(tokens // block):
        end = (b + 1) * block

        def step(t, _):
            at = pl.ds(pl.multiple_of(b * block + t * tile, tile), tile)
            q = q_ref[at, :] * jnp.asarray(HEAD**-0.5, bf16)
            ids_q = idc_ref[at, :]
            both = None
            for j in range(2):
                mine = (lane_id // HEAD) == j
                qj = jnp.where(mine, q, jnp.zeros_like(q))
                s = lax.dot_general(
                    qj, k_ref[:end, :], (((1,), (1,)), ((), ())), preferred_element_type=f32
                )
                s = s + slope_ref[0, 0, j] * idr_ref[:, :end]
                if one_seq:
                    own = s[:, b * block :]
                    own = attn_mask(own, idr_ref[:, b * block : end] <= ids_q)
                    s = jnp.concatenate([s[:, : b * block], own], axis=1) if b else own
                else:
                    ids_k = idr_ref[:, :end]
                    s = attn_mask(s, (ids_k <= ids_q) & (ids_k >= beginc_ref[at, :]))
                top = jnp.max(s, axis=1, keepdims=True)
                e = jnp.exp(s - top)
                total = jnp.sum(e, axis=1, keepdims=True)
                o = jnp.dot(e.astype(bf16), v_ref[:end, :], preferred_element_type=f32) / total
                both = o if both is None else jnp.where(mine, o, both)
            o_ref[at, :] = both.astype(bf16)
            return 0

        lax.fori_loop(0, block // tile, step, 0)


def attn_bwd_kernel(
    lanes, tile, one_seq, slope_ref, idc_ref, idr_ref, beginr_ref, q_ref, k_ref, v_ref, do_ref,
    dq_ref, dk_ref, dv_ref, dk_acc, dv_acc, bias_acc,
):
    tokens = q_ref.shape[0]
    block = ROWS * lanes
    lane_id = lax.broadcasted_iota(jnp.int32, (1, 2 * HEAD), 1)
    dk_acc[...] = jnp.zeros_like(dk_acc)
    dv_acc[...] = jnp.zeros_like(dv_acc)
    for j in range(2):
        bias_acc[j] = jnp.broadcast_to(slope_ref[0, 0, j] * idc_ref[...], (tokens, tile))
    for b in range(tokens // block):
        end = (b + 1) * block

        def step(t, _):
            at = pl.ds(pl.multiple_of(b * block + t * tile, tile), tile)
            q = q_ref[at, :] * jnp.asarray(HEAD**-0.5, bf16)
            do = do_ref[at, :]
            ids_q = idr_ref[:, at]
            both = None
            for j in range(2):
                mine = (lane_id // HEAD) == j
                qj = jnp.where(mine, q, jnp.zeros_like(q))
                doj = jnp.where(mine, do, jnp.zeros_like(do))
                s = lax.dot_general(
                    k_ref[:end, :], qj, (((1,), (1,)), ((), ())), preferred_element_type=f32
                )
                s = s + bias_acc[j, :end, :]
                if one_seq:
                    own = s[b * block :, :]
                    own = attn_mask(own, idc_ref[b * block : end, :] <= ids_q)
                    s = jnp.concatenate([s[: b * block, :], own], axis=0) if b else own
                else:
                    ids_k = idc_ref[:end, :]
                    s = attn_mask(s, (ids_k <= ids_q) & (ids_k >= beginr_ref[:, at]))
                top = jnp.max(s, axis=0, keepdims=True)
                e = jnp.exp(s - top)
                probs = e * (1.0 / jnp.sum(e, axis=0, keepdims=True))
                dv_acc[:end, :] += jnp.dot(probs.astype(bf16), doj, preferred_element_type=f32)
                dp = lax.dot_general(
                    v_ref[:end, :], doj, (((1,), (1,)), ((), ())), preferred_element_type=f32
                )
                inner = jnp.sum(probs * dp, axis=0, keepdims=True)
                ds = (probs * (dp - inner)).astype(bf16)
                dk_acc[:end, :] += jnp.dot(ds, qj, preferred_element_type=f32)
                dq = lax.dot_general(
                    ds, k_ref[:end, :], (((0,), (0,)), ((), ())), preferred_element_type=f32
                )
                both = dq if both is None else jnp.where(mine, dq, both)
            dq_ref[at, :] = (both * (HEAD**-0.5)).astype(bf16)
            return 0

        lax.fori_loop(0, block // tile, step, 0)
    dk_ref[...] = dk_acc[...].astype(bf16)
    dv_ref[...] = dv_acc[...].astype(bf16)


def attn_shape(tokens, width, lanes):
    pairs = width // (2 * HEAD)
    tile = min(256, ROWS * lanes)
    return pairs, tile


def attention_forward(qkv, slopes, ids, begins, lanes, one_seq):
    tokens, width = qkv.shape[0], qkv.shape[1] // 3
    pairs, tile = attn_shape(tokens, width, lanes)
    column = lambda part: pl.BlockSpec((tokens, 2 * HEAD), lambda h, part=part: (0, part * pairs + h))
    whole = lambda a: pl.BlockSpec(a.shape, lambda h: (0, 0))
    idc, idr, beginc = ids[:, None], ids[None, :], begins[:, None]
    half = tokens * tokens * 5 // 8
    return pl.pallas_call(
        functools.partial(attn_fwd_kernel, lanes, tile, one_seq),
        grid=(pairs,),
        in_specs=[
            pl.BlockSpec((1, 1, 2), lambda h: (h, 0, 0), memory_space=pltpu.SMEM),
            whole(idc), whole(idr), whole(beginc), column(0), column(1), column(2),
        ],
        out_specs=pl.BlockSpec((tokens, 2 * HEAD), lambda h: (0, h)),
        out_shape=jax.ShapeDtypeStruct((tokens, width), bf16),
        compiler_params=pltpu.CompilerParams(vmem_limit_bytes=48 * 2**20),
        cost_estimate=pl.CostEstimate(
            flops=8 * pairs * half * HEAD * 2, transcendentals=2 * pairs * half, bytes_accessed=8 * tokens * width
        ),
        name="attention_forward",
    )(slopes.reshape(pairs, 1, 2), idc, idr, beginc, qkv, qkv, qkv)


def attention_backward(qkv, grad_out, slopes, ids, begins, lanes, one_seq):
    tokens, width = qkv.shape[0], qkv.shape[1] // 3
    pairs, tile = attn_shape(tokens, width, lanes)
    column = lambda part: pl.BlockSpec((tokens, 2 * HEAD), lambda h, part=part: (0, part * pairs + h))
    whole = lambda a: pl.BlockSpec(a.shape, lambda h: (0, 0))
    idc, idr, beginr = ids[:, None], ids[None, :], begins[None, :]
    out = jax.ShapeDtypeStruct((tokens, width), bf16)
    half = tokens * tokens * 5 // 8
    return pl.pallas_call(
        functools.partial(attn_bwd_kernel, lanes, tile, one_seq),
        grid=(pairs,),
        in_specs=[
            pl.BlockSpec((1, 1, 2), lambda h: (h, 0, 0), memory_space=pltpu.SMEM),
            whole(idc), whole(idr), whole(beginr), column(0), column(1), column(2), column(0),
        ],
        out_specs=[column(0)] * 3,
        out_shape=[out] * 3,
        scratch_shapes=[
            pltpu.VMEM((tokens, 2 * HEAD), f32), pltpu.VMEM((tokens, 2 * HEAD), f32), pltpu.VMEM((2, tokens, tile), f32),
        ],
        compiler_params=pltpu.CompilerParams(vmem_limit_bytes=56 * 2**20),
        cost_estimate=pl.CostEstimate(
            flops=20 * pairs * half * HEAD * 2, transcendentals=2 * pairs * half, bytes_accessed=14 * tokens * width
        ),
        name="attention_backward",
    )(slopes.reshape(pairs, 1, 2), idc, idr, beginr, qkv, qkv, qkv, grad_out)


def take(blocks, index, axis=0):
    return lax.dynamic_index_in_dim(blocks, index, axis, keepdims=False)


def seq_gather(block, axis):
    n, me = lax.axis_size("seq"), lax.axis_index("seq")
    shape = block.shape[:axis] + (n,) + block.shape[axis:]
    if n == 2:
        peer = lax.ppermute(block, "seq", [(0, 1), (1, 0)])
        return jnp.where(me == 0, jnp.stack([block, peer], axis), jnp.stack([peer, block], axis))
    whole = lax.dynamic_update_index_in_dim(jnp.zeros(shape, block.dtype), block, me, axis)
    for d in range(1, n):
        got = lax.ppermute(block, "seq", [(i, (i + d) % n) for i in range(n)])
        whole = lax.dynamic_update_index_in_dim(whole, got, (me - d) % n, axis)
    return whole


def seq_blocks(whole, axis, dtype):
    n, me = lax.axis_size("seq"), lax.axis_index("seq")
    got = [take(whole, me, axis)]
    for d in range(1, n):
        sent = take(whole, (me + d) % n, axis).astype(dtype)
        got.append(lax.ppermute(sent, "seq", [(i, (i + d) % n) for i in range(n)]))
    return got


def seq_sum(whole, axis, dtype=bf16):
    got = seq_blocks(whole, axis, dtype)
    return sum((g.astype(f32) for g in got[1:]), got[0].astype(f32))


def shard_factors(n):
    nc = 2 if n % 2 == 0 else 1
    nz = 4 if n % (4 * nc) == 0 else 1
    return nz, n // (nz * nc), nc


def shard_reduce(blocks, dtype):
    n, me = lax.axis_size("shard"), lax.axis_index("shard")
    sizes = shard_factors(n)
    blocks = blocks.reshape(sizes + blocks.shape[1:])
    place = (me // (sizes[1] * sizes[2]), me // sizes[2] % sizes[1], me % sizes[2])
    strides = (sizes[1] * sizes[2], sizes[2], 1)
    for axis in (2, 1, 0):
        size, mine, stride = sizes[axis], place[axis], strides[axis]
        total = take(blocks, mine, axis).astype(f32)
        for d in range(1, size):
            sent = take(blocks, (mine + d) % size, axis).astype(dtype)
            pairs = [
                (i, i - (i // stride % size) * stride + ((i // stride % size + d) % size) * stride)
                for i in range(n)
            ]
            total = total + lax.ppermute(sent, "shard", pairs).astype(f32)
        blocks = total if axis == 0 else total.astype(dtype)
    return blocks


def layout_tables(lengths, lane_count, group_count, per_group):
    seq_rows = lengths // lane_count
    row_start = jnp.cumsum(seq_rows) - seq_rows
    slot_rows = seq_rows.reshape(group_count, per_group)
    slot_start = row_start.reshape(group_count, per_group)
    slot_before = jnp.cumsum(slot_rows, axis=1) - slot_rows
    return seq_rows, row_start, slot_rows, slot_start, slot_before


def per_device(
    tokens, cotangent, lengths, first_gain, first_bias, qkv_weight, qv_bias, dense_weight, dense_bias,
    second_gain, second_bias, fc1_weight, fc1_bias, fc2_weight, fc2_bias,
):
    shards, seqs = lax.axis_size("shard"), lax.axis_size("seq")
    lanes = shards * seqs
    slots, width = tokens.shape[1], tokens.shape[2]
    rows = slots // shards
    cap = slots * seqs
    per_group = lengths.shape[0] // shards
    hidden_units = fc1_weight.shape[1]
    me, group = lax.axis_index("seq"), lax.axis_index("shard")
    blocks = rows // ROWS
    heads = width // HEAD // seqs
    part = heads * HEAD
    ff_part = hidden_units // shards // seqs

    qkv_half = take(qkv_weight.reshape(-1, 3, seqs, part), me, 2).reshape(-1, 3 * part)
    fc1_half = take(fc1_weight.reshape(-1, shards, seqs, ff_part), me, 2).reshape(-1, shards * ff_part)
    fc2_half = take(fc2_weight.reshape(seqs, ff_part, width), me, 0)
    small = jnp.concatenate(
        [first_gain, first_bias, qv_bias, dense_bias, second_gain, second_bias, fc1_bias, fc2_bias]
    )
    small_rows = -(-small.shape[0] // (3 * part))
    small_rows += -small_rows % 16
    small = jnp.pad(small, (0, small_rows * 3 * part - small.shape[0])).reshape(small_rows, 3 * part)
    gather = lambda a: lax.all_gather(a, "shard", axis=0, tiled=False)
    qkv_small = gather(jnp.concatenate([qkv_half, small], axis=0))
    own_rows = qkv_half.shape[0]
    full_qkv = qkv_small[:, :own_rows].reshape(width, 3 * part)
    smalls = qkv_small[:, own_rows:].reshape(shards, -1).astype(f32)
    full_dense = gather(dense_weight).reshape(width, width)
    full_up = gather(fc1_half).reshape(width, shards * ff_part)
    full_down = gather(fc2_half).reshape(shards * ff_part, width)
    cuts, at = [], 0
    for a in (first_gain, first_bias, qv_bias, dense_bias, second_gain, second_bias, fc1_bias, fc2_bias):
        cuts.append(smalls[:, at : at + a.shape[0]].reshape(-1))
        at += a.shape[0]
    gain_one, bias_one, bias_qv, bias_dense, gain_two, bias_two, bias_up, bias_down = cuts
    bias_q, bias_v = (take(bias_qv[i * width : (i + 1) * width].reshape(seqs, part), me) for i in (0, 1))
    bias_all = jnp.concatenate([bias_q, jnp.zeros_like(bias_q), bias_v])
    bias_up = take(bias_up.reshape(shards, seqs, ff_part), me, 1).reshape(-1)

    seq_rows, row_start, slot_rows, slot_start, slot_before = layout_tables(lengths, lanes, shards, per_group)
    row_in = jnp.arange(rows, dtype=jnp.int32)[None, :, None]
    inside = ((row_in >= slot_before[:, None]) & (row_in < (slot_before + slot_rows)[:, None])).astype(jnp.int32)
    send_live = jnp.sum(inside, axis=2) > 0
    send_row = jnp.sum(inside * (slot_start[:, None] + row_in - slot_before[:, None]), axis=2).reshape(-1)

    def to_groups(source):
        packed = jnp.take(source, send_row, axis=0).reshape(shards, rows, width)
        packed = jnp.where(send_live[:, :, None], packed, jnp.zeros_like(packed))
        got = lax.all_to_all(packed, "shard", split_axis=0, concat_axis=0, tiled=True)
        own = got.reshape(shards, blocks, ROWS, width).transpose(1, 0, 2, 3).reshape(blocks, -1, width)
        return own, seq_gather(own, 1).reshape(cap, width)

    x_own, x_low = to_groups(tokens[0])
    cot_own, cot_low = to_groups(cotangent[0])

    def own_part(whole):
        return take(whole.reshape(blocks, seqs, -1, whole.shape[-1]), me, 1)

    place = jnp.arange(cap, dtype=jnp.int32)
    block_of, in_block = place // (ROWS * lanes), place % (ROWS * lanes)
    row_of = block_of * ROWS + in_block % ROWS
    ids = row_of * lanes + in_block // ROWS
    own_before, own_count = take(slot_before, group), take(slot_rows, group)
    holds = (row_of[:, None] >= own_before[None]) & (row_of[:, None] < (own_before + own_count)[None])
    begin_row = jnp.sum(jnp.where(holds, own_before[None], 0), axis=1)
    begins = jnp.where(jnp.any(holds, axis=1), begin_row * lanes, ids)
    ids, begins = ids.astype(f32), begins.astype(f32)
    head_ids = me * heads + jnp.arange(heads, dtype=jnp.int32)
    slopes = 2.0 ** (-8.0 * (head_ids.astype(f32) + 1.0) / HEADS)
    one_seq = per_group == 1

    hidden = x_low.astype(f32)
    xhat_one, _ = normalize(hidden)
    normed_one = (xhat_one * gain_one + bias_one).astype(bf16)
    qkv = (jnp.dot(normed_one, full_qkv, preferred_element_type=f32) + bias_all).astype(bf16)
    mixed = attention_forward(qkv, slopes, ids, begins, lanes, one_seq)
    mixed_all = seq_gather(mixed, 1).reshape(cap, width)
    branch = jnp.dot(mixed_all, full_dense, preferred_element_type=f32) + bias_dense
    resid = hidden + branch
    xhat_two, _ = normalize(resid)
    normed_two = (xhat_two * gain_two + bias_two).astype(bf16)
    upper = jnp.dot(normed_two, full_up, preferred_element_type=f32) + bias_up
    activ = gelu_tanh(upper).astype(bf16)
    down = jnp.dot(activ, full_down, preferred_element_type=f32)
    resid_own = own_part(resid)
    down_own = seq_sum(down.reshape(blocks, seqs, -1, width), 1)
    block_out = (resid_own + down_own + bias_down).astype(bf16)

    grad_down = jnp.dot(activ.T, cot_low, preferred_element_type=f32).astype(bf16)
    grad_activ = jnp.dot(cot_low, full_down.T, preferred_element_type=f32)
    grad_upper = jax.vjp(gelu_tanh, upper)[1](grad_activ)[0].astype(bf16)
    grad_up = jnp.dot(normed_two.T, grad_upper, preferred_element_type=f32).astype(bf16)
    grad_bup = jnp.sum(grad_upper.astype(f32), axis=0)
    grad_normed = jnp.dot(grad_upper, full_up.T, preferred_element_type=f32)
    grad_normed = seq_sum(grad_normed.reshape(blocks, seqs, -1, width), 1).reshape(slots, width)
    cot_full = cot_own.reshape(slots, width).astype(f32)
    grad_bdown = jnp.sum(cot_full, axis=0)
    xhat_two, root_two = normalize(resid_own.reshape(slots, width))
    grad_gain_two = jnp.sum(grad_normed * xhat_two, axis=0)
    grad_bias_two = jnp.sum(grad_normed, axis=0)
    grad_resid = cot_full + norm_pull(grad_normed, gain_two, xhat_two, root_two)

    grad_branch = grad_resid.astype(bf16)
    grad_dense = jnp.dot(own_part(mixed_all).reshape(slots, width).T, grad_branch, preferred_element_type=f32).astype(bf16)
    grad_bdense = jnp.sum(grad_branch.astype(f32), axis=0)
    grad_mixed = jnp.dot(grad_branch, full_dense.T, preferred_element_type=f32).astype(bf16)
    got = seq_blocks(grad_mixed.reshape(blocks, -1, seqs, part), 2, bf16)
    if seqs == 2:
        grad_mixed = jnp.where(me == 0, jnp.stack(got, 1), jnp.stack(got[::-1], 1))
    else:
        grad_mixed = jnp.zeros((blocks, seqs) + got[0].shape[1:], bf16)
        for d, g in enumerate(got):
            grad_mixed = lax.dynamic_update_index_in_dim(grad_mixed, g, (me - d) % seqs, 1)
    grad_mixed = grad_mixed.reshape(cap, part)
    grad_proj = jnp.concatenate(
        attention_backward(qkv, grad_mixed, slopes, ids, begins, lanes, one_seq), axis=1
    )
    grad_qkv = jnp.dot(normed_one.T, grad_proj, preferred_element_type=f32).astype(bf16)
    proj_sums = jnp.sum(grad_proj.astype(f32), axis=0)
    grad_one = jnp.dot(grad_proj, full_qkv.T, preferred_element_type=f32)
    grad_one = seq_sum(grad_one.reshape(blocks, seqs, -1, width), 1).reshape(slots, width)
    xhat_one, root_one = normalize(x_own.reshape(slots, width).astype(f32))
    grad_gain_one = jnp.sum(grad_one * xhat_one, axis=0)
    grad_bias_one = jnp.sum(grad_one, axis=0)
    tokens_grad = (grad_resid + norm_pull(grad_one, gain_one, xhat_one, root_one)).astype(bf16)

    row_here = jnp.arange(slots, dtype=jnp.int32)[:, None]
    seq_in = ((row_here >= row_start[None]) & (row_here < (row_start + seq_rows)[None])).astype(jnp.int32)
    home = jnp.arange(lengths.shape[0], dtype=jnp.int32) // per_group
    fetch = jnp.sum(seq_in * (home[None] * rows + slot_before.reshape(-1)[None] + row_here - row_start[None]), axis=1)
    fetch_live = jnp.sum(seq_in, axis=1) > 0

    def to_stream(own):
        sent = own.reshape(blocks, shards, ROWS, width).transpose(1, 0, 2, 3).reshape(shards, rows, width)
        got = lax.all_to_all(sent, "shard", split_axis=0, concat_axis=0, tiled=True)
        taken = jnp.take(got.reshape(-1, width), fetch, axis=0)
        return jnp.where(fetch_live[:, None], taken, jnp.zeros_like(taken))[None]

    down_block = shard_reduce(grad_down.reshape(shards, ff_part, width), bf16)
    up_block = shard_reduce(grad_up.reshape(shards, -1, shards * ff_part), bf16)
    dense_block = shard_reduce(grad_dense.reshape(shards, -1, width), bf16)
    qkv_block = shard_reduce(grad_qkv.reshape(shards, -1, 3 * part), bf16)

    def spread(vector, index_shape):
        zero = jnp.zeros(index_shape, f32)
        return lax.dynamic_update_index_in_dim(zero, vector, me, 1)

    sums = proj_sums.reshape(3, part)
    qv = spread(jnp.stack([sums[0], sums[2]]), (2, seqs, part)).reshape(shards, -1)
    bup = spread(grad_bup.reshape(shards, ff_part), (shards, seqs, ff_part)).reshape(shards, -1)
    rest = (grad_gain_one, grad_bias_one, grad_bdense, grad_gain_two, grad_bias_two, grad_bdown)
    packed = jnp.concatenate([a.reshape(shards, -1) for a in rest] + [qv, bup], axis=1)
    packed = shard_reduce(packed, f32)
    packed = jnp.sum(seq_gather(packed, 0), axis=0)
    cuts, at = [], 0
    for a in [a.reshape(shards, -1) for a in rest] + [qv, bup]:
        cuts.append(packed[at : at + a.shape[1]])
        at += a.shape[1]
    g_gain_one, g_bias_one, g_bdense, g_gain_two, g_bias_two, g_bdown, g_qv, g_bup = cuts

    g_dense = jnp.sum(seq_gather(dense_block.astype(bf16), 0).astype(f32), axis=0)
    g_qkv = seq_gather(qkv_block.astype(bf16).reshape(-1, 3, part), 2).reshape(-1, 3 * width).astype(f32)
    g_up = seq_gather(up_block.astype(bf16).reshape(-1, shards, ff_part), 2).reshape(-1, hidden_units).astype(f32)
    g_down = seq_gather(down_block.astype(bf16), 0).reshape(-1, width).astype(f32)
    return (
        to_stream(block_out), to_stream(tokens_grad.reshape(blocks, -1, width)),
        g_gain_one, g_bias_one, g_qkv, g_qv, g_dense, g_bdense, g_gain_two, g_bias_two, g_up, g_bup, g_down, g_bdown,
    )


def solution(mesh):
    rows, vector, stream = P("shard", None), P("shard"), P(("seq", "shard"), None, None)
    params = (vector, vector, rows, vector, rows, vector, vector, vector, rows, vector, rows, vector)
    return jax.shard_map(
        per_device, mesh=mesh, in_specs=(stream, stream, P()) + params, out_specs=(stream, stream) + params, check_vma=False
    )
```

time: 1120 us -> 574 us (0.51)
  matrix products: 265 us -> 69.5 us
  blocking collectives: 186 us -> 0 us
  local copies, waits for them, and re-layouts: 223 us -> 93.8 us
  waiting for transfers between devices: 306 us -> 197 us
  Pallas kernels: 0 us -> 46.1 us
  starting transfers between devices: 49.2 us -> 73.5 us
  other arithmetic: 53 us -> 70.9 us
    dot_general x26 -> x12, matrix products: 265 us -> 69.5 us  [the longest x1 14.5 us: per_device(): grad_activ = jnp.dot(cot_low, full_down.T, preferred_element_type=f32)]
    reduce_scatter x4 -> x0, waiting for transfers between devices: 153 us -> none  [the longest x1 108 us: per_device(): lax.psum_scatter(grads[10].astype(jnp.bfloat16), 'shard', scatter_dimensi...]
    unnamed x2 -> x0, blocking collectives: 141 us -> none
    ppermute x0 -> x37, waiting for transfers between devices: none -> 127 us  [the longest x25 68.9 us: shard_reduce(): total = total + lax.ppermute(sent, 'shard', pairs).astype(f32)]
    all_to_all x8 -> x4, waiting for transfers between devices: 116 us -> 49.3 us  [the longest x2 49.3 us: to_groups(): lax.all_to_all(packed, 'shard', split_axis=0, concat_axis=0, tiled=True)]
    reshape x11 -> x9, local copies, waits for them, and re-layouts: 61.1 us -> 5.7 us  [the longest x1 1.29 us: per_device(): qkv_weight.reshape(-1, 3, seqs, part)]
    all_to_all x11 -> x0, local copies, waits for them, and re-layouts: 53.1 us -> none  [the longest x2 24.5 us: per_device(): lax.all_to_all(projected, 'seq', split_axis=3, concat_axis=1, tiled=True)]
    unnamed x172 -> x115, local copies, waits for them, and re-layouts: 69.6 us -> 16.8 us
  transfers between devices with their start and end apart: 17 -> 45, of which waited for: 7 -> 19; matrix products, arithmetic and copies ran while one was open for 44% -> 29% of each run, Pallas kernels for 0% -> 8%
where the time goes in v1:
time: 574 us; the launch traced here: 567 us
  waiting for transfers between devices  197 us (34%)
  local copies, waits for them, and re-layouts  93.8 us (16%)
  starting transfers between devices  73.5 us (13%)
  other arithmetic  70.9 us (12%)
  matrix products  69.5 us (12%)
  Pallas kernels  46.1 us (8%)
  between operations  15.8 us (3%)
    ppermute x25, waiting for transfers between devices, shard_reduce(): total = total + lax.ppermute(sent, 'shard', pairs).astype(f32)  68.9 us
    all_to_all x2, waiting for transfers between devices, to_groups(): lax.all_to_all(packed, 'shard', split_axis=0, concat_axis=0, tiled=True)  49.3 us
    ppermute x4, waiting for transfers between devices, seq_blocks(): got.append(lax.ppermute(sent, 'seq', [(i, (i + d) % n) for i in range(n)]))  43.5 us
    pallas_call x1, Pallas kernels, attention_backward(): pl.pallas_call(functools.partial(attn_bwd_kernel, lanes, tile, one_seq),...  30.6 us
    ppermute x25, starting transfers between devices, shard_reduce(): total = total + lax.ppermute(sent, 'shard', pairs).astype(f32)  28.7 us
    all_to_all x2, starting transfers between devices, to_groups(): lax.all_to_all(packed, 'shard', split_axis=0, concat_axis=0, tiled=True)  23 us
    all_gather x4, waiting for transfers between devices, per_device(): gather = lambda a: lax.all_gather(a, 'shard', axis=0, tiled=False)  20.3 us
    unnamed x115, local copies, waits for them, and re-layouts  16.8 us
  transfers between devices with their start and end apart: 45, of which 19 were waited for; matrix products, arithmetic and copies ran while one was open for 29% of the time, Pallas kernels for 8%

profile of v1, /device:TPU:0, one launch (start us, length us, event | category | flops | bytes accessed | tf_op | source)
XLA Modules:
  0.0 566.8 jit_solution(17805745644133789024)
XLA Ops:
  7.3 5.5 concatenate.32
  26.6 7.5 %all-to-all-start = ((bf16[16,32,1024]{2,1,0:T(8,128)(2,1)}), bf16[16,32,1024]{2,1,0:T(8,128)(2,1)S(1)}, u32[]{:S(2)}, u32[]{:S(2)}) async-start(bf16[16,32,1024]{2,1,0:T(8,128)(2,1)} %get-tuple-element.88), calls=%async_computation | async-start | bytes 2097152 | tf_op jit(solution)/shard_map/all_to_all | solution.py:324
  35.0 31.3 %all-to-all-done = bf16[16,32,1024]{2,1,0:T(8,128)(2,1)S(1)} async-done(((bf16[16,32,1024]{2,1,0:T(8,128)(2,1)}), bf16[16,32,1024]{2,1,0:T(8,128)(2,1)S(1)}, u32[]{:S(2)}, u32[]{:S(2)}) %all-to-all-start) | async-done | bytes 1048608 | tf_op jit(solution)/shard_map/all_to_all | solution.py:324
  66.3 15.4 %all-to-all-start.2 = ((bf16[16,32,1024]{2,1,0:T(8,128)(2,1)}), bf16[16,32,1024]{2,1,0:T(8,128)(2,1)}, u32[]{:S(2)}, u32[]{:S(2)}) async-start(bf16[16,32,1024]{2,1,0:T(8,128)(2,1)} %get-tuple-element.87), calls=%async_computation.2 | async-start | bytes 2097152 | tf_op jit(solution)/shard_map/all_to_all | solution.py:324
  90.7 17.9 %all-to-all-done.2 = bf16[16,32,1024]{2,1,0:T(8,128)(2,1)} async-done(((bf16[16,32,1024]{2,1,0:T(8,128)(2,1)}), bf16[16,32,1024]{2,1,0:T(8,128)(2,1)}, u32[]{:S(2)}, u32[]{:S(2)}) %all-to-all-start.2) | async-done | bytes 1048608 | tf_op jit(solution)/shard_map/all_to_all | solution.py:324
  134.8 15.5 %attention_forward.1 = bf16[1024,512]{1,0:T(8,128)(2,1)} custom-call(f32[4,1,2]{2,1,0:T(1,128)S(1)} %multiply_power_fusion.slope_ref, f32[1024,1]{1,0:T(8,128)S(1)} %copy-done.3, f32[1,1024]{1,0:T(1,128)S(1)} %fusion.84.idr_ref, f32[1024,1]{1,0:T(8,128)S(1)} %copy-done.4, bf16[1024,1536]{1,0:T(8,128)(2,1)S(1)} %add_convert_fusion.q_ref.k_ref.v_ref, ...), custom_call_target="tpu_custom_call" | custom-call | flops 2684354560 | bytes 4194304 | tf_op jit(solution)/shard_map/attention_forward/pallas_call | solution.py:161
  165.6 9.7 %collective-permute-done.1 = bf16[1024,512]{1,0:T(8,128)(2,1)S(1)} collective-permute-done((bf16[1024,512]{1,0:T(8,128)(2,1)}, bf16[1024,512]{1,0:T(8,128)(2,1)S(1)}, u32[]{:S(2)}, u32[]{:S(2)}) %collective-permute-start.1) | collective-permute-done | bytes 1048608 | tf_op jit(solution)/shard_map/ppermute | solution.py:214
  183.2 5.1 select_n.632
  188.4 5.7 %fusion.94 = (f32[1024]{0:T(1024)S(1)}, f32[1024,1024]{1,0:T(8,128)S(1)}) fusion(f32[1024]{0:T(1024)S(1)} %add.765, bf16[1024,1024]{0,1:T(8,128)(2,1)S(1)} %bitcast.342, bf16[1024,1024]{1,0:T(8,128)(2,1)} %all-gather.13.cloned.1.call-done, f32[4,2,128,1024]{3,2,1,0:T(8,128)} %copy.190), kind=kOutput, calls=%fused_computation.284 | convolution fusion | flops 2150628352 | bytes 12591104 | tf_op jit(solution)/shard_map/dot_general | solution.py:353
  201.3 11.5 %fusion.86 = f32[1024,2048]{1,0:T(8,128)} fusion(bf16[1024,2048]{1,0:T(8,128)(2,1)} %bitcast.371, f32[1024,1024]{1,0:T(8,128)} %copy-done.8, f32[1024]{0:T(1024)S(1)} %add.770, f32[1024]{0:T(1024)S(1)} %mul.373, f32[1024]{0:T(1024)S(1)} %add_rsqrt_fusion.1, f32[1024]{0:T(1024)S(1)} %broadcast_multiply_fusion.1), kind=kOutput, calls=%fused_computation.278 | convolution fusion | flops 4300210176 | bytes 16793600 | tf_op jit(solution)/shard_map/dot_general | solution.py:357
  212.9 20.2 %all-gather.9.cloned.1.call-done = bf16[16,128,1024]{2,1,0:T(8,128)(2,1)} async-done(((bf16[1,128,1024]{2,1,0:T(8,128)(2,1)}), bf16[16,128,1024]{2,1,0:T(8,128)(2,1)}) %all-gather.9.cloned.1.call-update) | async-done | bytes 4194320 | tf_op jit(solution)/shard_map/all_gather | solution.py:298
  233.1 14.5 %convert_reduce_fusion = (f32[2048]{0:T(1024)S(1)}, bf16[1024,2048]{1,0:T(8,128)(2,1)S(1)}, bf16[1024,2048]{1,0:T(8,128)(2,1)S(1)}) fusion(f32[1024,2048]{1,0:T(8,128)} %fusion.86, f32[2048]{0:T(1024)S(1)} %bitcast.368, bf16[1024,1024]{1,0:T(8,128)(2,1)S(1)} %bitcast.339, bf16[2048,1024]{1,0:T(8,128)(2,1)} %bitcast.373), kind=kOutput, calls=%fused_computation.14 | convolution fusion | flops 4355782656 | bytes 23085056 | tf_op jit(solution)/shard_map/dot_general | solution.py:365
  247.5 5.1 convolution_convert_fusion.1
  267.6 5.8 %convolution_convert_fusion.2 = bf16[1024,2048]{1,0:T(8,128)(2,1)S(1)} fusion(bf16[1024,2048]{1,0:T(8,128)(2,1)S(1)} %get-tuple-element.36, f32[1024,1024]{1,0:T(8,128)S(1)} %copy-done.9, f32[1024]{0:T(1024)S(1)} %add.770, f32[1024]{0:T(1024)S(1)} %mul.373, f32[1024]{0:T(1024)S(1)} %add_rsqrt_fusion.1, f32[1024]{0:T(1024)S(1)} %broadcast_multiply_fusion.1), kind=kOutput, calls=%fused_computation.34 | convolution fusion | flops 4302307328 | bytes 12599296 | tf_op jit(solution)/shard_map/dot_general | solution.py:367
  276.0 12.6 %collective-permute-done.4 = bf16[4,128,1024]{2,1,0:T(8,128)(2,1)S(1)} collective-permute-done((bf16[4,128,1024]{2,1,0:T(8,128)(2,1)S(1)}, bf16[4,128,1024]{2,1,0:T(8,128)(2,1)S(1)}, u32[]{:S(2)}, u32[]{:S(2)}) %collective-permute-start.4) | collective-permute-done | bytes 1048608 | tf_op jit(solution)/shard_map/ppermute | solution.py:228
  288.6 21.8 %collective-permute-done.2 = bf16[4,128,1024]{2,1,0:T(8,128)(2,1)S(1)} collective-permute-done((bf16[4,128,1024]{2,1,0:T(8,128)(2,1)S(1)}, bf16[4,128,1024]{2,1,0:T(8,128)(2,1)S(1)}, u32[]{:S(2)}, u32[]{:S(2)}) %collective-permute-start.2) | collective-permute-done | bytes 1048608 | tf_op jit(solution)/shard_map/ppermute | solution.py:228
  339.5 30.6 %attention_backward.1 = (bf16[1024,512]{1,0:T(8,128)(2,1)}, bf16[1024,512]{1,0:T(8,128)(2,1)}, bf16[1024,512]{1,0:T(8,128)(2,1)}) custom-call(f32[4,1,2]{2,1,0:T(1,128)} %copy-done.6, f32[1024,1]{1,0:T(8,128)} %get-tuple-element.100.idc_ref, f32[1,1024]{1,0:T(1,128)} %copy-done.5, f32[1,1024]{1,0:T(1,128)} %fusion.79.beginr_ref, ...), custom_call_target="tpu_custom_call" | custom-call | flops 6710886400 | bytes 7340032 | tf_op jit(solution)/shard_map/attention_backward/pallas_call | solution.py:186
  374.3 6.4 %fusion.97 = f32[4,2,128,1024]{3,2,1,0:T(8,128)S(1)} fusion(bf16[4,2,128,1536]{3,2,1,0:T(8,128)(2,1)} %bitcast.324, bf16[1024,1536,1,1]{1,0,3,2:T(8,128)(2,1)} %bitcast.333), kind=kOutput, calls=%fused_computation.287 | convolution fusion | flops 3221225472 | bytes 10485760 | tf_op jit(solution)/shard_map/dot_general | solution.py:395
  398.5 6.1 %collective-permute-done.6 = bf16[4,128,1024]{2,1,0:T(8,128)(2,1)S(1)} collective-permute-done((bf16[4,128,1024]{2,1,0:T(8,128)(2,1)S(1)}, bf16[4,128,1024]{2,1,0:T(8,128)(2,1)S(1)}, u32[]{:S(2)}, u32[]{:S(2)}) %collective-permute-start.6) | collective-permute-done | bytes 1048608 | tf_op jit(solution)/shard_map/ppermute | solution.py:228
  416.5 12.4 %collective-permute-done.8 = f32[4,768]{1,0:T(4,128)S(1)} collective-permute-done((f32[4,768]{1,0:T(4,128)S(1)}, f32[4,768]{1,0:T(4,128)S(1)}, u32[]{:S(2)}, u32[]{:S(2)}) %collective-permute-start.8) | collective-permute-done | bytes 12320 | tf_op jit(solution)/shard_map/ppermute | solution.py:258
  460.7 11.0 %collective-permute-done.26 = bf16[4,64,2048]{2,1,0:T(8,128)(2,1)S(1)} collective-permute-done((bf16[4,64,2048]{2,1,0:T(8,128)(2,1)S(1)}, bf16[4,64,2048]{2,1,0:T(8,128)(2,1)S(1)}, u32[]{:S(2)}, u32[]{:S(2)}) %collective-permute-start.26) | collective-permute-done | bytes 1048608 | tf_op jit(solution)/shard_map/ppermute | solution.py:258
  489.0 11.5 %collective-permute-done.34 = bf16[128,1024]{1,0:T(8,128)(2,1)} collective-permute-done((bf16[128,1024]{1,0:T(8,128)(2,1)S(1)}, bf16[128,1024]{1,0:T(8,128)(2,1)}, u32[]{:S(2)}, u32[]{:S(2)}) %collective-permute-start.34) | collective-permute-done | bytes 262176 | tf_op jit(solution)/shard_map/ppermute | solution.py:258
  502.0 15.3 %collective-permute-done.28 = bf16[64,2048]{1,0:T(8,128)(2,1)} collective-permute-done((bf16[64,2048]{1,0:T(8,128)(2,1)}, bf16[64,2048]{1,0:T(8,128)(2,1)}, u32[]{:S(2)}, u32[]{:S(2)}) %collective-permute-start.28) | collective-permute-done | bytes 262176 | tf_op jit(solution)/shard_map/ppermute | solution.py:258
  531.6 9.5 %collective-permute-done.16 = bf16[64,1536]{1,0:T(8,128)(2,1)} collective-permute-done((bf16[64,1536]{1,0:T(8,128)(2,1)}, bf16[64,1536]{1,0:T(8,128)(2,1)}, u32[]{:S(2)}, u32[]{:S(2)}) %collective-permute-start.16) | collective-permute-done | bytes 196640 | tf_op jit(solution)/shard_map/ppermute | solution.py:258
  (395 shorter events, 243.0 us)
Async XLA Ops:
  7.2 111.1 %all-gather.11.cloned.1.call-start = ((), (), s32[]{:S(2)}) async-start(), calls=%async_computation.6 | async-start | bytes 4177920 | tf_op jit(solution)/shard_map/all_gather | solution.py:298
  16.3 172.0 %all-gather.13.cloned.1.call-start = ((), (), s32[]{:S(2)}) async-start(), calls=%async_computation.7 | async-start | bytes 2228224 | tf_op jit(solution)/shard_map/all_gather | solution.py:298
  17.1 184.3 %all-gather.7.cloned.1.call-start = ((), (), s32[]{:S(2)}) async-start(), calls=%async_computation.4 | async-start | bytes 4456448 | tf_op jit(solution)/shard_map/all_gather | solution.py:298
  26.6 39.7 %all-to-all-start = ((bf16[16,32,1024]{2,1,0:T(8,128)(2,1)}), bf16[16,32,1024]{2,1,0:T(8,128)(2,1)S(1)}, u32[]{:S(2)}, u32[]{:S(2)}) async-start(bf16[16,32,1024]{2,1,0:T(8,128)(2,1)} %get-tuple-element.88), calls=%async_computation | async-start | bytes 2097152 | tf_op jit(solution)/shard_map/all_to_all | solution.py:324
  34.1 198.9 %all-gather.9.cloned.1.call-start = ((), (), s32[]{:S(2)}) async-start(), calls=%async_computation.5 | async-start | bytes 4456448 | tf_op jit(solution)/shard_map/all_gather | solution.py:298
  66.3 42.3 %all-to-all-start.2 = ((bf16[16,32,1024]{2,1,0:T(8,128)(2,1)}), bf16[16,32,1024]{2,1,0:T(8,128)(2,1)}, u32[]{:S(2)}, u32[]{:S(2)}) async-start(bf16[16,32,1024]{2,1,0:T(8,128)(2,1)} %get-tuple-element.87), calls=%async_computation.2 | async-start | bytes 2097152 | tf_op jit(solution)/shard_map/all_to_all | solution.py:324
  87.6 25.9 %collective-permute-start = (bf16[4,128,1024]{2,1,0:T(8,128)(2,1)}, bf16[4,128,1024]{2,1,0:T(8,128)(2,1)}, u32[]{:S(2)}, u32[]{:S(2)}) collective-permute-start(bf16[4,128,1024]{2,1,0:T(8,128)(2,1)} %get-tuple-element.67), channel_id=1, source_target_pairs={{0,16},{16,0},{1,17},{17,1},{2,18},{18,2},{3,19},{19,3},{4,20},{20... | collective-permute-start | bytes 3145736 | tf_op jit(solution)/shard_map/ppermute | solution.py:214
  111.1 45.3 %collective-permute-start.3 = (bf16[4,128,1024]{2,1,0:T(8,128)(2,1)}, bf16[4,128,1024]{2,1,0:T(8,128)(2,1)}, u32[]{:S(2)}, u32[]{:S(2)}) collective-permute-start(bf16[4,128,1024]{2,1,0:T(8,128)(2,1)} %get-tuple-element.66), channel_id=1, source_target_pairs={{0,16},{16,0},{1,17},{17,1},{2,18},{18,2},{3,19},{19,3},{4,20},{20... | collective-permute-start | bytes 3145736 | tf_op jit(solution)/shard_map/ppermute | solution.py:214
  262.5 26.1 %collective-permute-start.4 = (bf16[4,128,1024]{2,1,0:T(8,128)(2,1)S(1)}, bf16[4,128,1024]{2,1,0:T(8,128)(2,1)S(1)}, u32[]{:S(2)}, u32[]{:S(2)}) collective-permute-start(bf16[4,128,1024]{2,1,0:T(8,128)(2,1)S(1)} %fusion.38), channel_id=1, source_target_pairs={{0,16},{16,0},{1,17},{17,1},{2,18},{18,2},{3,19},{19,3},{4,20},{20... | collective-permute-start | bytes 3145736 | tf_op jit(solution)/shard_map/ppermute | solution.py:228
  264.1 46.3 %collective-permute-start.2 = (bf16[4,128,1024]{2,1,0:T(8,128)(2,1)S(1)}, bf16[4,128,1024]{2,1,0:T(8,128)(2,1)S(1)}, u32[]{:S(2)}, u32[]{:S(2)}) collective-permute-start(bf16[4,128,1024]{2,1,0:T(8,128)(2,1)S(1)} %fusion.36), channel_id=1, source_target_pairs={{0,16},{16,0},{1,17},{17,1},{2,18},{18,2},{3,19},{19,3},{4,20},{20... | collective-permute-start | bytes 3145736 | tf_op jit(solution)/shard_map/ppermute | solution.py:228
  325.1 68.2 %collective-permute-start.31 = (bf16[4,2,128,1024]{3,2,1,0:T(8,128)(2,1)}, bf16[4,2,128,1024]{3,2,1,0:T(8,128)(2,1)}, u32[]{:S(2)}, u32[]{:S(2)}) collective-permute-start(bf16[4,2,128,1024]{3,2,1,0:T(8,128)(2,1)} %dynamic-slice_bitcast_fusion), channel_id=1, source_target_pairs={{0,1},{1,0},{2,3},{3,2},{4,5},{5,4},{6,7},{7,6},{8,9},{9,8},{10,11... | collective-permute-start | bytes 6291464 | tf_op jit(solution)/shard_map/ppermute | solution.py:258
  325.2 87.3 %collective-permute-start.25 = (bf16[4,2,64,2048]{3,2,1,0:T(8,128)(2,1)}, bf16[4,2,64,2048]{3,2,1,0:T(8,128)(2,1)}, u32[]{:S(2)}, u32[]{:S(2)}) collective-permute-start(bf16[4,2,64,2048]{3,2,1,0:T(8,128)(2,1)} %dynamic-slice_bitcast_fusion.1), channel_id=1, source_target_pairs={{0,1},{1,0},{2,3},{3,2},{4,5},{5,4},{6,7},{7,6},{8,9},{9,8},{10,11... | collective-permute-start | bytes 6291464 | tf_op jit(solution)/shard_map/ppermute | solution.py:258
  326.9 156.1 %all-to-all-start.1 = ((bf16[16,32,1024]{2,1,0:T(8,128)(2,1)}), bf16[16,32,1024]{2,1,0:T(8,128)(2,1)S(1)}, u32[]{:S(2)}, u32[]{:S(2)}) async-start(bf16[16,32,1024]{2,1,0:T(8,128)(2,1)} %bitcast.308), calls=%async_computation.1 | async-start | bytes 2097152 | tf_op jit(solution)/shard_map/all_to_all | solution.py:410
  333.6 55.5 %collective-permute-start.19 = (bf16[4,2,64,1024]{3,2,1,0:T(8,128)(2,1)S(1)}, bf16[4,2,64,1024]{3,2,1,0:T(8,128)(2,1)}, u32[]{:S(2)}, u32[]{:S(2)}) collective-permute-start(bf16[4,2,64,1024]{3,2,1,0:T(8,128)(2,1)S(1)} %dynamic-slice_bitcast_fusion.5), channel_id=1, source_target_pairs={{0,1},{1,0},{2,3},{3,2},{4,5},{5,4},{6,7},{7,6},{8,9},{9,8},{10,11... | collective-permute-start | bytes 3145736 | tf_op jit(solution)/shard_map/ppermute | solution.py:258
  389.1 62.4 %collective-permute-start.13 = (bf16[4,2,64,1536]{3,2,0,1:T(8,128)(2,1)}, bf16[4,2,64,1536]{3,2,0,1:T(8,128)(2,1)}, u32[]{:S(2)}, u32[]{:S(2)}) collective-permute-start(bf16[4,2,64,1536]{3,2,0,1:T(8,128)(2,1)} %bitcast.307), channel_id=1, source_target_pairs={{0,1},{1,0},{2,3},{3,2},{4,5},{5,4},{6,7},{7,6},{8,9},{9,8},{10,11... | collective-permute-start | bytes 4718600 | tf_op jit(solution)/shard_map/ppermute | solution.py:258
  392.8 40.0 %collective-permute-start.20 = (bf16[4,64,1024]{2,1,0:T(8,128)(2,1)}, bf16[4,64,1024]{2,1,0:T(8,128)(2,1)}, u32[]{:S(2)}, u32[]{:S(2)}) collective-permute-start(bf16[4,64,1024]{2,1,0:T(8,128)(2,1)} %dynamic-slice_bitcast_fusion.7), channel_id=1, source_target_pairs={{0,2},{1,3},{2,0},{3,1},{4,6},{5,7},{6,4},{7,5},{8,10},{9,11},{10,... | collective-permute-start | bytes 1572872 | tf_op jit(solution)/shard_map/ppermute | solution.py:258
  397.0 58.1 %collective-permute-start.32 = (bf16[4,128,1024]{2,1,0:T(8,128)(2,1)}, bf16[4,128,1024]{2,1,0:T(8,128)(2,1)}, u32[]{:S(2)}, u32[]{:S(2)}) collective-permute-start(bf16[4,128,1024]{2,1,0:T(8,128)(2,1)} %dynamic-slice_bitcast_fusion.3), channel_id=1, source_target_pairs={{0,2},{1,3},{2,0},{3,1},{4,6},{5,7},{6,4},{7,5},{8,10},{9,11},{10,... | collective-permute-start | bytes 3145736 | tf_op jit(solution)/shard_map/ppermute | solution.py:258
  445.7 26.1 %collective-permute-start.26 = (bf16[4,64,2048]{2,1,0:T(8,128)(2,1)S(1)}, bf16[4,64,2048]{2,1,0:T(8,128)(2,1)S(1)}, u32[]{:S(2)}, u32[]{:S(2)}) collective-permute-start(bf16[4,64,2048]{2,1,0:T(8,128)(2,1)S(1)} %dynamic-slice_bitcast_fusion.4), channel_id=1, source_target_pairs={{0,2},{1,3},{2,0},{3,1},{4,6},{5,7},{6,4},{7,5},{8,10},{9,11},{10,... | collective-permute-start | bytes 3145736 | tf_op jit(solution)/shard_map/ppermute | solution.py:258
  450.8 26.9 %collective-permute-start.24 = (bf16[64,1024]{1,0:T(8,128)(2,1)S(1)}, bf16[64,1024]{1,0:T(8,128)(2,1)S(1)}, u32[]{:S(2)}, u32[]{:S(2)}) collective-permute-start(bf16[64,1024]{1,0:T(8,128)(2,1)S(1)} %fusion.73), channel_id=1, source_target_pairs={{0,16},{16,0},{1,17},{17,1},{2,18},{18,2},{3,19},{19,3},{4,20},{20... | collective-permute-start | bytes 393224 | tf_op jit(solution)/shard_map/ppermute | solution.py:214
  454.6 64.9 %collective-permute-start.14 = (bf16[4,64,1536]{2,1,0:T(8,128)(2,1)}, bf16[4,64,1536]{2,1,0:T(8,128)(2,1)}, u32[]{:S(2)}, u32[]{:S(2)}) collective-permute-start(bf16[4,64,1536]{2,1,0:T(8,128)(2,1)} %dynamic-slice_bitcast_fusion.6), channel_id=1, source_target_pairs={{0,2},{1,3},{2,0},{3,1},{4,6},{5,7},{6,4},{7,5},{8,10},{9,11},{10,... | collective-permute-start | bytes 2359304 | tf_op jit(solution)/shard_map/ppermute | solution.py:258
  471.8 28.8 %collective-permute-start.34 = (bf16[128,1024]{1,0:T(8,128)(2,1)S(1)}, bf16[128,1024]{1,0:T(8,128)(2,1)}, u32[]{:S(2)}, u32[]{:S(2)}) collective-permute-start(bf16[128,1024]{1,0:T(8,128)(2,1)S(1)} %get-tuple-element.57), channel_id=1, source_target_pairs={{0,8},{1,9},{2,10},{3,11},{4,12},{5,13},{6,14},{7,15},{8,0},{9,1},... | collective-permute-start | bytes 786440 | tf_op jit(solution)/shard_map/ppermute | solution.py:258
  481.5 35.8 %collective-permute-start.28 = (bf16[64,2048]{1,0:T(8,128)(2,1)}, bf16[64,2048]{1,0:T(8,128)(2,1)}, u32[]{:S(2)}, u32[]{:S(2)}) collective-permute-start(bf16[64,2048]{1,0:T(8,128)(2,1)} %get-tuple-element.60), channel_id=1, source_target_pairs={{0,8},{1,9},{2,10},{3,11},{4,12},{5,13},{6,14},{7,15},{8,0},{9,1},... | collective-permute-start | bytes 786440 | tf_op jit(solution)/shard_map/ppermute | solution.py:258
  483.0 71.1 %all-to-all-start.3 = ((bf16[16,32,1024]{2,1,0:T(8,128)(2,1)}), bf16[16,32,1024]{2,1,0:T(8,128)(2,1)S(1)}, u32[]{:S(2)}, u32[]{:S(2)}) async-start(bf16[16,32,1024]{2,1,0:T(8,128)(2,1)} %get-tuple-element.62), calls=%async_computation.3 | async-start | bytes 2097152 | tf_op jit(solution)/shard_map/all_to_all | solution.py:410
  501.9 28.6 %collective-permute-start.36 = (bf16[128,1024]{1,0:T(8,128)(2,1)S(1)}, bf16[128,1024]{1,0:T(8,128)(2,1)}, u32[]{:S(2)}, u32[]{:S(2)}) collective-permute-start(bf16[128,1024]{1,0:T(8,128)(2,1)S(1)} %fusion.60), channel_id=1, source_target_pairs={{0,16},{16,0},{1,17},{17,1},{2,18},{18,2},{3,19},{19,3},{4,20},{20... | collective-permute-start | bytes 786440 | tf_op jit(solution)/shard_map/ppermute | solution.py:214
  (74 other events, 795.4 us)
Sparse Core Ops, SparseCore 0:
  16.4 63.8 all-gather.10
  82.5 46.5 all-gather.12
  131.8 49.4 all-gather.6
  184.0 49.0 all-gather.8

commit v2 on v1

--- a/solution.py
+++ b/solution.py
@@ -176,11 +176,12 @@
 
 
 def attention_backward(qkv, grad_out, slopes, ids, begins, lanes, one_seq):
-    tokens, width = qkv.shape[0], qkv.shape[1] // 3
+    tokens, width = grad_out.shape
     pairs, tile = attn_shape(tokens, width, lanes)
     column = lambda part: pl.BlockSpec((tokens, 2 * HEAD), lambda h, part=part: (0, part * pairs + h))
     whole = lambda a: pl.BlockSpec(a.shape, lambda h: (0, 0))
     idc, idr, beginr = ids[:, None], ids[None, :], begins[None, :]
+    plane = lambda part: pl.BlockSpec((None, tokens, 2 * HEAD), lambda h, part=part: (part * pairs + h, 0, 0))
     out = jax.ShapeDtypeStruct((tokens, width), bf16)
     half = tokens * tokens * 5 // 8
     return pl.pallas_call(
@@ -188,7 +189,7 @@
         grid=(pairs,),
         in_specs=[
             pl.BlockSpec((1, 1, 2), lambda h: (h, 0, 0), memory_space=pltpu.SMEM),
-            whole(idc), whole(idr), whole(beginr), column(0), column(1), column(2), column(0),
+            whole(idc), whole(idr), whole(beginr), plane(0), plane(1), plane(2), column(0),
         ],
         out_specs=[column(0)] * 3,
         out_shape=[out] * 3,
@@ -260,6 +261,379 @@
     return blocks
 
 
+MESH = pl.DeviceIdType.MESH
+
+
+class Geometry:
+    def __init__(self, seqs, shards):
+        self.seqs, self.shards = seqs, shards
+        self.sizes = shard_factors(shards)
+        self.s, self.k = lax.axis_index("seq"), lax.axis_index("shard")
+        nz, ny, nc = self.sizes
+        self.z, self.y, self.c = self.k // (ny * nc), self.k // nc % ny, self.k % nc
+        self.inner = (self.z + 1) // 2 % 2
+        high = self.z // 2
+        self.line = (self.z, self.z + 1 - 2 * (self.z % 2), 2 - high, 3 - 3 * high)
+
+    def slot(self, i, dy, dc):
+        nz, ny, nc = self.sizes
+        return (self.line[i] * ny + (self.y + dy) % ny) * nc + (self.c + dc) % nc
+
+
+class Wires:
+    def __init__(self, geometry, send_sems, recv_sems):
+        self.g, self.send_sems, self.recv_sems = geometry, send_sems, recv_sems
+        self.sends, self.used = [], 0
+
+    def block(self, count):
+        first = self.used
+        self.used += count
+        return first
+
+    def copy(self, src, dst, sent, got, s, k):
+        return pltpu.make_async_remote_copy(
+            src_ref=src, dst_ref=dst, send_sem=self.send_sems.at[sent], recv_sem=self.recv_sems.at[got],
+            device_id={"seq": s, "shard": k}, device_id_type=MESH,
+        )
+
+    def send_as(self, src, dst, sent, got, s, k, like):
+        self.copy(src, dst, sent, got, s, k).start()
+        self.sends.append((like, sent))
+
+    def send(self, src, dst, index, s, k, like):
+        self.send_as(src, dst, index, index, s, k, like)
+
+    def arrived(self, dst, index):
+        self.copy(dst, dst, index, index, 1 - self.g.s, self.g.k).wait_recv()
+
+    def drain(self):
+        for like, index in self.sends:
+            self.copy(like, like, index, index, 1 - self.g.s, self.g.k).wait_send()
+        self.sends = []
+
+
+def enter(geometry):
+    g = geometry
+    barrier = pltpu.get_barrier_semaphore()
+    for d in range(1, g.shards):
+        pl.semaphore_signal(
+            barrier, inc=1, device_id={"seq": g.s, "shard": (g.k + d) % g.shards}, device_id_type=MESH
+        )
+    pl.semaphore_signal(barrier, inc=1, device_id={"seq": 1 - g.s, "shard": g.k}, device_id_type=MESH)
+    pl.semaphore_wait(barrier, g.shards)
+
+
+class Gather:
+    def __init__(self, wires, own, out):
+        self.w, self.g, self.own, self.out = wires, wires.g, own, out
+        nz, ny, nc = self.g.sizes
+        self.z0 = wires.block(nz)
+        self.on0 = wires.block(nz)
+        self.y0 = wires.block(nz * ny)
+        self.c0 = wires.block(nz * ny * nc)
+
+    def on_y(self, i, src):
+        g = self.g
+        for dy in range(1, g.sizes[1]):
+            self.w.send(src, self.out.at[g.slot(i, 0, 0)], self.y0 + i * g.sizes[1] + dy, g.s, g.slot(0, dy, 0), self.own)
+
+    def on_core(self, i, dy, src):
+        g = self.g
+        for dc in range(1, g.sizes[2]):
+            index = self.c0 + (i * g.sizes[1] + dy) * g.sizes[2] + dc
+            self.w.send(src, self.out.at[g.slot(i, -dy, 0)], index, g.s, g.slot(0, 0, dc), self.own)
+
+    def start(self):
+        g = self.g
+        here = self.out.at[g.k]
+        self.w.send_as(self.own, here, self.z0 + 2, self.z0 + 3 - g.inner, g.s, g.slot(2, 0, 0), self.own)
+        self.w.send(self.own, here, self.z0 + 1, g.s, g.slot(1, 0, 0), self.own)
+        self.on_y(0, self.own)
+        self.on_core(0, 0, self.own)
+
+    def poll_z(self):
+        g = self.g
+        for i in (1, 2, 3):
+            at = self.out.at[g.slot(i, 0, 0)]
+            self.w.arrived(at, self.z0 + i)
+            if i > 1:
+
+                @pl.when(g.inner == 1)
+                def _(at=at, i=i):
+                    self.w.copy(at, at, self.on0 + i, self.z0 + i, g.s, g.slot(1, 0, 0)).start()
+
+            self.on_y(i, at)
+            self.on_core(i, 0, at)
+
+    def poll_y(self):
+        g = self.g
+        for i in range(g.sizes[0]):
+            for dy in range(1, g.sizes[1]):
+                at = self.out.at[g.slot(i, -dy, 0)]
+                self.w.arrived(at, self.y0 + i * g.sizes[1] + dy)
+                self.on_core(i, dy, at)
+
+    def finish(self):
+        g = self.g
+        for i in range(g.sizes[0]):
+            for dy in range(g.sizes[1]):
+                for dc in range(1, g.sizes[2]):
+                    at = self.out.at[g.slot(i, -dy, -dc)]
+                    self.w.arrived(at, self.c0 + (i * g.sizes[1] + dy) * g.sizes[2] + dc)
+
+        @pl.when(g.inner == 1)
+        def _():
+            for i in (2, 3):
+                self.w.copy(self.own, self.own, self.on0 + i, self.z0 + i, g.s, g.k).wait_send()
+
+
+class Tokens:
+    def __init__(self, wires, packed, out):
+        self.w, self.g, self.packed, self.out = wires, wires.g, packed, out
+        self.a0, self.f0 = wires.block(self.g.shards), wires.block(self.g.shards)
+
+    def lane(self, s, k):
+        return self.out.at[:, s * self.g.shards + k]
+
+    def start(self):
+        g = self.g
+        for d in range(1, g.shards):
+            to = (g.k + d) % g.shards
+            self.w.send(self.packed.at[to], self.lane(g.s, g.k), self.a0 + d, g.s, to, self.packed.at[0])
+        self.w.send(self.packed.at[g.k], self.lane(g.s, g.k), self.f0, 1 - g.s, g.k, self.packed.at[0])
+
+    def poll(self):
+        g = self.g
+        for d in range(1, g.shards):
+            at = self.lane(g.s, (g.k - d) % g.shards)
+            self.w.arrived(at, self.a0 + d)
+            self.w.send(at, at, self.f0 + d, 1 - g.s, g.k, self.packed.at[0])
+
+    def finish(self):
+        g = self.g
+        for d in range(g.shards):
+            self.w.arrived(self.lane(1 - g.s, (g.k - d) % g.shards), self.f0 + d)
+
+
+def forward_kernel(
+    seqs, shards, counts, one_seq,
+    packed, packed_cot, qkv_w, small, dense_w, fc1_w, fc2_w, slopes, idc, idr, beginc,
+    x_out, cot_out, n1_out, qkvw_out, small_out, dense_out, fc1_out, fc2_out, qkv_out, o_out,
+    x_v, n1_v, qkvw_v, small_v, dense_v, fc1_v, fc2_v, cot_v, qkv_v, o_v, vec_v,
+    send_sems, recv_sems, copy_sems,
+):
+    g = Geometry(seqs, shards)
+    wires = Wires(g, send_sems, recv_sems)
+    lanes = seqs * shards
+    width = n1_v.shape[1]
+    pairs = o_v.shape[0] // seqs
+    part = pairs * 2 * HEAD
+    ff_part = fc1_v.shape[1] // shards
+    block = ROWS * lanes
+    blocks = x_v.shape[0]
+
+    local = []
+
+    def bring(src, dst):
+        made = pltpu.make_async_copy(src, dst, copy_sems.at[len(local)])
+        made.start()
+        local.append(made)
+        return made
+
+    tokens = Tokens(wires, packed, x_v)
+    cots = Tokens(wires, packed_cot, cot_out)
+    smalls_at = wires.block(shards)
+    qkv_all = Gather(wires, qkvw_v.at[g.k], qkvw_v)
+    dense_all = Gather(wires, dense_v, dense_out)
+    up_all = Gather(wires, fc1_v, fc1_out)
+    down_all = Gather(wires, fc2_v, fc2_out)
+    heads_at = wires.block(pairs)
+
+    staged_qkv = [
+        bring(
+            qkv_w.at[:, pl.ds(pl.multiple_of(p * width + g.s * part, 128), part)],
+            qkvw_v.at[g.k, :, pl.ds(p * part, part)],
+        )
+        for p in range(3)
+    ]
+    staged_x = bring(packed.at[g.k], x_v.at[:, g.s * shards + g.k])
+    staged_small = bring(small, small_v.at[g.k])
+    staged_dense = bring(dense_w, dense_v)
+    staged_down = bring(fc2_w.at[pl.ds(pl.multiple_of(g.s * ff_part, 8), ff_part), :], fc2_v)
+    staged_cot = bring(packed_cot.at[g.k], cot_v)
+    staged_up = [
+        bring(
+            fc1_w.at[:, pl.ds(pl.multiple_of((i * seqs + g.s) * ff_part, 128), ff_part)],
+            fc1_v.at[:, pl.ds(i * ff_part, ff_part)],
+        )
+        for i in range(shards)
+    ]
+    enter(g)
+    tokens.start()
+    for made in staged_qkv:
+        made.wait()
+    qkv_all.start()
+    staged_small.wait()
+    for d in range(1, shards):
+        wires.send(small_v.at[g.k], small_v.at[g.k], smalls_at + d, g.s, (g.k + d) % shards, small_v.at[0])
+    tokens.poll()
+    staged_dense.wait()
+    for made in staged_up:
+        made.wait()
+    staged_down.wait()
+    staged_cot.wait()
+    kept = [
+        bring(dense_v, dense_out.at[g.k]), bring(fc1_v, fc1_out.at[g.k]), bring(fc2_v, fc2_out.at[g.k]),
+        bring(cot_v, cot_out.at[:, g.s * shards + g.k]),
+    ]
+    dense_all.start()
+    up_all.start()
+    qkv_all.poll_z()
+    for d in range(1, shards):
+        wires.arrived(small_v.at[(g.k - d) % shards], smalls_at + d)
+    qkv_all.poll_y()
+
+    own = width // shards
+    for j in range(shards):
+        for row in range(2):
+            vec_v[row : row + 1, j * own : (j + 1) * own] = small_v[j, row : row + 1, :own]
+    vec_v[2:3, :] = jnp.zeros((1, vec_v.shape[1]), f32)
+    per = 2 * width // shards
+    for i in range(part // per):
+        for row, half in ((0, 0), (2, 1)):
+            j = (half * width + g.s * part) // per + i
+            vec_v[2:3, row * part + i * per : row * part + (i + 1) * per] = small_v[j, 2:3, :per]
+
+    qkv_all.finish()
+    down_all.start()
+    cots.start()
+    kept += [bring(qkvw_v, qkvw_out), bring(small_v, small_out)]
+    staged_x.wait()
+    tokens.finish()
+    kept.append(bring(x_v, x_out))
+
+    @pl.loop(0, blocks)
+    def _(b):
+        x = x_v[b].astype(f32).reshape(block, width)
+        xhat, _ = normalize(x)
+        n1 = (xhat * vec_v[0:1, :width] + vec_v[1:2, :width]).astype(bf16)
+        at = pl.ds(pl.multiple_of(b * block, block), block)
+        n1_v[at, :] = n1
+        for p in range(3):
+            weight = qkvw_v[:, :, p * part : (p + 1) * part].reshape(width, part)
+            out = jnp.dot(n1, weight, preferred_element_type=f32) + vec_v[2:3, p * part : (p + 1) * part]
+            out = out.astype(bf16)
+            for h in range(pairs):
+                qkv_v[p * pairs + h, at, :] = out[:, h * 2 * HEAD : (h + 1) * 2 * HEAD]
+
+    kept += [bring(n1_v, n1_out), bring(qkv_v, qkv_out)]
+    dense_all.poll_z()
+    lane_id = lax.broadcasted_iota(jnp.int32, (1, 2 * HEAD), 1)
+
+    tile = min(256, block)
+
+    def attend(h):
+        q_ref, k_ref, v_ref = qkv_v.at[h], qkv_v.at[pairs + h], qkv_v.at[2 * pairs + h]
+        at_o = g.s * pairs + h
+        for b in range(blocks):
+            end = (b + 1) * block
+            for t in range(block // tile):
+                at = pl.ds(b * block + t * tile, tile)
+                q = q_ref[at, :] * jnp.asarray(HEAD**-0.5, bf16)
+                ids_q = idc[at, :]
+                both = None
+                for j in range(2):
+                    mine = (lane_id // HEAD) == j
+                    qj = jnp.where(mine, q, jnp.zeros_like(q))
+                    s = lax.dot_general(
+                        qj, k_ref[:end, :], (((1,), (1,)), ((), ())), preferred_element_type=f32
+                    )
+                    s = s + slopes[h, j] * idr[:, :end]
+                    if one_seq:
+                        tail = attn_mask(s[:, b * block :], idr[:, b * block : end] <= ids_q)
+                        s = jnp.concatenate([s[:, : b * block], tail], axis=1) if b else tail
+                    else:
+                        ids_k = idr[:, :end]
+                        s = attn_mask(s, (ids_k <= ids_q) & (ids_k >= beginc[at, :]))
+                    top = jnp.max(s, axis=1, keepdims=True)
+                    e = jnp.exp(s - top)
+                    total = jnp.sum(e, axis=1, keepdims=True)
+                    o = jnp.dot(e.astype(bf16), v_ref[:end, :], preferred_element_type=f32) / total
+                    both = o if both is None else jnp.where(mine, o, both)
+                o_v[at_o, at, :] = both.astype(bf16)
+
+    @pl.loop(0, pairs)
+    def _(h):
+        attend(h)
+
+        @pl.when(h == 0)
+        def _():
+            dense_all.poll_y()
+
+        @pl.when(h == 1)
+        def _():
+            up_all.poll_z()
+
+        mine = o_v.at[g.s * pairs + h]
+        wires.copy(mine, mine, heads_at + h, heads_at + h, 1 - g.s, g.k).start()
+
+    up_all.poll_y()
+    down_all.poll_z()
+    cots.poll()
+    down_all.poll_y()
+    dense_all.finish()
+    up_all.finish()
+    down_all.finish()
+    cots.finish()
+    for h in range(pairs):
+        other = o_v.at[(1 - g.s) * pairs + h]
+        wires.arrived(other, heads_at + h)
+    for h in range(pairs):
+        mine = o_v.at[g.s * pairs + h]
+        wires.copy(mine, mine, heads_at + h, heads_at + h, 1 - g.s, g.k).wait_send()
+    kept.append(bring(o_v, o_out))
+    wires.drain()
+    for made in kept:
+        made.wait()
+    assert wires.used <= counts[0] and len(local) <= counts[1]
+
+
+def forward_exchange(packed, packed_cot, qkv_w, small, dense_w, fc1_w, fc2_w, slopes, ids, begins, seqs, shards, one_seq):
+    width, own = qkv_w.shape[0] * shards, qkv_w.shape[0]
+    lanes = seqs * shards
+    blocks = packed.shape[1]
+    cap = blocks * lanes * ROWS
+    part = width // seqs
+    pairs = part // (2 * HEAD)
+    ff = fc1_w.shape[1] // seqs
+    ff_part = ff // shards
+    counts = (320, 48)
+    any_ = pl.BlockSpec(memory_space=pl.ANY)
+    vmem = pl.BlockSpec(memory_space=pltpu.VMEM)
+    smem = pl.BlockSpec(memory_space=pltpu.SMEM)
+    x_shape = (blocks, lanes, ROWS, width)
+    outs = [
+        (x_shape, bf16), (x_shape, bf16), ((cap, width), bf16), ((shards, own, 3 * part), bf16), ((shards,) + small.shape, f32),
+        ((shards, own, width), bf16), ((shards, own, ff), bf16), ((shards, ff_part, width), bf16), ((3 * pairs, cap, 2 * HEAD), bf16),
+        ((seqs * pairs, cap, 2 * HEAD), bf16),
+    ]
+    scratch = [
+        (x_shape, bf16), ((cap, width), bf16), ((shards, own, 3 * part), bf16), ((shards,) + small.shape, f32),
+        ((own, width), bf16), ((own, ff), bf16), ((ff_part, width), bf16), ((blocks, ROWS, width), bf16), ((3 * pairs, cap, 2 * HEAD), bf16),
+        ((seqs * pairs, cap, 2 * HEAD), bf16), ((8, max(width, 3 * part)), f32),
+    ]
+    return pl.pallas_call(
+        functools.partial(forward_kernel, seqs, shards, counts, one_seq),
+        in_specs=[any_] * 7 + [smem, vmem, vmem, vmem],
+        out_specs=[any_] * len(outs),
+        out_shape=[jax.ShapeDtypeStruct(s, d) for s, d in outs],
+        scratch_shapes=[pltpu.VMEM(s, d) for s, d in scratch]
+        + [pltpu.SemaphoreType.DMA((counts[0],)), pltpu.SemaphoreType.DMA((counts[0],)), pltpu.SemaphoreType.DMA((counts[1],))],
+        compiler_params=pltpu.CompilerParams(collective_id=1, has_side_effects=True, vmem_limit_bytes=56 * 2**20),
+        name="forward_exchange",
+    )(packed, packed_cot, qkv_w, small, dense_w, fc1_w, fc2_w, slopes.reshape(pairs, 2), ids[:, None], ids[None, :], begins[:, None])
+
+
 def layout_tables(lengths, lane_count, group_count, per_group):
     seq_rows = lengths // lane_count
     row_start = jnp.cumsum(seq_rows) - seq_rows
@@ -270,6 +644,166 @@
 
 
 def per_device(
+    tokens, cotangent, lengths, first_gain, first_bias, qkv_weight, qv_bias, dense_weight, dense_bias,
+    second_gain, second_bias, fc1_weight, fc1_bias, fc2_weight, fc2_bias,
+):
+    shards, seqs = lax.axis_size("shard"), lax.axis_size("seq")
+    lanes = shards * seqs
+    slots, width = tokens.shape[1], tokens.shape[2]
+    rows = slots // shards
+    cap = slots * seqs
+    per_group = lengths.shape[0] // shards
+    hidden_units = fc1_weight.shape[1]
+    me, group = lax.axis_index("seq"), lax.axis_index("shard")
+    blocks = rows // ROWS
+    heads = width // HEAD // seqs
+    part = heads * HEAD
+    ff_part = hidden_units // shards // seqs
+
+    smalls = (first_gain, first_bias, qv_bias, dense_bias, second_gain, second_bias, fc1_bias, fc2_bias)
+    small_width = -(-max(a.shape[0] for a in smalls) // 128) * 128
+    small = jnp.stack([jnp.pad(a.astype(f32), (0, small_width - a.shape[0])) for a in smalls])
+
+    seq_rows, row_start, slot_rows, slot_start, slot_before = layout_tables(lengths, lanes, shards, per_group)
+    row_in = jnp.arange(rows, dtype=jnp.int32)[None, :, None]
+    inside = ((row_in >= slot_before[:, None]) & (row_in < (slot_before + slot_rows)[:, None])).astype(jnp.int32)
+    send_live = jnp.sum(inside, axis=2) > 0
+    send_row = jnp.sum(inside * (slot_start[:, None] + row_in - slot_before[:, None]), axis=2).reshape(-1)
+
+    def pack(source):
+        return jnp.take(source, send_row, axis=0).reshape(shards, rows, width)
+
+    def own_part(whole):
+        return take(whole.reshape(blocks, seqs, -1, whole.shape[-1]), me, 1)
+
+    place = jnp.arange(cap, dtype=jnp.int32)
+    block_of, in_block = place // (ROWS * lanes), place % (ROWS * lanes)
+    row_of = block_of * ROWS + in_block % ROWS
+    ids = row_of * lanes + in_block // ROWS
+    own_before, own_count = take(slot_before, group), take(slot_rows, group)
+    holds = (row_of[:, None] >= own_before[None]) & (row_of[:, None] < (own_before + own_count)[None])
+    begin_row = jnp.sum(jnp.where(holds, own_before[None], 0), axis=1)
+    begins = jnp.where(jnp.any(holds, axis=1), begin_row * lanes, ids)
+    ids, begins = ids.astype(f32), begins.astype(f32)
+    head_ids = me * heads + jnp.arange(heads, dtype=jnp.int32)
+    slopes = 2.0 ** (-8.0 * (head_ids.astype(f32) + 1.0) / HEADS)
+    one_seq = per_group == 1
+
+    packed_cot = pack(cotangent[0])
+    packed_cot = jnp.where(send_live[:, :, None], packed_cot, jnp.zeros_like(packed_cot))
+    blocked = (shards, blocks, ROWS, width)
+    x_all, cot_all, normed_one, full_qkv, smalls, full_dense, full_up, full_down, qkv, mixed_all = forward_exchange(
+        pack(tokens[0]).reshape(blocked), packed_cot.reshape(blocked),
+        qkv_weight, small, dense_weight, fc1_weight, fc2_weight,
+        slopes, ids, begins, seqs, shards, one_seq,
+    )
+    full_qkv = full_qkv.reshape(width, 3 * part)
+    full_dense = full_dense.reshape(width, width)
+    full_up = full_up.reshape(width, shards * ff_part)
+    full_down = full_down.reshape(shards * ff_part, width)
+    cot_low = cot_all.reshape(cap, width)
+    cot_own = own_part(cot_low)
+    unpack = lambda i, count: smalls[:, i, :count].reshape(-1)
+    own_rows = width // shards
+    gain_one, bias_dense, gain_two, bias_two, bias_down = (unpack(i, own_rows) for i in (0, 3, 4, 5, 7))
+    bias_up = take(unpack(6, seqs * ff_part).reshape(shards, seqs, ff_part), me, 1).reshape(-1)
+    x_own = own_part(x_all.reshape(cap, width))
+    hidden = x_all.reshape(cap, width).astype(f32)
+    mixed_all = mixed_all.transpose(1, 0, 2).reshape(cap, width)
+    branch = jnp.dot(mixed_all, full_dense, preferred_element_type=f32) + bias_dense
+    resid = hidden + branch
+    xhat_two, _ = normalize(resid)
+    normed_two = (xhat_two * gain_two + bias_two).astype(bf16)
+    upper = jnp.dot(normed_two, full_up, preferred_element_type=f32) + bias_up
+    activ = gelu_tanh(upper).astype(bf16)
+    down = jnp.dot(activ, full_down, preferred_element_type=f32)
+    resid_own = own_part(resid)
+    down_own = seq_sum(down.reshape(blocks, seqs, -1, width), 1)
+    block_out = (resid_own + down_own + bias_down).astype(bf16)
+
+    grad_down = jnp.dot(activ.T, cot_low, preferred_element_type=f32).astype(bf16)
+    grad_activ = jnp.dot(cot_low, full_down.T, preferred_element_type=f32)
+    grad_upper = jax.vjp(gelu_tanh, upper)[1](grad_activ)[0].astype(bf16)
+    grad_up = jnp.dot(normed_two.T, grad_upper, preferred_element_type=f32).astype(bf16)
+    grad_bup = jnp.sum(grad_upper.astype(f32), axis=0)
+    grad_normed = jnp.dot(grad_upper, full_up.T, preferred_element_type=f32)
+    grad_normed = seq_sum(grad_normed.reshape(blocks, seqs, -1, width), 1).reshape(slots, width)
+    cot_full = cot_own.reshape(slots, width).astype(f32)
+    grad_bdown = jnp.sum(cot_full, axis=0)
+    xhat_two, root_two = normalize(resid_own.reshape(slots, width))
+    grad_gain_two = jnp.sum(grad_normed * xhat_two, axis=0)
+    grad_bias_two = jnp.sum(grad_normed, axis=0)
+    grad_resid = cot_full + norm_pull(grad_normed, gain_two, xhat_two, root_two)
+
+    grad_branch = grad_resid.astype(bf16)
+    grad_dense = jnp.dot(own_part(mixed_all).reshape(slots, width).T, grad_branch, preferred_element_type=f32).astype(bf16)
+    grad_bdense = jnp.sum(grad_branch.astype(f32), axis=0)
+    grad_mixed = jnp.dot(grad_branch, full_dense.T, preferred_element_type=f32).astype(bf16)
+    got = seq_blocks(grad_mixed.reshape(blocks, -1, seqs, part), 2, bf16)
+    if seqs == 2:
+        grad_mixed = jnp.where(me == 0, jnp.stack(got, 1), jnp.stack(got[::-1], 1))
+    else:
+        grad_mixed = jnp.zeros((blocks, seqs) + got[0].shape[1:], bf16)
+        for d, g in enumerate(got):
+            grad_mixed = lax.dynamic_update_index_in_dim(grad_mixed, g, (me - d) % seqs, 1)
+    grad_mixed = grad_mixed.reshape(cap, part)
+    grad_proj = jnp.concatenate(
+        attention_backward(qkv, grad_mixed, slopes, ids, begins, lanes, one_seq), axis=1
+    )
+    grad_qkv = jnp.dot(normed_one.T, grad_proj, preferred_element_type=f32).astype(bf16)
+    proj_sums = jnp.sum(grad_proj.astype(f32), axis=0)
+    grad_one = jnp.dot(grad_proj, full_qkv.T, preferred_element_type=f32)
+    grad_one = seq_sum(grad_one.reshape(blocks, seqs, -1, width), 1).reshape(slots, width)
+    xhat_one, root_one = normalize(x_own.reshape(slots, width).astype(f32))
+    grad_gain_one = jnp.sum(grad_one * xhat_one, axis=0)
+    grad_bias_one = jnp.sum(grad_one, axis=0)
+    tokens_grad = (grad_resid + norm_pull(grad_one, gain_one, xhat_one, root_one)).astype(bf16)
+
+    row_here = jnp.arange(slots, dtype=jnp.int32)[:, None]
+    seq_in = ((row_here >= row_start[None]) & (row_here < (row_start + seq_rows)[None])).astype(jnp.int32)
+    home = jnp.arange(lengths.shape[0], dtype=jnp.int32) // per_group
+    fetch = jnp.sum(seq_in * (home[None] * rows + slot_before.reshape(-1)[None] + row_here - row_start[None]), axis=1)
+    fetch_live = jnp.sum(seq_in, axis=1) > 0
+
+    def to_stream(own):
+        sent = own.reshape(blocks, shards, ROWS, width).transpose(1, 0, 2, 3).reshape(shards, rows, width)
+        got = lax.all_to_all(sent, "shard", split_axis=0, concat_axis=0, tiled=True)
+        taken = jnp.take(got.reshape(-1, width), fetch, axis=0)
+        return jnp.where(fetch_live[:, None], taken, jnp.zeros_like(taken))[None]
+
+    down_block = shard_reduce(grad_down.reshape(shards, ff_part, width), bf16)
+    up_block = shard_reduce(grad_up.reshape(shards, -1, shards * ff_part), bf16)
+    dense_block = shard_reduce(grad_dense.reshape(shards, -1, width), bf16)
+    qkv_block = shard_reduce(grad_qkv.reshape(shards, -1, 3 * part), bf16)
+
+    def spread(vector, index_shape):
+        zero = jnp.zeros(index_shape, f32)
+        return lax.dynamic_update_index_in_dim(zero, vector, me, 1)
+
+    sums = proj_sums.reshape(3, part)
+    qv = spread(jnp.stack([sums[0], sums[2]]), (2, seqs, part)).reshape(shards, -1)
+    bup = spread(grad_bup.reshape(shards, ff_part), (shards, seqs, ff_part)).reshape(shards, -1)
+    rest = (grad_gain_one, grad_bias_one, grad_bdense, grad_gain_two, grad_bias_two, grad_bdown)
+    packed = jnp.concatenate([a.reshape(shards, -1) for a in rest] + [qv, bup], axis=1)
+    packed = shard_reduce(packed, f32)
+    packed = jnp.sum(seq_gather(packed, 0), axis=0)
+    cuts, at = [], 0
+    for a in [a.reshape(shards, -1) for a in rest] + [qv, bup]:
+        cuts.append(packed[at : at + a.shape[1]])
+        at += a.shape[1]
+    g_gain_one, g_bias_one, g_bdense, g_gain_two, g_bias_two, g_bdown, g_qv, g_bup = cuts
+
+    g_dense = jnp.sum(seq_gather(dense_block.astype(bf16), 0).astype(f32), axis=0)
+    g_qkv = seq_gather(qkv_block.astype(bf16).reshape(-1, 3, part), 2).reshape(-1, 3 * width).astype(f32)
+    g_up = seq_gather(up_block.astype(bf16).reshape(-1, shards, ff_part), 2).reshape(-1, hidden_units).astype(f32)
+    g_down = seq_gather(down_block.astype(bf16), 0).reshape(-1, width).astype(f32)
+    return (
+        to_stream(block_out), to_stream(tokens_grad.reshape(blocks, -1, width)),
+        g_gain_one, g_bias_one, g_qkv, g_qv, g_dense, g_bdense, g_gain_two, g_bias_two, g_up, g_bup, g_down, g_bdown,
+    )
+
+
+def per_device_any(
     tokens, cotangent, lengths, first_gain, first_bias, qkv_weight, qv_bias, dense_weight, dense_bias,
     second_gain, second_bias, fc1_weight, fc1_bias, fc2_weight, fc2_bias,
 ):
@@ -387,8 +921,9 @@
         for d, g in enumerate(got):
             grad_mixed = lax.dynamic_update_index_in_dim(grad_mixed, g, (me - d) % seqs, 1)
     grad_mixed = grad_mixed.reshape(cap, part)
+    planes = qkv.reshape(cap, -1, 2 * HEAD).transpose(1, 0, 2)
     grad_proj = jnp.concatenate(
-        attention_backward(qkv, grad_mixed, slopes, ids, begins, lanes, one_seq), axis=1
+        attention_backward(planes, grad_mixed, slopes, ids, begins, lanes, one_seq), axis=1
     )
     grad_qkv = jnp.dot(normed_one.T, grad_proj, preferred_element_type=f32).astype(bf16)
     proj_sums = jnp.sum(grad_proj.astype(f32), axis=0)
@@ -446,6 +981,7 @@
 def solution(mesh):
     rows, vector, stream = P("shard", None), P("shard"), P(("seq", "shard"), None, None)
     params = (vector, vector, rows, vector, rows, vector, vector, vector, rows, vector, rows, vector)
+    fused = mesh.shape["seq"] == 2 and shard_factors(mesh.shape["shard"])[0] == 4
     return jax.shard_map(
-        per_device, mesh=mesh, in_specs=(stream, stream, P()) + params, out_specs=(stream, stream) + params, check_vma=False
+        per_device if fused else per_device_any, mesh=mesh, in_specs=(stream, stream, P()) + params, out_specs=(stream, stream) + params, check_vma=False
     )

time: 574 us -> 536 us (0.934)
  Pallas kernels: 46.1 us -> 181 us
  waiting for transfers between devices: 197 us -> 70.6 us
  starting transfers between devices: 73.5 us -> 55.3 us
  other arithmetic: 70.9 us -> 55.7 us
  between operations: 15.8 us -> 2.42 us
  local copies, waits for them, and re-layouts: 93.8 us -> 86.2 us
  matrix products: 69.5 us -> 77 us
    pallas_call x1, Pallas kernels: 15.5 us -> 150 us  [forward_exchange(): pl.pallas_call(functools.partial(forward_kernel, seqs, shards, counts, on...]
    all_to_all x2 -> x0, waiting for transfers between devices: 49.3 us -> none  [to_groups(): lax.all_to_all(packed, 'shard', split_axis=0, concat_axis=0, tiled=True)]
    ppermute x4, waiting for transfers between devices: 43.5 us -> 1.2 us  [seq_blocks(): got.append(lax.ppermute(sent, 'seq', [(i, (i + d) % n) for i in range(n)]))]
    all_to_all x2 -> x0, starting transfers between devices: 23 us -> none  [to_groups(): lax.all_to_all(packed, 'shard', split_axis=0, concat_axis=0, tiled=True)]
    all_gather x4 -> x0, waiting for transfers between devices: 20.3 us -> none  [per_device(): gather = lambda a: lax.all_gather(a, 'shard', axis=0, tiled=False)]
    select_n x4 -> x0, local copies, waits for them, and re-layouts: 12.7 us -> none  [seq_gather(): jnp.where(me == 0, jnp.stack([block, peer], axis), jnp.stack([peer, block...]
    convert_element_type x4 -> x0, other arithmetic: 10.2 us -> none  [the longest x2 6.9 us: per_device(): normed_one = (xhat_one * gain_one + bias_one).astype(bf16)]
    ppermute x8 -> x5, waiting for transfers between devices: 14.6 us -> 5.09 us  [seq_gather(): peer = lax.ppermute(block, 'seq', [(0, 1), (1, 0)])]
  transfers between devices with their start and end apart: 45 -> 36, of which waited for: 19 -> 7; matrix products, arithmetic and copies ran while one was open for 29% -> 26% of each run, Pallas kernels for 8% -> 6%
where the time goes in v2:
time: 536 us; the launch traced here: 528 us
  Pallas kernels  181 us (34%)
  local copies, waits for them, and re-layouts  86.2 us (16%)
  matrix products  77 us (14%)
  waiting for transfers between devices  70.6 us (13%)
  other arithmetic  55.7 us (10%)
  starting transfers between devices  55.3 us (10%)
    pallas_call x1, Pallas kernels, forward_exchange(): pl.pallas_call(functools.partial(forward_kernel, seqs, shards, counts, on...  150 us
    ppermute x25, waiting for transfers between devices, shard_reduce(): total = total + lax.ppermute(sent, 'shard', pairs).astype(f32)  64.3 us
    pallas_call x1, Pallas kernels, attention_backward(): pl.pallas_call(functools.partial(attn_bwd_kernel, lanes, tile, one_seq),...  30.6 us
    ppermute x25, starting transfers between devices, shard_reduce(): total = total + lax.ppermute(sent, 'shard', pairs).astype(f32)  26.3 us
    unnamed x123, local copies, waits for them, and re-layouts  18.6 us
    dot_general x1, matrix products, per_device(): grad_activ = jnp.dot(cot_low, full_down.T, preferred_element_type=f32)  14.9 us
    squeeze x12, local copies, waits for them, and re-layouts, take(): return lax.dynamic_index_in_dim(blocks, index, axis, keepdims=False)  14.2 us
    convert_element_type x8, other arithmetic, shard_reduce(): blocks = total if axis == 0 else total.astype(dtype)  13.9 us
  transfers between devices with their start and end apart: 36, of which 7 were waited for; matrix products, arithmetic and copies ran while one was open for 26% of the time, Pallas kernels for 6%

profile of v2, /device:TPU:0, one launch (start us, length us, event | category | flops | bytes accessed | tf_op | source)
XLA Modules:
  0.0 527.7 jit_solution(9808192631998800237)
XLA Ops:
  15.3 150.0 %forward_exchange.1 = (bf16[4,32,8,1024]{3,2,1,0:T(8,128)(2,1)}, bf16[4,32,8,1024]{3,2,1,0:T(8,128)(2,1)}, bf16[1024,1024]{1,0:T(8,128)(2,1)}, bf16[16,64,1536]{...) custom-call(bf16[16,4,8,1024]{3,2,1,0:T(8,128)(2,1)} %bitcast.371, ...), custom_call_target="tpu_custom_call" | custom-call | tf_op jit(solution)/shard_map/forward_exchange/pallas_call | solution.py:625
  167.6 4.2 copy.108
  172.0 5.1 fusion.98
  179.1 11.5 %fusion.93 = f32[1024,2048]{1,0:T(8,128)} fusion(bf16[1024,2048]{1,0:T(8,128)(2,1)} %bitcast.405, f32[1024,1024]{1,0:T(8,128)} %copy-done.3, f32[1024]{0:T(1024)S(1)} %add.746, f32[1024]{0:T(1024)S(1)} %mul.337, f32[1024]{0:T(1024)S(1)} %add_rsqrt_fusion, f32[1024]{0:T(1024)S(1)} %broadcast_multiply_fusion), kind=kOutput, calls=%fused_computation.269 | convolution fusion | flops 4300210176 | bytes 16793600 | tf_op jit(solution)/shard_map/dot_general | solution.py:717
  190.6 14.9 %convert_reduce_fusion = (f32[2048]{0:T(1024)S(1)}, bf16[1024,2048]{1,0:T(8,128)(2,1)S(1)}, bf16[1024,2048]{1,0:T(8,128)(2,1)}) fusion(f32[1024,2048]{1,0:T(8,128)} %fusion.93, f32[2048]{0:T(1024)S(1)} %bitcast.400, bf16[1024,1024]{1,0:T(8,128)(2,1)S(1)} %bitcast.384, bf16[2048,1024]{1,0:T(8,128)(2,1)S(1)} %bitcast.404), kind=kOutput, calls=%fused_computation.14 | convolution fusion | flops 4355782656 | bytes 23085056 | tf_op jit(solution)/shard_map/dot_general | solution.py:725
  207.5 6.1 %fusion.100 = f32[4,2,128,1024]{3,2,1,0:T(8,128)} fusion(bf16[4,2,128,2048]{3,2,1,0:T(8,128)(2,1)S(1)} %bitcast.411, bf16[1024,2048,1,1]{1,0,3,2:T(8,128)(2,1)S(1)} %bitcast.406), kind=kOutput, calls=%fused_computation.274 | convolution fusion | flops 4294967296 | bytes 12582912 | tf_op jit(solution)/shard_map/dot_general | solution.py:729
  216.8 7.7 %fusion.99 = f32[4,2,128,1024]{3,2,1,0:T(8,128)S(1)} fusion(bf16[4,2,128,2048]{3,2,1,0:T(8,128)(2,1)} %bitcast.410, bf16[2048,1024,1,1]{1,0,3,2:T(8,128)(2,1)} %bitcast.403), kind=kOutput, calls=%fused_computation.273 | convolution fusion | flops 4294967296 | bytes 12582912 | tf_op jit(solution)/shard_map/dot_general | solution.py:719
  229.1 10.3 %convolution_convert_fusion.2 = bf16[1024,2048]{1,0:T(8,128)(2,1)} fusion(bf16[1024,2048]{1,0:T(8,128)(2,1)} %copy-done.57, f32[1024,1024]{1,0:T(8,128)} %copy-done.3, f32[1024]{0:T(1024)S(1)} %add.746, f32[1024]{0:T(1024)S(1)} %mul.337, f32[1024]{0:T(1024)S(1)} %add_rsqrt_fusion, f32[1024]{0:T(1024)S(1)} %broadcast_multiply_fusion), kind=kOutput, calls=%fused_computation.27 | convolution fusion | flops 4302307328 | bytes 12599296 | tf_op jit(solution)/shard_map/dot_general | solution.py:727
  242.7 7.0 %convolution_convert_fusion.1 = bf16[2048,1024]{1,0:T(8,128)(2,1)S(1)} fusion(bf16[1024,2048]{1,0:T(8,128)(2,1)} %get-tuple-element.68, bf16[1024,1024]{1,0:T(8,128)(2,1)S(1)} %bitcast.385), kind=kOutput, calls=%fused_computation.26 | convolution fusion | flops 4297064448 | bytes 10485760 | tf_op jit(solution)/shard_map/dot_general | solution.py:724
  258.9 4.6 reshape_reshape.29
  264.7 5.6 %multiply_reduce_fusion.1 = (f32[1024]{0:T(1024)S(1)}, f32[4,128]{1,0:T(4,128)S(1)}, f32[4,128]{1,0:T(4,128)S(1)}, f32[1024]{0:T(1024)S(1)}, f32[4,128,1024]{2,1,0:T(8,128)S(1)}, /*index=5*/bf16[4,16,8,1024]{3,2,1,0:T(8,128)(2,1)}) fusion(f32[4,2,128,1024]{3,2,1,0:T(8,128)} %bitcast.359, s32[]{:T(128)S(6)} %select_n.528, f32[4,128]{1,0:T(4,128)S(1)} %add_rsqrt_fusion.2, ...), kind=kLoop, calls=%fused_computation.84 | loop fusion | flops 8385536 | bytes 11558916 | tf_op jit(solution)/shard_map/reduce_sum | solution.py:734
  285.1 8.2 %all-to-all-start = ((bf16[16,32,1024]{2,1,0:T(8,128)(2,1)}), bf16[16,32,1024]{2,1,0:T(8,128)(2,1)S(1)}, u32[]{:S(2)}, u32[]{:S(2)}) async-start(bf16[16,32,1024]{2,1,0:T(8,128)(2,1)} %bitcast.377), calls=%async_computation | async-start | bytes 2097152 | tf_op jit(solution)/shard_map/all_to_all | solution.py:770
  300.5 30.6 %attention_backward.1 = (bf16[1024,512]{1,0:T(8,128)(2,1)}, bf16[1024,512]{1,0:T(8,128)(2,1)}, bf16[1024,512]{1,0:T(8,128)(2,1)}) custom-call(f32[4,1,2]{2,1,0:T(1,128)} %multiply_power_fusion.slope_ref, f32[1024,1]{1,0:T(8,128)} %get-tuple-element.110.idc.idc_ref, f32[1,1024]{1,0:T(1,128)} %get-tuple-element.106.idr.idr_ref, ...), custom_call_target="tpu_custom_call" | custom-call | flops 6710886400 | bytes 7340032 | tf_op jit(solution)/shard_map/attention_backward/pallas_call | solution.py:187
  342.6 6.0 %convolution_convert_fusion = bf16[1024,1536]{1,0:T(8,128)(2,1)S(1)} fusion(bf16[1024,1024]{1,0:T(8,128)(2,1)} %get-tuple-element.40, bf16[1024,1536]{1,0:T(8,128)(2,1)} %copy-done.16), kind=kOutput, calls=%fused_computation.25 | convolution fusion | flops 3222798336 | bytes 8388608 | tf_op jit(solution)/shard_map/dot_general | solution.py:753
  366.7 3.7 fusion.25
  374.4 17.5 %collective-permute-done.5 = f32[4,768]{1,0:T(4,128)S(1)} collective-permute-done((f32[4,768]{1,0:T(4,128)S(1)}, f32[4,768]{1,0:T(4,128)S(1)}, u32[]{:S(2)}, u32[]{:S(2)}) %collective-permute-start.5) | collective-permute-done | bytes 12320 | tf_op jit(solution)/shard_map/ppermute | solution.py:259
  404.0 4.5 copy_bitcast_fusion.2
  411.9 3.5 collective-permute-done.18
  424.9 11.6 %collective-permute-done.29 = bf16[4,128,1024]{2,1,0:T(8,128)(2,1)S(1)} collective-permute-done((bf16[4,128,1024]{2,1,0:T(8,128)(2,1)S(1)}, bf16[4,128,1024]{2,1,0:T(8,128)(2,1)S(1)}, u32[]{:S(2)}, u32[]{:S(2)}) %collective-permute-start.29) | collective-permute-done | bytes 1048608 | tf_op jit(solution)/shard_map/ppermute | solution.py:259
  442.4 14.6 %collective-permute-done.25 = bf16[64,2048]{1,0:T(8,128)(2,1)S(1)} collective-permute-done((bf16[64,2048]{1,0:T(8,128)(2,1)S(1)}, bf16[64,2048]{1,0:T(8,128)(2,1)S(1)}, u32[]{:S(2)}, u32[]{:S(2)}) %collective-permute-start.25) | collective-permute-done | bytes 262176 | tf_op jit(solution)/shard_map/ppermute | solution.py:259
  458.4 4.9 all-to-all-start.1
  469.5 6.9 %collective-permute-start.33 = (bf16[128,1024]{1,0:T(8,128)(2,1)S(1)}, bf16[128,1024]{1,0:T(8,128)(2,1)}, u32[]{:S(2)}, u32[]{:S(2)}) collective-permute-start(bf16[128,1024]{1,0:T(8,128)(2,1)S(1)} %fusion.67), channel_id=1, source_target_pairs={{0,16},{16,0},{1,17},{17,1},{2,18},{18,2},{3,19},{19,3},{4,20},{20... | collective-permute-start | bytes 786440 | tf_op jit(solution)/shard_map/ppermute | solution.py:215
  489.9 17.1 %collective-permute-done.13 = bf16[64,1536]{1,0:T(8,128)(2,1)} collective-permute-done((bf16[64,1536]{1,0:T(8,128)(2,1)}, bf16[64,1536]{1,0:T(8,128)(2,1)}, u32[]{:S(2)}, u32[]{:S(2)}) %collective-permute-start.13) | collective-permute-done | bytes 196640 | tf_op jit(solution)/shard_map/ppermute | solution.py:259
  512.1 5.1 collective-permute-done.15
  (348 shorter events, 164.3 us)
Async XLA Ops:
  216.3 48.5 %collective-permute-start.1 = (bf16[4,128,1024]{2,1,0:T(8,128)(2,1)}, bf16[4,128,1024]{2,1,0:T(8,128)(2,1)S(1)}, u32[]{:S(2)}, u32[]{:S(2)}) collective-permute-start(bf16[4,128,1024]{2,1,0:T(8,128)(2,1)} %fusion.42), channel_id=1, source_target_pairs={{0,16},{16,0},{1,17},{17,1},{2,18},{18,2},{3,19},{19,3},{4,20},{20... | collective-permute-start | bytes 3145736 | tf_op jit(solution)/shard_map/ppermute | solution.py:229
  227.6 37.2 %collective-permute-start = (bf16[4,128,1024]{2,1,0:T(8,128)(2,1)}, bf16[4,128,1024]{2,1,0:T(8,128)(2,1)}, u32[]{:S(2)}, u32[]{:S(2)}) collective-permute-start(bf16[4,128,1024]{2,1,0:T(8,128)(2,1)} %fusion.40), channel_id=1, source_target_pairs={{0,16},{16,0},{1,17},{17,1},{2,18},{18,2},{3,19},{19,3},{4,20},{20... | collective-permute-start | bytes 3145736 | tf_op jit(solution)/shard_map/ppermute | solution.py:229
  242.7 114.1 %collective-permute-start.22 = (bf16[4,2,64,2048]{3,2,1,0:T(8,128)(2,1)}, bf16[4,2,64,2048]{3,2,1,0:T(8,128)(2,1)}, u32[]{:S(2)}, u32[]{:S(2)}) collective-permute-start(bf16[4,2,64,2048]{3,2,1,0:T(8,128)(2,1)} %dynamic-slice_bitcast_fusion.1), channel_id=1, source_target_pairs={{0,1},{1,0},{2,3},{3,2},{4,5},{5,4},{6,7},{7,6},{8,9},{9,8},{10,11... | collective-permute-start | bytes 6291464 | tf_op jit(solution)/shard_map/ppermute | solution.py:259
  252.9 108.3 %collective-permute-start.28 = (bf16[4,2,128,1024]{3,2,1,0:T(8,128)(2,1)}, bf16[4,2,128,1024]{3,2,1,0:T(8,128)(2,1)}, u32[]{:S(2)}, u32[]{:S(2)}) collective-permute-start(bf16[4,2,128,1024]{3,2,1,0:T(8,128)(2,1)} %dynamic-slice_bitcast_fusion), channel_id=1, source_target_pairs={{0,1},{1,0},{2,3},{3,2},{4,5},{5,4},{6,7},{7,6},{8,9},{9,8},{10,11... | collective-permute-start | bytes 6291464 | tf_op jit(solution)/shard_map/ppermute | solution.py:259
  280.6 17.5 %collective-permute-start.2 = (bf16[4,128,512]{2,1,0:T(8,128)(2,1)}, bf16[4,128,512]{2,1,0:T(8,128)(2,1)}, u32[]{:S(2)}, u32[]{:S(2)}) collective-permute-start(bf16[4,128,512]{2,1,0:T(8,128)(2,1)} %bitcast.350), channel_id=1, source_target_pairs={{0,16},{16,0},{1,17},{17,1},{2,18},{18,2},{3,19},{19,3},{4,20},{20... | collective-permute-start | bytes 1572872 | tf_op jit(solution)/shard_map/ppermute | solution.py:229
  285.1 173.3 %all-to-all-start = ((bf16[16,32,1024]{2,1,0:T(8,128)(2,1)}), bf16[16,32,1024]{2,1,0:T(8,128)(2,1)S(1)}, u32[]{:S(2)}, u32[]{:S(2)}) async-start(bf16[16,32,1024]{2,1,0:T(8,128)(2,1)} %bitcast.377), calls=%async_computation | async-start | bytes 2097152 | tf_op jit(solution)/shard_map/all_to_all | solution.py:770
  297.5 53.8 %collective-permute-start.16 = (bf16[4,2,64,1024]{3,2,1,0:T(8,128)(2,1)}, bf16[4,2,64,1024]{3,2,1,0:T(8,128)(2,1)}, u32[]{:S(2)}, u32[]{:S(2)}) collective-permute-start(bf16[4,2,64,1024]{3,2,1,0:T(8,128)(2,1)} %dynamic-slice_bitcast_fusion.4), channel_id=1, source_target_pairs={{0,1},{1,0},{2,3},{3,2},{4,5},{5,4},{6,7},{7,6},{8,9},{9,8},{10,11... | collective-permute-start | bytes 3145736 | tf_op jit(solution)/shard_map/ppermute | solution.py:259
  340.4 25.7 %collective-permute-start.3 = (bf16[4,128,1024]{2,1,0:T(8,128)(2,1)}, bf16[4,128,1024]{2,1,0:T(8,128)(2,1)}, u32[]{:S(2)}, u32[]{:S(2)}) collective-permute-start(bf16[4,128,1024]{2,1,0:T(8,128)(2,1)} %fusion.41), channel_id=1, source_target_pairs={{0,16},{16,0},{1,17},{17,1},{2,18},{18,2},{3,19},{19,3},{4,20},{20... | collective-permute-start | bytes 3145736 | tf_op jit(solution)/shard_map/ppermute | solution.py:229
  351.3 66.4 %collective-permute-start.10 = (bf16[4,2,64,1536]{3,2,0,1:T(8,128)(2,1)}, bf16[4,2,64,1536]{3,2,0,1:T(8,128)(2,1)}, u32[]{:S(2)}, u32[]{:S(2)}) collective-permute-start(bf16[4,2,64,1536]{3,2,0,1:T(8,128)(2,1)} %bitcast.348), channel_id=1, source_target_pairs={{0,1},{1,0},{2,3},{3,2},{4,5},{5,4},{6,7},{7,6},{8,9},{9,8},{10,11... | collective-permute-start | bytes 4718600 | tf_op jit(solution)/shard_map/ppermute | solution.py:259
  360.6 61.6 %collective-permute-start.23 = (bf16[4,64,2048]{2,1,0:T(8,128)(2,1)}, bf16[4,64,2048]{2,1,0:T(8,128)(2,1)}, u32[]{:S(2)}, u32[]{:S(2)}) collective-permute-start(bf16[4,64,2048]{2,1,0:T(8,128)(2,1)} %dynamic-slice_bitcast_fusion.3), channel_id=1, source_target_pairs={{0,2},{1,3},{2,0},{3,1},{4,6},{5,7},{6,4},{7,5},{8,10},{9,11},{10,... | collective-permute-start | bytes 3145736 | tf_op jit(solution)/shard_map/ppermute | solution.py:259
  372.3 19.5 %collective-permute-start.5 = (f32[4,768]{1,0:T(4,128)S(1)}, f32[4,768]{1,0:T(4,128)S(1)}, u32[]{:S(2)}, u32[]{:S(2)}) collective-permute-start(f32[4,768]{1,0:T(4,128)S(1)} %bitcast.398), channel_id=1, source_target_pairs={{0,2},{1,3},{2,0},{3,1},{4,6},{5,7},{6,4},{7,5},{8,10},{9,11},{10,... | collective-permute-start | bytes 36872 | tf_op jit(solution)/shard_map/ppermute | solution.py:259
  410.3 26.2 %collective-permute-start.29 = (bf16[4,128,1024]{2,1,0:T(8,128)(2,1)S(1)}, bf16[4,128,1024]{2,1,0:T(8,128)(2,1)S(1)}, u32[]{:S(2)}, u32[]{:S(2)}) collective-permute-start(bf16[4,128,1024]{2,1,0:T(8,128)(2,1)S(1)} %copy-done.35), channel_id=1, source_target_pairs={{0,2},{1,3},{2,0},{3,1},{4,6},{5,7},{6,4},{7,5},{8,10},{9,11},{10,... | collective-permute-start | bytes 3145736 | tf_op jit(solution)/shard_map/ppermute | solution.py:259
  416.3 24.1 %collective-permute-start.21 = (bf16[64,1024]{1,0:T(8,128)(2,1)S(1)}, bf16[64,1024]{1,0:T(8,128)(2,1)S(1)}, u32[]{:S(2)}, u32[]{:S(2)}) collective-permute-start(bf16[64,1024]{1,0:T(8,128)(2,1)S(1)} %fusion.80), channel_id=1, source_target_pairs={{0,16},{16,0},{1,17},{17,1},{2,18},{18,2},{3,19},{19,3},{4,20},{20... | collective-permute-start | bytes 393224 | tf_op jit(solution)/shard_map/ppermute | solution.py:215
  420.7 55.7 %collective-permute-start.11 = (bf16[4,64,1536]{2,1,0:T(8,128)(2,1)}, bf16[4,64,1536]{2,1,0:T(8,128)(2,1)}, u32[]{:S(2)}, u32[]{:S(2)}) collective-permute-start(bf16[4,64,1536]{2,1,0:T(8,128)(2,1)} %dynamic-slice_bitcast_fusion.5), channel_id=1, source_target_pairs={{0,2},{1,3},{2,0},{3,1},{4,6},{5,7},{6,4},{7,5},{8,10},{9,11},{10,... | collective-permute-start | bytes 2359304 | tf_op jit(solution)/shard_map/ppermute | solution.py:259
  424.7 17.1 %collective-permute-start.26 = (bf16[64,2048]{1,0:T(8,128)(2,1)S(1)}, bf16[64,2048]{1,0:T(8,128)(2,1)S(1)}, u32[]{:S(2)}, u32[]{:S(2)}) collective-permute-start(bf16[64,2048]{1,0:T(8,128)(2,1)S(1)} %get-tuple-element.77), channel_id=1, source_target_pairs={{0,12},{1,13},{2,14},{3,15},{4,0},{5,1},{6,2},{7,3},{8,4},{9,5},{1... | collective-permute-start | bytes 786440 | tf_op jit(solution)/shard_map/ppermute | solution.py:259
  424.7 32.2 %collective-permute-start.25 = (bf16[64,2048]{1,0:T(8,128)(2,1)S(1)}, bf16[64,2048]{1,0:T(8,128)(2,1)S(1)}, u32[]{:S(2)}, u32[]{:S(2)}) collective-permute-start(bf16[64,2048]{1,0:T(8,128)(2,1)S(1)} %get-tuple-element.78), channel_id=1, source_target_pairs={{0,8},{1,9},{2,10},{3,11},{4,12},{5,13},{6,14},{7,15},{8,0},{9,1},... | collective-permute-start | bytes 786440 | tf_op jit(solution)/shard_map/ppermute | solution.py:259
  436.5 28.9 %collective-permute-start.24 = (bf16[64,2048]{1,0:T(8,128)(2,1)}, bf16[64,2048]{1,0:T(8,128)(2,1)}, u32[]{:S(2)}, u32[]{:S(2)}) collective-permute-start(bf16[64,2048]{1,0:T(8,128)(2,1)} %get-tuple-element.76), channel_id=1, source_target_pairs={{0,4},{1,5},{2,6},{3,7},{4,8},{5,9},{6,10},{7,11},{8,12},{9,13},{1... | collective-permute-start | bytes 786440 | tf_op jit(solution)/shard_map/ppermute | solution.py:259
  440.4 27.7 %collective-permute-start.32 = (bf16[128,1024]{1,0:T(8,128)(2,1)}, bf16[128,1024]{1,0:T(8,128)(2,1)}, u32[]{:S(2)}, u32[]{:S(2)}) collective-permute-start(bf16[128,1024]{1,0:T(8,128)(2,1)} %get-tuple-element.74), channel_id=1, source_target_pairs={{0,12},{1,13},{2,14},{3,15},{4,0},{5,1},{6,2},{7,3},{8,4},{9,5},{1... | collective-permute-start | bytes 786440 | tf_op jit(solution)/shard_map/ppermute | solution.py:259
  441.8 26.4 %collective-permute-start.31 = (bf16[128,1024]{1,0:T(8,128)(2,1)}, bf16[128,1024]{1,0:T(8,128)(2,1)}, u32[]{:S(2)}, u32[]{:S(2)}) collective-permute-start(bf16[128,1024]{1,0:T(8,128)(2,1)} %get-tuple-element.75), channel_id=1, source_target_pairs={{0,8},{1,9},{2,10},{3,11},{4,12},{5,13},{6,14},{7,15},{8,0},{9,1},... | collective-permute-start | bytes 786440 | tf_op jit(solution)/shard_map/ppermute | solution.py:259
  458.4 63.1 %all-to-all-start.1 = ((bf16[16,32,1024]{2,1,0:T(8,128)(2,1)}), bf16[16,32,1024]{2,1,0:T(8,128)(2,1)S(1)}, u32[]{:S(2)}, u32[]{:S(2)}) async-start(bf16[16,32,1024]{2,1,0:T(8,128)(2,1)} %copy_bitcast_fusion.2), calls=%async_computation.1 | async-start | bytes 2097152 | tf_op jit(solution)/shard_map/all_to_all | solution.py:770
  466.8 17.0 %collective-permute-start.27 = (bf16[64,16,128]{2,1,0:T(8,128)(2,1)S(1)}, bf16[64,16,128]{2,1,0:T(8,128)(2,1)S(1)}, u32[]{:S(2)}, u32[]{:S(2)}) collective-permute-start(bf16[64,16,128]{2,1,0:T(8,128)(2,1)S(1)} %bitcast.389), channel_id=1, source_target_pairs={{0,16},{16,0},{1,17},{17,1},{2,18},{18,2},{3,19},{19,3},{4,20},{20... | collective-permute-start | bytes 786440 | tf_op jit(solution)/shard_map/ppermute | solution.py:215
  469.5 19.2 %collective-permute-start.33 = (bf16[128,1024]{1,0:T(8,128)(2,1)S(1)}, bf16[128,1024]{1,0:T(8,128)(2,1)}, u32[]{:S(2)}, u32[]{:S(2)}) collective-permute-start(bf16[128,1024]{1,0:T(8,128)(2,1)S(1)} %fusion.67), channel_id=1, source_target_pairs={{0,16},{16,0},{1,17},{17,1},{2,18},{18,2},{3,19},{19,3},{4,20},{20... | collective-permute-start | bytes 786440 | tf_op jit(solution)/shard_map/ppermute | solution.py:215
  478.7 28.3 %collective-permute-start.13 = (bf16[64,1536]{1,0:T(8,128)(2,1)}, bf16[64,1536]{1,0:T(8,128)(2,1)}, u32[]{:S(2)}, u32[]{:S(2)}) collective-permute-start(bf16[64,1536]{1,0:T(8,128)(2,1)} %get-tuple-element.83), channel_id=1, source_target_pairs={{0,8},{1,9},{2,10},{3,11},{4,12},{5,13},{6,14},{7,15},{8,0},{9,1},... | collective-permute-start | bytes 589832 | tf_op jit(solution)/shard_map/ppermute | solution.py:259
  481.8 25.2 %collective-permute-start.12 = (bf16[64,1536]{1,0:T(8,128)(2,1)}, bf16[64,1536]{1,0:T(8,128)(2,1)}, u32[]{:S(2)}, u32[]{:S(2)}) collective-permute-start(bf16[64,1536]{1,0:T(8,128)(2,1)} %get-tuple-element.81), channel_id=1, source_target_pairs={{0,4},{1,5},{2,6},{3,7},{4,8},{5,9},{6,10},{7,11},{8,12},{9,13},{1... | collective-permute-start | bytes 589832 | tf_op jit(solution)/shard_map/ppermute | solution.py:259
  (70 other events, 623.9 us)

commit v3 on v2

--- a/solution.py
+++ b/solution.py
@@ -634,6 +634,374 @@
     )(packed, packed_cot, qkv_w, small, dense_w, fc1_w, fc2_w, slopes.reshape(pairs, 2), ids[:, None], ids[None, :], begins[:, None])
 
 
+class Scatter:
+    def __init__(self, wires, full, own, bufs):
+        self.w, self.g, self.full, self.own = wires, wires.g, full, own
+        self.rc, self.ry, self.rz, self.fin = bufs
+        self.at = wires.block(8)
+
+    def add(self, count, into, other):
+        @pl.loop(0, count)
+        def _(i):
+            a, b = into(i), other(i)
+            a[...] = (a[...].astype(f32) + b[...].astype(f32)).astype(bf16)
+
+    def core_send(self):
+        g = self.g
+        self.w.send(self.full.at[:, :, 1 - g.c], self.rc, self.at, g.s, g.slot(0, 0, 1), self.rc)
+
+    def core_done(self):
+        g = self.g
+        self.w.arrived(self.rc, self.at)
+        self.add(8, lambda i: self.rc.at[i // 2, i % 2], lambda i: self.own(i // 2, i % 2))
+        self.w.send(self.rc.at[:, 1 - g.y], self.ry, self.at + 1, g.s, g.slot(0, 1, 0), self.ry)
+
+    def y_done(self):
+        g = self.g
+        self.w.arrived(self.ry, self.at + 1)
+        self.add(4, lambda i: self.ry.at[i], lambda i: self.rc.at[i, g.y])
+        partner = g.slot(1, 0, 0)
+        self.w.send(self.ry.at[g.line[1]], self.rz.at[0], self.at + 2, g.s, partner, self.rz.at[0])
+
+        @pl.when(g.inner == 0)
+        def _():
+            for i in (2, 3):
+                self.w.copy(self.ry.at[g.line[i]], self.rz.at[i], self.at + 1 + i, self.at + 1 + i, g.s, partner).start()
+
+    def z_done(self):
+        g = self.g
+
+        @pl.when(g.inner == 1)
+        def _():
+            for i in (2, 3):
+                self.w.arrived(self.rz.at[i], self.at + 1 + i)
+                a = self.rz.at[i]
+                a[...] = (a[...].astype(f32) + self.ry[g.line[i]].astype(f32)).astype(bf16)
+                self.w.copy(a, self.rz.at[1], self.at + 1 + i, self.at + 5, g.s, g.slot(i, 0, 0)).start()
+
+    def final(self):
+        g = self.g
+        self.w.arrived(self.rz.at[0], self.at + 2)
+        self.w.arrived(self.rz.at[1], self.at + 5)
+        total = self.ry[g.z].astype(f32) + self.rz[0].astype(f32) + self.rz[1].astype(f32)
+        self.fin[0] = total.astype(bf16)
+        self.w.send(self.fin.at[0], self.fin.at[1], self.at + 6, 1 - g.s, g.k, self.fin.at[0])
+
+    def done(self):
+        self.w.arrived(self.fin.at[1], self.at + 6)
+        for i in (2, 3):
+            self.w.copy(self.fin.at[0], self.fin.at[0], self.at + 1 + i, self.at + 1 + i, self.g.s, self.g.k).wait_send()
+
+
+class Back:
+    def __init__(self, wires, src, dst, pieces):
+        self.w, self.g, self.src, self.dst, self.pieces = wires, wires.g, src, dst, pieces
+        self.at = wires.block(wires.g.shards * pieces)
+        self.per = src.shape[0] // pieces
+
+    def cut(self, ref, i):
+        return ref.at[pl.ds(i * self.per, self.per)]
+
+    def send(self, i):
+        g = self.g
+        for d in range(1, g.shards):
+            to = (g.k + d) % g.shards
+            src = self.src.at[pl.ds(i * self.per, self.per), to]
+            self.w.send(src, self.cut(self.dst.at[g.k], i), self.at + i * g.shards + d, g.s, to, src)
+
+    def finish(self):
+        g = self.g
+        for i in range(self.pieces):
+            for d in range(1, g.shards):
+                self.w.arrived(self.cut(self.dst.at[(g.k - d) % g.shards], i), self.at + i * g.shards + d)
+
+
+def backward_kernel(
+    seqs, shards, counts, one_seq,
+    qkv, do, n1, qkvw, x_all, dh2, y_own, w2, w1, wd, smalls, gain, slopes, idc, idr, beginr,
+    ret_y, ret_x, o_qkv, o_dense, o_up, o_down, o_small,
+    qkv_v, do_v, dqkv_v, n1_v, qkvw_v, x_v, dh2_v, dk_acc, dv_acc, bias_acc, mine_v, sent_v, got_v, dx_v, gq_v,
+    small_v, small_got, small_fin, small_last, f_qkv, f_dense, f_up, f_down, own_w2, own_w1, own_wd,
+    *rest,
+):
+    bufs, (send_sems, recv_sems, copy_sems) = rest[:-3], rest[-3:]
+    g = Geometry(seqs, shards)
+    wires = Wires(g, send_sems, recv_sems)
+    pairs, tokens = do_v.shape[0], do_v.shape[1]
+    part = pairs * 2 * HEAD
+    width = n1_v.shape[1]
+    lanes = seqs * shards
+    block = ROWS * lanes
+    blocks = tokens // block
+    half = block // seqs
+    tile = bias_acc.shape[2]
+    local = []
+
+    def bring(src, dst):
+        made = pltpu.make_async_copy(src, dst, copy_sems.at[len(local)])
+        made.start()
+        local.append(made)
+        return made
+
+    def held(ref):
+        return lambda i, j: ref.at[i, j]
+
+    down = Scatter(wires, w2, held(own_w2), bufs[0:4])
+    up = Scatter(wires, w1, held(own_w1), bufs[4:8])
+    dense = Scatter(wires, wd, held(own_wd), bufs[8:12])
+    qkv_sum = Scatter(wires, gq_v, lambda i, j: gq_v.at[i, j, g.c], bufs[12:16])
+    back_y = Back(wires, y_own, ret_y, 1)
+    back_x = Back(wires, dx_v, ret_x, blocks)
+    half_at = wires.block(blocks)
+    small_at = wires.block(shards + 1)
+
+    first = [bring(qkv, qkv_v)] + [bring(do.at[:, pl.ds(h * 2 * HEAD, 2 * HEAD)], do_v.at[h]) for h in range(pairs)]
+    owns = [bring(a.at[:, :, g.c], b) for a, b in ((w2, own_w2), (w1, own_w1), (wd, own_wd))]
+    later = [
+        bring(n1, n1_v), bring(qkvw, qkvw_v), bring(x_all.at[:, pl.ds(g.s * shards, shards)], x_v), bring(dh2, dh2_v),
+        bring(smalls, small_v),
+    ]
+    enter(g)
+    down.core_send()
+    up.core_send()
+    dense.core_send()
+    back_y.send(0)
+    own_y = bring(y_own.at[:, g.k], dx_v.at[:, g.k])
+    for made in first + owns:
+        made.wait()
+
+    lane_id = lax.broadcasted_iota(jnp.int32, (1, 2 * HEAD), 1)
+
+    def attend(h):
+        q_ref, k_ref, v_ref, do_ref = qkv_v.at[h], qkv_v.at[pairs + h], qkv_v.at[2 * pairs + h], do_v.at[h]
+        dk_acc[...] = jnp.zeros_like(dk_acc)
+        dv_acc[...] = jnp.zeros_like(dv_acc)
+        for j in range(2):
+            bias_acc[j] = jnp.broadcast_to(slopes[h, j] * idc[...], bias_acc.shape[1:])
+        cols = pl.ds(pl.multiple_of(h * 2 * HEAD, 2 * HEAD), 2 * HEAD)
+        for b in range(blocks):
+            end = (b + 1) * block
+            for t in range(block // tile):
+                at = pl.ds(b * block + t * tile, tile)
+                q = q_ref[at, :] * jnp.asarray(HEAD**-0.5, bf16)
+                grad = do_ref[at, :]
+                ids_q = idr[:, at]
+                both = None
+                for j in range(2):
+                    mine = (lane_id // HEAD) == j
+                    qj = jnp.where(mine, q, jnp.zeros_like(q))
+                    doj = jnp.where(mine, grad, jnp.zeros_like(grad))
+                    s = lax.dot_general(
+                        k_ref[:end, :], qj, (((1,), (1,)), ((), ())), preferred_element_type=f32
+                    )
+                    s = s + bias_acc[j, :end, :]
+                    if one_seq:
+                        tail = attn_mask(s[b * block :, :], idc[b * block : end, :] <= ids_q)
+                        s = jnp.concatenate([s[: b * block, :], tail], axis=0) if b else tail
+                    else:
+                        ids_k = idc[:end, :]
+                        s = attn_mask(s, (ids_k <= ids_q) & (ids_k >= beginr[:, at]))
+                    top = jnp.max(s, axis=0, keepdims=True)
+                    e = jnp.exp(s - top)
+                    probs = e * (1.0 / jnp.sum(e, axis=0, keepdims=True))
+                    dv_acc[:end, :] += jnp.dot(probs.astype(bf16), doj, preferred_element_type=f32)
+                    dp = lax.dot_general(
+                        v_ref[:end, :], doj, (((1,), (1,)), ((), ())), preferred_element_type=f32
+                    )
+                    inner = jnp.sum(probs * dp, axis=0, keepdims=True)
+                    ds = (probs * (dp - inner)).astype(bf16)
+                    dk_acc[:end, :] += jnp.dot(ds, qj, preferred_element_type=f32)
+                    dq = lax.dot_general(
+                        ds, k_ref[:end, :], (((0,), (0,)), ((), ())), preferred_element_type=f32
+                    )
+                    both = dq if both is None else jnp.where(mine, dq, both)
+                dqkv_v[0, at, cols] = (both * (HEAD**-0.5)).astype(bf16)
+        dqkv_v[1, :, cols] = dk_acc[...].astype(bf16)
+        dqkv_v[2, :, cols] = dv_acc[...].astype(bf16)
+
+    @pl.loop(0, pairs)
+    def _(h):
+        attend(h)
+
+        @pl.when(h == 0)
+        def _():
+            down.core_done()
+
+        @pl.when(h == 1)
+        def _():
+            up.core_done()
+
+        @pl.when(h == 2)
+        def _():
+            dense.core_done()
+
+    for made in later:
+        made.wait()
+
+    for b in range(blocks):
+        total = None
+        for p in range(3):
+            weight = qkvw_v[:, :, p * part : (p + 1) * part].reshape(width, part)
+            term = lax.dot_general(
+                dqkv_v[p, b * block : (b + 1) * block, :], weight, (((1,), (1,)), ((), ())), preferred_element_type=f32
+            )
+            total = term if total is None else total + term
+
+        @pl.when(g.s == 0)
+        def _(total=total, b=b):
+            mine_v[b] = total[:half]
+            sent_v[b] = total[half:].astype(bf16)
+
+        @pl.when(g.s == 1)
+        def _(total=total, b=b):
+            mine_v[b] = total[half:]
+            sent_v[b] = total[:half].astype(bf16)
+
+        if b:
+            wires.send(sent_v.at[b - 1], got_v.at[b - 1], half_at + b - 1, 1 - g.s, g.k, sent_v.at[b - 1])
+    down.y_done()
+    wires.send(sent_v.at[blocks - 1], got_v.at[blocks - 1], half_at + blocks - 1, 1 - g.s, g.k, sent_v.at[0])
+
+    rows = width // shards
+
+    @pl.loop(0, blocks)
+    def _(m):
+        cut = n1_v[:, pl.ds(pl.multiple_of(m * block, block), block)]
+        for p in range(3):
+            out = lax.dot_general(cut, dqkv_v[p], (((0,), (0,)), ((), ())), preferred_element_type=f32).astype(bf16)
+            out = out.reshape(block // rows // 2, 2, rows, part)
+            for i in range(block // rows // 2):
+                at = m * (block // rows // 2) + i
+                for j in range(2):
+                    gq_v[at // 2, at % 2, j, :, p * part : (p + 1) * part] = out[i, j]
+
+    sums = [jnp.sum(dqkv_v[p].astype(f32), axis=0, keepdims=True) for p in (0, 2)]
+    per = 2 * width // shards
+    for i in range(part // per):
+        for half_no in range(2):
+            small_v[(half_no * width + g.s * part) // per + i, 2:3, :per] = sums[half_no][:, i * per : (i + 1) * per]
+    qkv_sum.core_send()
+    own_y.wait()
+    kept_y = bring(dx_v.at[:, g.k], ret_y.at[g.k])
+    kept_y.wait()
+
+    gains = biases = jnp.zeros((1, width), f32)
+    for b in range(blocks):
+        wires.arrived(got_v.at[b], half_at + b)
+        grad = mine_v[b] + got_v[b].astype(f32)
+        xhat, root = normalize(x_v[b].astype(f32).reshape(half, width))
+        gains = gains + jnp.sum(grad * xhat, axis=0, keepdims=True)
+        biases = biases + jnp.sum(grad, axis=0, keepdims=True)
+        dx = dh2_v[b] + norm_pull(grad, gain[...], xhat, root)
+        dx_v[b] = dx.reshape(shards, ROWS, width).astype(bf16)
+        back_x.send(b)
+        if b == 0:
+            up.y_done()
+        if b == 1:
+            down.z_done()
+    for j in range(shards):
+        small_v[j, 0:1, :rows] = gains[:, j * rows : (j + 1) * rows]
+        small_v[j, 1:2, :rows] = biases[:, j * rows : (j + 1) * rows]
+    kept = [bring(dx_v.at[:, g.k], ret_x.at[g.k])]
+    for d in range(1, shards):
+        to = (g.k + d) % shards
+        wires.send(small_v.at[to], small_got.at[g.k], small_at + d, g.s, to, small_v.at[0])
+    small_got[g.k] = small_v[g.k]
+    qkv_sum.core_done()
+    dense.y_done()
+    up.z_done()
+    down.final()
+    dense.z_done()
+    qkv_sum.y_done()
+    for d in range(1, shards):
+        wires.arrived(small_got.at[(g.k - d) % shards], small_at + d)
+    small_fin[0] = jnp.sum(small_got[...], axis=0)
+    wires.send(small_fin.at[0], small_fin.at[1], small_at + shards, 1 - g.s, g.k, small_fin.at[0])
+    up.final()
+    dense.final()
+    qkv_sum.z_done()
+
+    down.done()
+    ff_part = f_down.shape[0] // seqs
+    for i, at in ((0, g.s), (1, 1 - g.s)):
+        f_down[pl.ds(pl.multiple_of(at * ff_part, ff_part), ff_part), :] = down.fin[i].astype(f32)
+    kept.append(bring(f_down, o_down))
+    up.done()
+    for i, at in ((0, g.s), (1, 1 - g.s)):
+        for j in range(shards):
+            f_up[:, pl.ds(pl.multiple_of((j * seqs + at) * ff_part, 128), ff_part)] = up.fin[
+                i, :, j * ff_part : (j + 1) * ff_part
+            ].astype(f32)
+    kept.append(bring(f_up, o_up))
+    dense.done()
+    f_dense[...] = dense.fin[0].astype(f32) + dense.fin[1].astype(f32)
+    kept.append(bring(f_dense, o_dense))
+    wires.arrived(small_fin.at[1], small_at + shards)
+    small_last[...] = small_fin[0] + small_fin[1]
+    kept.append(bring(small_last, o_small))
+    qkv_sum.final()
+    qkv_sum.done()
+    for i, at in ((0, g.s), (1, 1 - g.s)):
+        for p in range(3):
+            f_qkv[:, pl.ds(pl.multiple_of(p * width + at * part, 128), part)] = qkv_sum.fin[
+                i, :, p * part : (p + 1) * part
+            ].astype(f32)
+    kept.append(bring(f_qkv, o_qkv))
+    back_y.finish()
+    back_x.finish()
+    wires.drain()
+    for made in kept:
+        made.wait()
+    assert wires.used <= counts[0] and len(local) <= counts[1]
+
+
+def backward_exchange(
+    qkv, do, n1, qkvw, x_all, dh2, y_own, w2, w1, wd, smalls, gain, slopes, ids, begins, seqs, shards, one_seq
+):
+    tokens, part = do.shape
+    width = n1.shape[1]
+    pairs = part // (2 * HEAD)
+    lanes = seqs * shards
+    block = ROWS * lanes
+    blocks, half = tokens // block, block // seqs
+    tile = min(256, block)
+    rows, ff = width // shards, w1.shape[2]
+    ff_part = ff // shards
+    counts = (256, 48)
+    cut = lambda a: a.reshape((4, 2, 2) + a.shape[1:])
+    any_, vmem = pl.BlockSpec(memory_space=pl.ANY), pl.BlockSpec(memory_space=pltpu.VMEM)
+    ret = (shards, blocks, ROWS, width)
+    outs = [
+        (ret, bf16), (ret, bf16), ((rows, 3 * width), f32), ((rows, width), f32), ((rows, seqs * ff), f32),
+        ((seqs * ff_part, width), f32), (smalls.shape[1:], f32),
+    ]
+    blks = [(ff_part, width), (rows, ff), (rows, width), (rows, 3 * part)]
+    scratch = [
+        ((3 * pairs, tokens, 2 * HEAD), bf16), ((pairs, tokens, 2 * HEAD), bf16), ((3, tokens, part), bf16),
+        ((tokens, width), bf16), ((shards, rows, 3 * part), bf16), ((blocks, shards, ROWS, width), bf16),
+        ((blocks, half, width), f32), ((tokens, 2 * HEAD), f32), ((tokens, 2 * HEAD), f32), ((2, tokens, tile), f32),
+        ((blocks, half, width), f32), ((blocks, half, width), bf16), ((blocks, half, width), bf16),
+        ((blocks, shards, ROWS, width), bf16), ((4, 2, 2) + blks[3], bf16), (smalls.shape, f32), (smalls.shape, f32),
+        ((2,) + smalls.shape[1:], f32), (smalls.shape[1:], f32), ((rows, 3 * width), f32), ((rows, width), f32), ((rows, seqs * ff), f32),
+        ((seqs * ff_part, width), f32), ((4, 2) + blks[0], bf16), ((4, 2) + blks[1], bf16), ((4, 2) + blks[2], bf16),
+    ]
+    for blk in blks:
+        scratch += [((4, 2) + blk, bf16), ((4,) + blk, bf16), ((4,) + blk, bf16), ((2,) + blk, bf16)]
+    return pl.pallas_call(
+        functools.partial(backward_kernel, seqs, shards, counts, one_seq),
+        in_specs=[any_] * 11 + [vmem, pl.BlockSpec(memory_space=pltpu.SMEM)] + [vmem] * 3,
+        out_specs=[any_] * len(outs),
+        out_shape=[jax.ShapeDtypeStruct(s, d) for s, d in outs],
+        scratch_shapes=[pltpu.VMEM(s, d) for s, d in scratch]
+        + [pltpu.SemaphoreType.DMA((counts[0],)), pltpu.SemaphoreType.DMA((counts[0],)), pltpu.SemaphoreType.DMA((counts[1],))],
+        compiler_params=pltpu.CompilerParams(collective_id=2, has_side_effects=True, vmem_limit_bytes=60 * 2**20),
+        name="backward_exchange",
+    )(
+        qkv, do, n1, qkvw, x_all, dh2, y_own, cut(w2), cut(w1), cut(wd), smalls, gain, slopes.reshape(pairs, 2),
+        ids[:, None], ids[None, :], begins[None, :],
+    )
+
+
 def layout_tables(lengths, lane_count, group_count, per_group):
     seq_rows = lengths // lane_count
     row_start = jnp.cumsum(seq_rows) - seq_rows
@@ -660,9 +1028,9 @@
     part = heads * HEAD
     ff_part = hidden_units // shards // seqs
 
-    smalls = (first_gain, first_bias, qv_bias, dense_bias, second_gain, second_bias, fc1_bias, fc2_bias)
-    small_width = -(-max(a.shape[0] for a in smalls) // 128) * 128
-    small = jnp.stack([jnp.pad(a.astype(f32), (0, small_width - a.shape[0])) for a in smalls])
+    smalls_in = (first_gain, first_bias, qv_bias, dense_bias, second_gain, second_bias, fc1_bias, fc2_bias)
+    small_width = -(-max(a.shape[0] for a in smalls_in) // 128) * 128
+    small = jnp.stack([jnp.pad(a.astype(f32), (0, small_width - a.shape[0])) for a in smalls_in])
 
     seq_rows, row_start, slot_rows, slot_start, slot_before = layout_tables(lengths, lanes, shards, per_group)
     row_in = jnp.arange(rows, dtype=jnp.int32)[None, :, None]
@@ -747,17 +1115,18 @@
         for d, g in enumerate(got):
             grad_mixed = lax.dynamic_update_index_in_dim(grad_mixed, g, (me - d) % seqs, 1)
     grad_mixed = grad_mixed.reshape(cap, part)
-    grad_proj = jnp.concatenate(
-        attention_backward(qkv, grad_mixed, slopes, ids, begins, lanes, one_seq), axis=1
+    vectors = {3: grad_bdense, 4: grad_gain_two, 5: grad_bias_two, 7: grad_bdown}
+    zero = jnp.zeros((shards, seqs, ff_part), f32)
+    vectors[6] = lax.dynamic_update_index_in_dim(zero, grad_bup.reshape(shards, ff_part), me, 1)
+    pieces = [vectors[i].reshape(shards, -1) if i in vectors else jnp.zeros((shards, 1), f32) for i in range(8)]
+    small_grads = jnp.stack([jnp.pad(p, ((0, 0), (0, small_width - p.shape[1]))) for p in pieces], axis=1)
+    ret_out, ret_grad, g_qkv, g_dense, g_up, g_down, g_small = backward_exchange(
+        qkv, grad_mixed, normed_one, full_qkv.reshape(shards, -1, 3 * part), x_all,
+        grad_resid.reshape(blocks, -1, width), block_out.reshape(blocks, shards, ROWS, width),
+        grad_down.reshape(shards, ff_part, width), grad_up.reshape(shards, -1, shards * ff_part),
+        grad_dense.reshape(shards, -1, width), small_grads, gain_one[None],
+        slopes, ids, begins, seqs, shards, one_seq,
     )
-    grad_qkv = jnp.dot(normed_one.T, grad_proj, preferred_element_type=f32).astype(bf16)
-    proj_sums = jnp.sum(grad_proj.astype(f32), axis=0)
-    grad_one = jnp.dot(grad_proj, full_qkv.T, preferred_element_type=f32)
-    grad_one = seq_sum(grad_one.reshape(blocks, seqs, -1, width), 1).reshape(slots, width)
-    xhat_one, root_one = normalize(x_own.reshape(slots, width).astype(f32))
-    grad_gain_one = jnp.sum(grad_one * xhat_one, axis=0)
-    grad_bias_one = jnp.sum(grad_one, axis=0)
-    tokens_grad = (grad_resid + norm_pull(grad_one, gain_one, xhat_one, root_one)).astype(bf16)
 
     row_here = jnp.arange(slots, dtype=jnp.int32)[:, None]
     seq_in = ((row_here >= row_start[None]) & (row_here < (row_start + seq_rows)[None])).astype(jnp.int32)
@@ -765,40 +1134,15 @@
     fetch = jnp.sum(seq_in * (home[None] * rows + slot_before.reshape(-1)[None] + row_here - row_start[None]), axis=1)
     fetch_live = jnp.sum(seq_in, axis=1) > 0
 
-    def to_stream(own):
-        sent = own.reshape(blocks, shards, ROWS, width).transpose(1, 0, 2, 3).reshape(shards, rows, width)
-        got = lax.all_to_all(sent, "shard", split_axis=0, concat_axis=0, tiled=True)
+    def to_stream(got):
         taken = jnp.take(got.reshape(-1, width), fetch, axis=0)
         return jnp.where(fetch_live[:, None], taken, jnp.zeros_like(taken))[None]
 
-    down_block = shard_reduce(grad_down.reshape(shards, ff_part, width), bf16)
-    up_block = shard_reduce(grad_up.reshape(shards, -1, shards * ff_part), bf16)
-    dense_block = shard_reduce(grad_dense.reshape(shards, -1, width), bf16)
-    qkv_block = shard_reduce(grad_qkv.reshape(shards, -1, 3 * part), bf16)
-
-    def spread(vector, index_shape):
-        zero = jnp.zeros(index_shape, f32)
-        return lax.dynamic_update_index_in_dim(zero, vector, me, 1)
-
-    sums = proj_sums.reshape(3, part)
-    qv = spread(jnp.stack([sums[0], sums[2]]), (2, seqs, part)).reshape(shards, -1)
-    bup = spread(grad_bup.reshape(shards, ff_part), (shards, seqs, ff_part)).reshape(shards, -1)
-    rest = (grad_gain_one, grad_bias_one, grad_bdense, grad_gain_two, grad_bias_two, grad_bdown)
-    packed = jnp.concatenate([a.reshape(shards, -1) for a in rest] + [qv, bup], axis=1)
-    packed = shard_reduce(packed, f32)
-    packed = jnp.sum(seq_gather(packed, 0), axis=0)
-    cuts, at = [], 0
-    for a in [a.reshape(shards, -1) for a in rest] + [qv, bup]:
-        cuts.append(packed[at : at + a.shape[1]])
-        at += a.shape[1]
-    g_gain_one, g_bias_one, g_bdense, g_gain_two, g_bias_two, g_bdown, g_qv, g_bup = cuts
-
-    g_dense = jnp.sum(seq_gather(dense_block.astype(bf16), 0).astype(f32), axis=0)
-    g_qkv = seq_gather(qkv_block.astype(bf16).reshape(-1, 3, part), 2).reshape(-1, 3 * width).astype(f32)
-    g_up = seq_gather(up_block.astype(bf16).reshape(-1, shards, ff_part), 2).reshape(-1, hidden_units).astype(f32)
-    g_down = seq_gather(down_block.astype(bf16), 0).reshape(-1, width).astype(f32)
+    g_gain_one, g_bias_one, g_qv, g_bdense, g_gain_two, g_bias_two, g_bup, g_bdown = (
+        g_small[i, : a.shape[0]] for i, a in enumerate(smalls_in)
+    )
     return (
-        to_stream(block_out), to_stream(tokens_grad.reshape(blocks, -1, width)),
+        to_stream(ret_out), to_stream(ret_grad),
         g_gain_one, g_bias_one, g_qkv, g_qv, g_dense, g_bdense, g_gain_two, g_bias_two, g_up, g_bup, g_down, g_bdown,
     )
 

time: 536 us -> 451 us (0.84)
  Pallas kernels: 181 us -> 290 us
  waiting for transfers between devices: 70.6 us -> 14.2 us
  starting transfers between devices: 55.3 us -> 2.6 us
  local copies, waits for them, and re-layouts: 86.2 us -> 46.3 us
  other arithmetic: 55.7 us -> 23.9 us
  matrix products: 77 us -> 64.3 us
    pallas_call x1, Pallas kernels: 30.6 us -> 140 us  [backward_exchange(): pl.pallas_call(functools.partial(backward_kernel, seqs, shards, counts, o...]
    ppermute x30 -> x0, waiting for transfers between devices: 69.4 us -> none  [the longest x25 64.3 us: shard_reduce(): total = total + lax.ppermute(sent, 'shard', pairs).astype(f32)]
    ppermute x30 -> x0, starting transfers between devices: 38.4 us -> none  [the longest x25 26.3 us: shard_reduce(): total = total + lax.ppermute(sent, 'shard', pairs).astype(f32)]
    convert_element_type x14 -> x0, other arithmetic: 18.9 us -> none  [the longest x8 13.9 us: shard_reduce(): blocks = total if axis == 0 else total.astype(dtype)]
    squeeze x12 -> x1, local copies, waits for them, and re-layouts: 14.2 us -> 0.59 us  [take(): return lax.dynamic_index_in_dim(blocks, index, axis, keepdims=False)]
    all_to_all x2 -> x0, starting transfers between devices: 13.1 us -> none  [to_stream(): got = lax.all_to_all(sent, 'shard', split_axis=0, concat_axis=0, tiled=True)]
    ppermute x4 -> x3, waiting for transfers between devices: 1.2 us -> 14.2 us  [seq_blocks(): got.append(lax.ppermute(sent, 'seq', [(i, (i + d) % n) for i in range(n)]))]
    dot_general x2 -> x0, matrix products: 9.42 us -> none  [the longest x1 5.99 us: per_device(): jnp.dot(normed_one.T, grad_proj, preferred_element_type=f32).astype(bf16)]
  transfers between devices with their start and end apart: 36 -> 3, of which waited for: 7 -> 2; matrix products, arithmetic and copies ran while one was open for 26% -> 10% of each run, Pallas kernels for 6% -> 0%
where the time goes in v3:
time: 451 us; the launch traced here: 443 us
  Pallas kernels  290 us (64%)
  matrix products  64.3 us (14%)
  local copies, waits for them, and re-layouts  46.3 us (10%)
  other arithmetic  23.9 us (5%)
  waiting for transfers between devices  14.2 us (3%)
    pallas_call x1, Pallas kernels, forward_exchange(): pl.pallas_call(functools.partial(forward_kernel, seqs, shards, counts, on...  150 us
    pallas_call x1, Pallas kernels, backward_exchange(): pl.pallas_call(functools.partial(backward_kernel, seqs, shards, counts, o...  140 us
    ppermute x3, waiting for transfers between devices, seq_blocks(): got.append(lax.ppermute(sent, 'seq', [(i, (i + d) % n) for i in range(n)]))  14.2 us
    dot_general x1, matrix products, per_device(): grad_activ = jnp.dot(cot_low, full_down.T, preferred_element_type=f32)  13.2 us
    unnamed x72, local copies, waits for them, and re-layouts  9.99 us
    dot_general x1, matrix products, per_device(): jnp.dot(activ.T, cot_low, preferred_element_type=f32).astype(bf16)  9.55 us
  transfers between devices with their start and end apart: 3, of which 2 were waited for; matrix products, arithmetic and copies ran while one was open for 10% of the time, Pallas kernels for 0%

profile of v3, /device:TPU:0, one launch (start us, length us, event | category | flops | bytes accessed | tf_op | source)
XLA Modules:
  0.0 443.2 jit_solution(17613694821607348060)
XLA Ops:
  4.1 2.1 gather_fusion
  6.3 2.1 gather_fusion.1
  14.7 150.0 %forward_exchange.1 = (bf16[4,32,8,1024]{3,2,1,0:T(8,128)(2,1)}, bf16[4,32,8,1024]{3,2,1,0:T(8,128)(2,1)}, bf16[1024,1024]{1,0:T(8,128)(2,1)}, bf16[16,64,1536]{...) custom-call(bf16[16,4,8,1024]{3,2,1,0:T(8,128)(2,1)} %bitcast.168, ...), custom_call_target="tpu_custom_call" | custom-call | tf_op jit(solution)/shard_map/forward_exchange/pallas_call | solution.py:625
  167.3 3.0 copy.45
  170.3 5.1 %fusion.45 = (f32[1024]{0:T(1024)S(1)}, f32[1024,1024]{1,0:T(8,128)S(1)}) fusion(f32[1024]{0:T(1024)S(1)} %add.466, bf16[1024,1024]{0,1:T(8,128)(2,1)S(1)} %bitcast.174, bf16[1024,1024]{1,0:T(8,128)(2,1)} %bitcast.192, bf16[4,32,8,1024]{3,2,1,0:T(8,128)(2,1)} %get-tuple-element.34.x_all), kind=kOutput, calls=%fused_computation.147 | convolution fusion | flops 2151676928 | bytes 10493952 | tf_op jit(solution)/shard_map/dot_general | solution.py:1081
  178.1 7.8 %fusion.42 = f32[1024,2048]{1,0:T(8,128)S(1)} fusion(bf16[1024,2048]{1,0:T(8,128)(2,1)} %bitcast.188, f32[1024,1024]{1,0:T(8,128)} %copy-done.4, f32[1024]{0:T(1024)S(1)} %add.474, f32[1024]{0:T(1024)S(1)} %mul.270, f32[1024]{0:T(1024)S(1)} %add_rsqrt_fusion, f32[1024]{0:T(1024)S(1)} %broadcast_multiply_fusion), kind=kOutput, calls=%fused_computation.146 | convolution fusion | flops 4300210176 | bytes 16793600 | tf_op jit(solution)/shard_map/dot_general | solution.py:1085
  185.9 13.2 %convert_reduce_fusion = (f32[2048]{0:T(1024)S(1)}, bf16[1024,2048]{1,0:T(8,128)(2,1)}, bf16[1024,2048]{1,0:T(8,128)(2,1)S(1)}) fusion(f32[1024,2048]{1,0:T(8,128)S(1)} %fusion.42, f32[2048]{0:T(1024)S(1)} %bitcast.186, bf16[1024,1024]{1,0:T(8,128)(2,1)S(1)} %bitcast.176, bf16[2048,1024]{1,0:T(8,128)(2,1)S(1)} %bitcast.190), kind=kOutput, calls=%fused_computation.14 | convolution fusion | flops 4355782656 | bytes 23085056 | tf_op jit(solution)/shard_map/dot_general | solution.py:1093
  201.0 6.0 %fusion.47 = f32[4,2,128,1024]{3,2,1,0:T(8,128)} fusion(bf16[4,2,128,2048]{3,2,1,0:T(8,128)(2,1)S(1)} %bitcast.194, bf16[2048,1024,1,1]{1,0,3,2:T(8,128)(2,1)S(1)} %bitcast.191), kind=kOutput, calls=%fused_computation.149 | convolution fusion | flops 4294967296 | bytes 12582912 | tf_op jit(solution)/shard_map/dot_general | solution.py:1087
  207.0 2.7 fusion.14
  210.3 7.9 %fusion.46 = f32[4,2,128,1024]{3,2,1,0:T(8,128)S(1)} fusion(bf16[4,2,128,2048]{3,2,1,0:T(8,128)(2,1)} %bitcast.195, bf16[1024,2048,1,1]{1,0,3,2:T(8,128)(2,1)} %bitcast.189), kind=kOutput, calls=%fused_computation.148 | convolution fusion | flops 4294967296 | bytes 12582912 | tf_op jit(solution)/shard_map/dot_general | solution.py:1097
  222.3 6.6 %convolution_convert_fusion = bf16[1024,2048]{1,0:T(8,128)(2,1)} fusion(bf16[1024,2048]{1,0:T(8,128)(2,1)S(1)} %copy-done.32, f32[1024,1024]{1,0:T(8,128)S(1)} %copy-done.5, f32[1024]{0:T(1024)S(1)} %add.474, f32[1024]{0:T(1024)S(1)} %mul.270, f32[1024]{0:T(1024)S(1)} %add_rsqrt_fusion, f32[1024]{0:T(1024)S(1)} %broadcast_multiply_fusion), kind=kOutput, calls=%fused_computation.20 | convolution fusion | flops 4302307328 | bytes 12599296 | tf_op jit(solution)/shard_map/dot_general | solution.py:1095
  234.0 2.3 reshape_reshape.22
  237.3 9.5 %convolution_convert_fusion.1 = bf16[2048,1024]{1,0:T(8,128)(2,1)} fusion(bf16[1024,2048]{1,0:T(8,128)(2,1)} %copy-done.31, bf16[1024,1024]{1,0:T(8,128)(2,1)} %bitcast.175), kind=kOutput, calls=%fused_computation.21 | convolution fusion | flops 4297064448 | bytes 10485760 | tf_op jit(solution)/shard_map/dot_general | solution.py:1092
  246.9 10.4 %collective-permute-done = bf16[4,128,1024]{2,1,0:T(8,128)(2,1)} collective-permute-done((bf16[4,128,1024]{2,1,0:T(8,128)(2,1)}, bf16[4,128,1024]{2,1,0:T(8,128)(2,1)}, u32[]{:S(2)}, u32[]{:S(2)}) %collective-permute-start) | collective-permute-done | bytes 1048608 | tf_op jit(solution)/shard_map/ppermute | solution.py:229
  257.3 3.7 multiply_reduce_fusion.1
  262.9 3.8 convolution_convert_fusion.2
  266.8 2.3 reshape.816
  269.1 2.2 constant_dynamic-slice_fusion.1
  273.7 4.3 bitcast_convert_fusion
  278.1 2.1 fusion.7.dh2
  280.2 3.8 collective-permute-done.1
  287.3 140.3 %backward_exchange.1 = (bf16[16,4,8,1024]{3,2,1,0:T(8,128)(2,1)}, bf16[16,4,8,1024]{3,2,1,0:T(8,128)(2,1)}, f32[64,3072]{1,0:T(8,128)}, f32[64,1024]{1,0:T(8,128...) custom-call(bf16[12,1024,128]{2,1,0:T(8,128)(2,1)} %get-tuple-element.32.qkv, ...), custom_call_target="tpu_custom_call" | custom-call | tf_op jit(solution)/shard_map/backward_exchange/pallas_call | solution.py:990
  431.4 4.2 gather_fusion.2
  435.6 2.1 gather_fusion.3
  (163 shorter events, 44.2 us)
Async XLA Ops:
  6.2 5.3 %copy-start.23 = (bf16[64]{0:T(256)(128)(2,1)S(1)}, bf16[64]{0:T(256)(128)(2,1)}, u32[]{:S(2)}) copy-start(bf16[64]{0:T(256)(128)(2,1)} %param.20) | copy-start | bytes 388
  6.2 5.3 %copy-start.24 = (bf16[64]{0:T(256)(128)(2,1)S(1)}, bf16[64]{0:T(256)(128)(2,1)}, u32[]{:S(2)}) copy-start(bf16[64]{0:T(256)(128)(2,1)} %param.21) | copy-start | bytes 388
  6.2 5.3 %copy-start.25 = (bf16[128]{0:T(256)(128)(2,1)S(1)}, bf16[128]{0:T(256)(128)(2,1)}, u32[]{:S(2)}) copy-start(bf16[128]{0:T(256)(128)(2,1)} %param.23) | copy-start | bytes 772
  6.3 5.4 %copy-start.26 = (bf16[64]{0:T(256)(128)(2,1)S(1)}, bf16[64]{0:T(256)(128)(2,1)}, u32[]{:S(2)}) copy-start(bf16[64]{0:T(256)(128)(2,1)} %param.25) | copy-start | bytes 388
  6.3 5.4 %copy-start.27 = (bf16[64]{0:T(256)(128)(2,1)S(1)}, bf16[64]{0:T(256)(128)(2,1)}, u32[]{:S(2)}) copy-start(bf16[64]{0:T(256)(128)(2,1)} %param.26) | copy-start | bytes 388
  6.3 5.4 %copy-start.28 = (bf16[64]{0:T(256)(128)(2,1)S(1)}, bf16[64]{0:T(256)(128)(2,1)}, u32[]{:S(2)}) copy-start(bf16[64]{0:T(256)(128)(2,1)} %param.27) | copy-start | bytes 388
  6.3 5.4 %copy-start.29 = (bf16[64]{0:T(256)(128)(2,1)S(1)}, bf16[64]{0:T(256)(128)(2,1)}, u32[]{:S(2)}) copy-start(bf16[64]{0:T(256)(128)(2,1)} %param.31) | copy-start | bytes 388
  6.3 5.4 %copy-start.30 = (bf16[256]{0:T(256)(128)(2,1)S(1)}, bf16[256]{0:T(256)(128)(2,1)}, u32[]{:S(2)}) copy-start(bf16[256]{0:T(256)(128)(2,1)} %param.29) | copy-start | bytes 1540
  178.1 7.8 %copy-start.13 = (bf16[4,32,8,1024]{3,2,1,0:T(8,128)(2,1)S(1)}, bf16[4,32,8,1024]{3,2,1,0:T(8,128)(2,1)}, u32[]{:S(2)}) copy-start(bf16[4,32,8,1024]{3,2,1,0:T(8,128)(2,1)} %get-tuple-element.33) | copy-start | bytes 6291460
  178.1 7.8 %copy-start.22 = (bf16[16,128,1024]{2,1,0:T(8,128)(2,1)S(1)}, bf16[16,128,1024]{2,1,0:T(8,128)(2,1)}, u32[]{:S(2)}) copy-start(bf16[16,128,1024]{2,1,0:T(8,128)(2,1)} %get-tuple-element.39) | copy-start | bytes 12582916
  209.7 37.1 %collective-permute-start.2 = (bf16[4,128,1024]{2,1,0:T(8,128)(2,1)}, bf16[4,128,1024]{2,1,0:T(8,128)(2,1)S(1)}, u32[]{:S(2)}, u32[]{:S(2)}) collective-permute-start(bf16[4,128,1024]{2,1,0:T(8,128)(2,1)} %fusion.14), channel_id=1, source_target_pairs={{0,16},{16,0},{1,17},{17,1},{2,18},{18,2},{3,19},{19,3},{4,20},{20... | collective-permute-start | bytes 3145736 | tf_op jit(solution)/shard_map/ppermute | solution.py:229
  210.3 10.6 %copy-start.8 = (bf16[8,1024,128]{2,1,0:T(8,128)(2,1)S(1)}, bf16[8,1024,128]{2,1,0:T(8,128)(2,1)}, u32[]{:S(2)}) copy-start(bf16[8,1024,128]{2,1,0:T(8,128)(2,1)} %get-tuple-element.35) | copy-start | bytes 6291460
  210.3 12.0 %copy-start.32 = (bf16[1024,2048]{1,0:T(8,128)(2,1)S(1)}, bf16[1024,2048]{1,0:T(8,128)(2,1)}, u32[]{:S(2)}) copy-start(bf16[1024,2048]{1,0:T(8,128)(2,1)} %get-tuple-element.61) | copy-start | bytes 12582916
  219.4 37.9 %collective-permute-start = (bf16[4,128,1024]{2,1,0:T(8,128)(2,1)}, bf16[4,128,1024]{2,1,0:T(8,128)(2,1)}, u32[]{:S(2)}, u32[]{:S(2)}) collective-permute-start(bf16[4,128,1024]{2,1,0:T(8,128)(2,1)} %fusion.12), channel_id=1, source_target_pairs={{0,16},{16,0},{1,17},{17,1},{2,18},{18,2},{3,19},{19,3},{4,20},{20... | collective-permute-start | bytes 3145736 | tf_op jit(solution)/shard_map/ppermute | solution.py:229
  237.3 20.0 %copy-start.6 = (f32[1024,1024]{1,0:T(8,128)S(1)}, f32[1024,1024]{1,0:T(8,128)}, u32[]{:S(2)}) copy-start(f32[1024,1024]{1,0:T(8,128)} %copy-done.4) | copy-start | bytes 12582916
  237.3 20.0 %copy-start.9 = (f32[4,2,128,1024]{3,2,1,0:T(8,128)S(1)}, f32[4,2,128,1024]{3,2,1,0:T(8,128)}, u32[]{:S(2)}) copy-start(f32[4,2,128,1024]{3,2,1,0:T(8,128)} %fusion.47) | copy-start | bytes 12582916
  237.3 20.0 %copy-start.11 = (f32[4,2,128,1024]{3,2,1,0:T(8,128)S(1)}, f32[4,2,128,1024]{3,2,1,0:T(8,128)}, u32[]{:S(2)}) copy-start(f32[4,2,128,1024]{3,2,1,0:T(8,128)} %copy-done.10) | copy-start | bytes 12582916
  246.9 14.1 %copy-start.14 = (bf16[4,32,8,1024]{3,2,1,0:T(8,128)(2,1)S(1)}, bf16[4,32,8,1024]{3,2,1,0:T(8,128)(2,1)}, u32[]{:S(2)}) copy-start(bf16[4,32,8,1024]{3,2,1,0:T(8,128)(2,1)} %get-tuple-element.33) | copy-start | bytes 6291460
  271.4 12.7 %collective-permute-start.1 = (bf16[4,128,512]{2,1,0:T(8,128)(2,1)S(1)}, bf16[4,128,512]{2,1,0:T(8,128)(2,1)S(1)}, u32[]{:S(2)}, u32[]{:S(2)}) collective-permute-start(bf16[4,128,512]{2,1,0:T(8,128)(2,1)S(1)} %bitcast.182), channel_id=1, source_target_pairs={{0,16},{16,0},{1,17},{17,1},{2,18},{18,2},{3,19},{19,3},{4,20},{20... | collective-permute-start | bytes 1572872 | tf_op jit(solution)/shard_map/ppermute | solution.py:229
  273.7 4.3 copy-start.7
  273.7 4.3 copy-start.15
  278.1 6.7 %copy-start.12 = (bf16[4,128,1,512]{3,1,0,2:T(8,128)(2,1)S(1)}, bf16[4,128,1,512]{3,1,0,2:T(8,128)(2,1)}, u32[]{:S(2)}) copy-start(bf16[4,128,1,512]{3,1,0,2:T(8,128)(2,1)} %copy.65) | copy-start | bytes 1572868
  437.7 4.2 copy-start.16
  437.7 5.2 %copy-start.1 = (bf16[1,512,1024]{2,1,0:T(8,128)(2,1)S(1)}, bf16[1,512,1024]{2,1,0:T(8,128)(2,1)}, u32[]{:S(2)}) copy-start(bf16[1,512,1024]{2,1,0:T(8,128)(2,1)} %param.17) | copy-start | bytes 3145732
  (12 other events, 31.0 us)
